TPU v7x, 32 devices: a whole 2x2x4 slice. The times are simulated.
32 devices in a mesh: brain: 2 (over x), slab: 16 (over z, y, core).
Axes of the slice: x: 2, y: 2, z: 4, core: 2. Of those that a mesh axis runs over, the one named last changes fastest.
Arguments:
- features: bfloat16 [32, 192, 16, 128], P(None, ('brain', 'slab')), parts along dimension 1, may hold values from -6 to 6
- conv_weight: bfloat16 [3, 128, 288], replicated, may hold values from -0.21875 to 0.21875
- norm_gain: float32 [4, 32], replicated, may hold values from 0.25 to 1.75
- norm_bias: float32 [4, 32], replicated, may hold values from -3 to 3
- head_weight: bfloat16 [4, 6, 32], replicated, may hold values from -2 to 2
- head_bias: float32 [4, 6], replicated, may hold values from -4 to 308
- patch_offsets: int32 [32, 2], P(('brain', 'slab')), parts along dimension 0, may hold values from -2 to 2
- fg_mask: int32 [32, 2], P(('brain', 'slab')), parts along dimension 0, may hold values 0 or 1
- acq_counts: int32 [32], P(('brain', 'slab')), parts along dimension 0, may hold values from 1 to 8, 64 in all
Outputs:
- resampled: float32 [6, 256, 16, 128], P(None, ('brain', 'slab')), parts along dimension 1
There are 2 independent parts, one for each index of `brain`. A program takes and returns all parts, laid end to end along the dimension named above; an argument that names none is the same for every part. Nothing has to cross between parts.
Inputs may be any that keep to these rules, and one draw needn't show every extreme that they name: `acq_counts`: within each brain volume separately, the 16 counts of that volume sum to 64 and some slab of that volume has exactly 8; the array of all volumes together sums to 64 once for every volume.
All inputs are finite; a program needn't handle non-finite values. No bound on the sum of `fg_mask` or of `acq_counts` on one device may be relied on, other than what follows from the above.
Results may differ from a plain program's by a relative error of at most 0.0003.
Values may be sent and summed in bfloat16 or wider, within the bound.
No kernel may reach another device: no remote copies, remote signals or barrier semaphores. Data moves between devices by JAX's collectives and lax.ppermute only.
A program may use at most 64 MiB of HBM per device.

v0:
```python
import jax
import jax.numpy as jnp
from jax import lax
from jax.sharding import PartitionSpec as P

CLASSES = 6
MARGIN = 2
PATCHES = 2
PATCH_ROWS = 8
RIM = 4
PATCH_X = 10
MOST_ACQ = 8


prior_weight = 0.1


def with_halo(value, sides, width):
    for axis, dim in sides:
        size, length = (lax.axis_size(axis), value.shape[dim])
        up = [(i, (i + 1) % size) for i in range(size - 1)]
        down = [(j, i) for i, j in up]
        last = lax.slice_in_dim(value, length - width, length, axis=dim)
        leading = lax.slice_in_dim(value, 0, width, axis=dim)
        before = lax.ppermute(last, axis, up)
        after = lax.ppermute(leading, axis, down)
        value = jnp.concatenate([before, value, after], axis=dim)
    return value


def from_behind(value, axis, steps):
    count = lax.axis_size(axis)
    leading, last = (max(0, -steps), min(count, count - steps))
    return lax.ppermute(value, axis, [(source, source + steps) for source in range(leading, last)])


def gauss_line(length):
    positions = jnp.arange(length, dtype=jnp.float32)
    centre = (length - 1) / 2.0
    spread = length / 4.0
    scaled = (positions - centre) / spread
    return jnp.exp(-0.5 * scaled * scaled)


def patch_scores(patch, conv_weight, norm_gain, norm_bias, head_weight, head_bias):
    channels, length, row_span, column_count = patch.shape
    padded = jnp.pad(patch, ((0, 0), (1, 1), (1, 1), (0, 0)))
    zero_col = jnp.zeros(padded.shape[:-1] + (1,), padded.dtype)
    shifted = (
        jnp.concatenate([zero_col, padded[..., :-1]], -1),
        padded,
        jnp.concatenate([padded[..., 1:], zero_col], -1),
    )
    tap_list = [
        source[:, :, row_shift : row_shift + row_span]
        for row_shift in range(3)
        for source in shifted
    ]
    stacked = jnp.concatenate(tap_list, 0)
    conv_out = jnp.zeros((conv_weight.shape[1], length * row_span * column_count), jnp.float32)
    for depth_tap in range(3):
        sliced = stacked[:, depth_tap : depth_tap + length].reshape(9 * channels, -1)
        conv_out = conv_out + jnp.dot(
            conv_weight[depth_tap], sliced, preferred_element_type=jnp.float32
        )
    centre_mean = jnp.mean(conv_out, axis=1, keepdims=True)
    centred = conv_out - centre_mean
    variance = jnp.mean(centred * centred, axis=1, keepdims=True)
    normed = (
        centred * lax.rsqrt(variance + 1e-05) * norm_gain.reshape(-1)[:, None]
        + norm_bias.reshape(-1)[:, None]
    )
    activated = jnp.where(normed > 0, normed, 0.01 * normed)
    fold_count = head_weight.shape[0]
    logits = (
        jnp.einsum(
            "fkc,fcv->fkv",
            head_weight.astype(jnp.float32),
            activated.reshape(fold_count, channels, -1),
            precision=lax.Precision.HIGHEST,
        )
        + head_bias[:, :, None]
    )
    class_probs = jnp.sum(jax.nn.softmax(logits, axis=1), axis=0) / fold_count
    window = (
        gauss_line(length)[:, None, None]
        * gauss_line(row_span)[None, :, None]
        * gauss_line(column_count)[None, None, :]
    ).reshape(-1)
    weighted = (class_probs * window[None, :]).reshape(-1, length, row_span, column_count)
    return (weighted, window.reshape(length, row_span, column_count))


def local(
    features,
    conv_weight,
    norm_gain,
    norm_bias,
    head_weight,
    head_bias,
    patch_offsets,
    fg_mask,
    acq_counts,
):
    channels, planes, row_total, column_count = features.shape
    slab_count = lax.axis_size("slab")
    slab_index = lax.axis_index("slab")
    extended = with_halo(features, (("slab", 1),), RIM)
    span_planes = planes + 2 * RIM
    prob_parts = []
    weight_parts = []
    for patch_index in range(PATCHES):
        row_first = patch_index * PATCH_ROWS
        patch_start = RIM - MARGIN + patch_offsets[0, patch_index]
        patch = lax.dynamic_slice_in_dim(
            extended[:, :, row_first : row_first + PATCH_ROWS], patch_start, PATCH_X, 1
        )
        keep_mask = fg_mask[0, patch_index]

        def scored(patch=patch):
            return patch_scores(patch, conv_weight, norm_gain, norm_bias, head_weight, head_bias)

        class_probs, window = scored()
        keep_value = keep_mask.astype(jnp.float32)
        class_probs = class_probs * keep_value
        window = window * keep_value
        placed_probs = jnp.zeros((CLASSES, span_planes, PATCH_ROWS, column_count), jnp.float32)
        placed_weights = jnp.zeros((span_planes, PATCH_ROWS, column_count), jnp.float32)
        prob_parts.append(
            lax.dynamic_update_slice_in_dim(placed_probs, class_probs, patch_start, 1)
        )
        weight_parts.append(lax.dynamic_update_slice_in_dim(placed_weights, window, patch_start, 0))
    prob_sums = jnp.concatenate(prob_parts, 2)
    weight_sums = jnp.concatenate(weight_parts, 1)
    extra_plane = 1
    from_above = from_behind(
        (prob_sums[:, : RIM + extra_plane], weight_sums[: RIM + extra_plane]), "slab", -1
    )
    from_below = from_behind(
        (prob_sums[:, RIM + planes - extra_plane :], weight_sums[RIM + planes - extra_plane :]),
        "slab",
        1,
    )
    pad_low = ((0, 0), (0, planes - RIM), (0, 0), (0, 0))
    pad_high = ((0, 0), (planes - RIM, 0), (0, 0), (0, 0))
    total_probs = (
        prob_sums[:, RIM : RIM + planes]
        + jnp.pad(from_below[0][:, extra_plane:], pad_low)
        + jnp.pad(from_above[0][:, :RIM], pad_high)
    )
    total_weights = (
        weight_sums[RIM : RIM + planes]
        + jnp.pad(from_below[1][extra_plane:], pad_low[1:])
        + jnp.pad(from_above[1][:RIM], pad_high[1:])
    )
    background = (jnp.arange(CLASSES) == 0).astype(jnp.float32)[:, None, None, None] * prior_weight
    merged = (total_probs + background) / (total_weights + prior_weight)
    below_plane = (from_below[0][:, 0] + prob_sums[:, RIM - 1] + background[:, 0]) / (
        from_below[1][0] + weight_sums[RIM - 1] + prior_weight
    )
    above_plane = (from_above[0][:, RIM] + prob_sums[:, RIM + planes] + background[:, 0]) / (
        from_above[1][RIM] + weight_sums[RIM + planes] + prior_weight
    )
    edged = jnp.concatenate([below_plane[:, None], merged, above_plane[:, None]], 1)
    acq_count = acq_counts[0].astype(jnp.float32)
    slot_ids = jnp.arange(MOST_ACQ, dtype=jnp.float32)
    step_size = planes / jnp.maximum(acq_count - 1.0, 1.0)
    local_pos = slot_ids * step_size - 0.5
    slab_anchor = (slab_index * planes).astype(jnp.float32)
    global_pos = jnp.clip(slab_anchor + local_pos, 0.0, float(slab_count * planes - 1))
    local_pos = global_pos - slab_anchor
    plane_pos = jnp.arange(planes + 2, dtype=jnp.float32) - 1.0
    used = (slot_ids < acq_count).astype(jnp.float32)
    resample_matrix = (
        jnp.maximum(0.0, 1.0 - jnp.abs(local_pos[:, None] - plane_pos[None, :])) * used[:, None]
    )
    return jnp.einsum("kj,cjhw->ckhw", resample_matrix, edged, precision=lax.Precision.HIGHEST)


def solution(mesh):
    in_specs = (
        P(None, ("brain", "slab"), None, None),
        P(),
        P(),
        P(),
        P(),
        P(),
        P(("brain", "slab"), None),
        P(("brain", "slab"), None),
        P(("brain", "slab")),
    )
    out_specs = P(None, ("brain", "slab"), None, None)
    return jax.shard_map(local, mesh=mesh, in_specs=in_specs, out_specs=out_specs, check_vma=False)
```

profile of v0, /device:TPU:11, one launch (start us, length us, event | category | flops | bytes accessed | tf_op | source)
XLA Modules:
  0.0 93.2 jit_solution(6910389079511696735)
XLA Ops:
  0.0 1.4 %fusion.107 = (bf16[32,4,16,128]{3,2,1,0:T(8,128)(2,1)S(1)}, bf16[32,4,16,128]{3,2,1,0:T(8,128)(2,1)S(1)}) fusion(bf16[32,6,16,128]{3,2,1,0:T(8,128)(2,1)} %param.9), kind=kLoop, calls=%fused_computation.184 | loop fusion | bytes 2097152 | tf_op jit(solution)/shard_map/slice | solution.py:24
  1.4 3.7 %collective-permute-start = (bf16[32,4,16,128]{3,2,1,0:T(8,128)(2,1)S(1)}, bf16[32,4,16,128]{3,2,1,0:T(8,128)(2,1)S(1)}, u32[]{:S(2)}, u32[]{:S(2)}) collective-permute-start(bf16[32,4,16,128]{3,2,1,0:T(8,128)(2,1)S(1)} %get-tuple-element.18), channel_id=1, source_target_pairs={{0,1},{1,2},{2,3},{3,4},{4,5},{5,6},{6,7},{7,8},{8,9},{9,10},{10,1... | collective-permute-start | bytes 1572872 | tf_op jit(solution)/shard_map/ppermute | solution.py:25
  5.1 1.9 %collective-permute-start.1 = (bf16[32,4,16,128]{3,2,1,0:T(8,128)(2,1)S(1)}, bf16[32,4,16,128]{3,2,1,0:T(8,128)(2,1)S(1)}, u32[]{:S(2)}, u32[]{:S(2)}) collective-permute-start(bf16[32,4,16,128]{3,2,1,0:T(8,128)(2,1)S(1)} %get-tuple-element.17), channel_id=1, source_target_pairs={{1,0},{2,1},{3,2},{4,3},{5,4},{6,5},{7,6},{8,7},{9,8},{10,9},{11,1... | collective-permute-start | bytes 1572872 | tf_op jit(solution)/shard_map/ppermute | solution.py:26
  7.1 1.4 %fusion.109 = (s32[1,1]{1,0:T(1,128)}, s32[1,1]{1,0:T(1,128)}) fusion(s32[1,2]{1,0:T(1,128)} %param.15), kind=kLoop, calls=%fused_computation.186 | loop fusion | bytes 16 | tf_op jit(solution)/shard_map/slice | solution.py:114
  11.0 1.4 %fusion.108 = (s32[1,1]{1,0:T(1,128)}, s32[1,1]{1,0:T(1,128)}) fusion(s32[1,2]{1,0:T(1,128)} %param.16), kind=kLoop, calls=%fused_computation.185 | loop fusion | bytes 16 | tf_op jit(solution)/shard_map/slice | solution.py:118
  13.9 3.6 %collective-permute-start.3 = (f32[5,16,128]{2,1,0:T(8,128)S(1)}, f32[5,16,128]{2,1,0:T(8,128)S(1)}, u32[]{:S(2)}, u32[]{:S(2)}) collective-permute-start(f32[5,16,128]{2,1,0:T(8,128)S(1)} %get-tuple-element.25), channel_id=1, source_target_pairs={{0,1},{1,2},{2,3},{3,4},{4,5},{5,6},{6,7},{7,8},{8,9},{9,10},{10,1... | collective-permute-start | bytes 122888 | tf_op jit(solution)/shard_map/ppermute | solution.py:34
  17.6 1.9 %collective-permute-start.5 = (f32[5,16,128]{2,1,0:T(8,128)S(1)}, f32[5,16,128]{2,1,0:T(8,128)S(1)}, u32[]{:S(2)}, u32[]{:S(2)}) collective-permute-start(f32[5,16,128]{2,1,0:T(8,128)S(1)} %get-tuple-element.26), channel_id=1, source_target_pairs={{1,0},{2,1},{3,2},{4,3},{5,4},{6,5},{7,6},{8,7},{9,8},{10,9},{11,1... | collective-permute-start | bytes 122888 | tf_op jit(solution)/shard_map/ppermute | solution.py:34
  20.3 0.8 add.231
  21.0 0.8 mul.311
  21.8 1.1 %collective-permute-done.5 = f32[5,16,128]{2,1,0:T(8,128)S(1)} collective-permute-done((f32[5,16,128]{2,1,0:T(8,128)S(1)}, f32[5,16,128]{2,1,0:T(8,128)S(1)}, u32[]{:S(2)}, u32[]{:S(2)}) %collective-permute-start.5) | collective-permute-done | bytes 40992 | tf_op jit(solution)/shard_map/ppermute | solution.py:34
  23.0 1.3 %constant_dynamic-update-slice_fusion.1 = bf16[32,14,16,128]{3,2,1,0:T(8,128)(2,1)S(1)} fusion(bf16[32,14,16,128]{3,2,1,0:T(8,128)(2,1)S(1)} %constant_dynamic-update-slice_fusion.2, bf16[32,6,16,128]{3,2,1,0:T(8,128)(2,1)} %param.9), kind=kLoop, calls=%fused_computation.137 | loop fusion | bytes 1572864
  24.4 0.3 fusion.106
  24.9 1.1 %pad_slice_fusion.2 = (bf16[32,12,10,127]{3,2,1,0:T(8,128)(2,1)S(1)}, bf16[32,12,10,127]{3,2,1,0:T(8,128)(2,1)S(1)}) fusion(bf16[32,10,8,128]{3,2,1,0:T(8,128)(2,1)S(1)} %get-tuple-element.41), kind=kLoop, calls=%fused_computation.38 | loop fusion | bytes 2606080 | tf_op jit(solution)/shard_map/slice | solution.py:52
  26.0 0.3 fusion.32
  26.5 0.2 fusion.35
  26.8 0.7 fusion.33
  27.6 0.4 fusion.36
  28.0 0.7 fusion.34
  28.9 0.4 fusion.37
  29.4 3.3 %fusion.105 = (bf16[288,10,8,128]{3,2,1,0:T(8,128)(2,1)S(1)}, bf16[288,10,8,128]{3,2,1,0:T(8,128)(2,1)S(1)}, bf16[288,10,8,128]{3,2,1,0:T(8,128)(2,1)S(1)}) fusion(bf16[288,12,8,128]{3,2,1,0:T(8,128)(2,1)S(1)} %fusion.37), kind=kLoop, calls=%fused_computation.182 | loop fusion | bytes 35389440 | tf_op jit(solution)/shard_map/slice | solution.py:62
  32.6 1.7 %fusion.16 = f32[10240,128]{0,1:T(8,128)S(1)} fusion(bf16[36,8,80,128]{3,2,1,0:T(8,128)(2,1)S(1)} %bitcast.99, bf16[3,128,288]{1,2,0:T(8,128)(2,1)S(1)} %copy-done.1), kind=kOutput, calls=%fused_computation.24 | convolution fusion | flops 754974720 | bytes 11214848 | tf_op jit(solution)/shard_map/dot_general | solution.py:63
  34.4 2.0 %convolution_add_fusion.1 = f32[10240,128]{0,1:T(8,128)S(1)} fusion(f32[10240,128]{0,1:T(8,128)S(1)} %fusion.16, bf16[36,8,80,128]{3,2,1,0:T(8,128)(2,1)S(1)} %bitcast.97, bf16[3,128,288]{1,2,0:T(8,128)(2,1)S(1)} %copy-done.1), kind=kOutput, calls=%fused_computation.7 | convolution fusion | flops 756285440 | bytes 16457728 | tf_op jit(solution)/shard_map/dot_general | solution.py:63
  36.3 1.8 %fusion.111 = (f32[128]{0:T(128)S(1)}, f32[10240,128]{0,1:T(8,128)S(1)}) fusion(f32[10240,128]{0,1:T(8,128)S(1)} %convolution_add_fusion.1, bf16[3,128,288]{1,2,0:T(8,128)(2,1)S(1)} %copy-done.1, bf16[36,8,80,128]{3,2,1,0:T(8,128)(2,1)S(1)} %bitcast.95), kind=kOutput, calls=%fused_computation.188 | convolution fusion | flops 757596032 | bytes 16458240 | tf_op jit(solution)/shard_map/dot_general | solution.py:63
  38.1 0.7 multiply_reduce_fusion
  38.9 1.1 %pad_slice_fusion.7 = (bf16[32,12,10,127]{3,2,1,0:T(8,128)(2,1)S(1)}, bf16[32,12,10,127]{3,2,1,0:T(8,128)(2,1)S(1)}) fusion(bf16[32,10,8,128]{3,2,1,0:T(8,128)(2,1)S(1)} %get-tuple-element.42), kind=kLoop, calls=%fused_computation.43 | loop fusion | bytes 2606080 | tf_op jit(solution)/shard_map/slice | solution.py:52
  40.0 0.3 fusion.26
  40.8 0.7 fusion.27
  41.6 0.4 fusion.30
  42.0 0.7 fusion.28
  42.9 0.4 fusion.31
  43.3 4.9 %fusion.104 = (bf16[288,10,8,128]{3,2,1,0:T(8,128)(2,1)S(1)}, bf16[288,10,8,128]{3,2,1,0:T(8,128)(2,1)}, bf16[288,10,8,128]{3,2,1,0:T(8,128)(2,1)S(1)}) fusion(bf16[288,12,8,128]{3,2,1,0:T(8,128)(2,1)S(1)} %fusion.31), kind=kLoop, calls=%fused_computation.181 | loop fusion | bytes 35389440 | tf_op jit(solution)/shard_map/slice | solution.py:62
  48.2 1.7 %fusion.23 = f32[10240,128]{0,1:T(8,128)S(1)} fusion(bf16[36,8,80,128]{3,2,1,0:T(8,128)(2,1)S(1)} %bitcast.100, bf16[3,128,288]{1,2,0:T(8,128)(2,1)S(1)} %copy-done.1), kind=kOutput, calls=%fused_computation.31 | convolution fusion | flops 754974720 | bytes 11214848 | tf_op jit(solution)/shard_map/dot_general | solution.py:63
  49.9 4.4 %convolution_add_fusion.3 = f32[10240,128]{0,1:T(8,128)S(1)} fusion(f32[10240,128]{0,1:T(8,128)S(1)} %fusion.23, bf16[36,8,80,128]{3,2,1,0:T(8,128)(2,1)} %bitcast.98, bf16[3,128,288]{1,2,0:T(8,128)(2,1)S(1)} %copy-done.1), kind=kOutput, calls=%fused_computation.9 | convolution fusion | flops 756285440 | bytes 16457728 | tf_op jit(solution)/shard_map/dot_general | solution.py:63
  54.3 1.8 %fusion.110 = (f32[128]{0:T(128)S(1)}, f32[10240,128]{0,1:T(8,128)S(1)}) fusion(f32[10240,128]{0,1:T(8,128)S(1)} %convolution_add_fusion.3, bf16[3,128,288]{1,2,0:T(8,128)(2,1)S(1)} %copy-done.1, bf16[36,8,80,128]{3,2,1,0:T(8,128)(2,1)S(1)} %bitcast.96), kind=kOutput, calls=%fused_computation.187 | convolution fusion | flops 757596032 | bytes 16458240 | tf_op jit(solution)/shard_map/dot_general | solution.py:63
  56.2 0.7 multiply_reduce_fusion.1
  56.9 4.1 %compare_select_fusion.1 = (f32[128,10240]{1,0:T(8,128)}, f32[128,10240]{1,0:T(8,128)S(1)}) fusion(f32[10240,128]{0,1:T(8,128)S(1)} %get-tuple-element.38, f32[128]{0:T(128)S(1)} %add.231, f32[128]{0:T(128)S(1)} %mul.311, f32[128]{0:T(128)S(1)} %add_rsqrt_fusion.1, f32[128]{0:T(128)S(1)} %broadcast_multiply_fusion.2, f32[128]{0:T(128)S(1)} %add_rsqrt_fusion, ...), kind=kLoop, calls=%fused_computation.5 | loop fusion | flops 18350080 | bytes 20974592 | tf_op jit(solution)/shard_map/jit(_where)/select_n | solution.py:73
  61.0 1.9 %fusion.10 = f32[4,6,10240]{2,1,0:T(8,128)S(1)} fusion(f32[4,32,10240]{2,1,0:T(8,128)S(1)} %bitcast.102, f32[4,6]{1,0:T(4,128)S(1)} %copy-done.6, bf16[4,6,32]{2,0,1:T(4,128)(2,1)S(1)} %copy-done), kind=kOutput, calls=%fused_computation.17 | convolution fusion | flops 94617600 | bytes 6227552 | tf_op jit(solution)/shard_map/fkc,fcv->fkv/dot_general | solution.py:76
  63.0 0.9 fusion.113
  64.0 4.4 %fusion.11 = f32[4,6,10240]{2,1,0:T(8,128)S(1)} fusion(f32[4,32,10240]{2,1,0:T(8,128)} %bitcast.101, f32[4,6]{1,0:T(4,128)S(1)} %copy-done.6, bf16[4,6,32]{2,0,1:T(4,128)(2,1)S(1)} %copy-done), kind=kOutput, calls=%fused_computation.19 | convolution fusion | flops 94617600 | bytes 6227552 | tf_op jit(solution)/shard_map/fkc,fcv->fkv/dot_general | solution.py:76
  68.4 0.9 fusion.112
  69.5 3.5 %dynamic_update_slice.12 = f32[6,14,8,128]{3,1,2,0:T(8,128)S(1)} dynamic-update-slice(f32[6,14,8,128]{3,1,2,0:T(8,128)S(1)} %broadcast.272.clone.1, f32[6,10,8,128]{3,1,2,0:T(8,128)S(1)} %get-tuple-element.27, s32[]{:T(128)} %constant.30.clone.1, s32[]{:T(128)S(6)} %select_n.17, s32[]{:T(128)} %constant.30.clone.1, s32[]{:T(128)} %constant.30.clone.1) | dynamic-update-slice | bytes 491524 | tf_op jit(solution)/shard_map/dynamic_update_slice | solution.py:130
  73.0 3.5 %dynamic_update_slice.13 = f32[6,14,8,128]{3,1,2,0:T(8,128)S(1)} dynamic-update-slice(f32[6,14,8,128]{3,1,2,0:T(8,128)S(1)} %broadcast.272.clone, f32[6,10,8,128]{3,1,2,0:T(8,128)S(1)} %get-tuple-element.28, s32[]{:T(128)} %constant.30.clone.1, s32[]{:T(128)S(6)} %select_n.19, s32[]{:T(128)} %constant.30.clone.1, s32[]{:T(128)} %constant.30.clone.1) | dynamic-update-slice | bytes 491524 | tf_op jit(solution)/shard_map/dynamic_update_slice | solution.py:130
  76.6 2.5 %collective-permute-start.2 = (f32[6,5,16,128]{3,1,2,0:T(8,128)S(1)}, f32[6,5,16,128]{3,1,2,0:T(8,128)S(1)}, u32[]{:S(2)}, u32[]{:S(2)}) collective-permute-start(f32[6,5,16,128]{3,1,2,0:T(8,128)S(1)} %get-tuple-element.15), channel_id=1, source_target_pairs={{0,1},{1,2},{2,3},{3,4},{4,5},{5,6},{6,7},{7,8},{8,9},{9,10},{10,1... | collective-permute-start | bytes 737288 | tf_op jit(solution)/shard_map/ppermute | solution.py:34
  79.1 2.7 %collective-permute-start.4 = (f32[6,5,16,128]{3,1,2,0:T(8,128)S(1)}, f32[6,5,16,128]{3,1,2,0:T(8,128)S(1)}, u32[]{:S(2)}, u32[]{:S(2)}) collective-permute-start(f32[6,5,16,128]{3,1,2,0:T(8,128)S(1)} %get-tuple-element.16), channel_id=1, source_target_pairs={{1,0},{2,1},{3,2},{4,3},{5,4},{6,5},{7,6},{8,7},{9,8},{10,9},{11,1... | collective-permute-start | bytes 737288 | tf_op jit(solution)/shard_map/ppermute | solution.py:34
  81.8 1.9 %collective-permute-done.2 = f32[6,5,16,128]{3,1,2,0:T(8,128)S(1)} collective-permute-done((f32[6,5,16,128]{3,1,2,0:T(8,128)S(1)}, f32[6,5,16,128]{3,1,2,0:T(8,128)S(1)}, u32[]{:S(2)}, u32[]{:S(2)}) %collective-permute-start.2) | collective-permute-done | bytes 245792 | tf_op jit(solution)/shard_map/ppermute | solution.py:34
  83.8 7.6 %collective-permute-done.4 = f32[6,5,16,128]{3,1,2,0:T(8,128)S(1)} collective-permute-done((f32[6,5,16,128]{3,1,2,0:T(8,128)S(1)}, f32[6,5,16,128]{3,1,2,0:T(8,128)S(1)}, u32[]{:S(2)}, u32[]{:S(2)}) %collective-permute-start.4) | collective-permute-done | bytes 245792 | tf_op jit(solution)/shard_map/ppermute | solution.py:34
  91.8 0.6 convolution_bitcast_fusion
  92.4 0.8 copy.21
  (61 shorter events, 2.8 us)
Async XLA Ops:
  0.0 61.0 %copy-start = (bf16[4,6,32]{2,0,1:T(4,128)(2,1)S(1)}, bf16[4,6,32]{2,0,1:T(4,128)(2,1)}, u32[]{:S(2)}) copy-start(bf16[4,6,32]{2,0,1:T(4,128)(2,1)} %param.13) | copy-start | bytes 4612
  1.4 21.5 %collective-permute-start = (bf16[32,4,16,128]{3,2,1,0:T(8,128)(2,1)S(1)}, bf16[32,4,16,128]{3,2,1,0:T(8,128)(2,1)S(1)}, u32[]{:S(2)}, u32[]{:S(2)}) collective-permute-start(bf16[32,4,16,128]{3,2,1,0:T(8,128)(2,1)S(1)} %get-tuple-element.18), channel_id=1, source_target_pairs={{0,1},{1,2},{2,3},{3,4},{4,5},{5,6},{6,7},{7,8},{8,9},{9,10},{10,1... | collective-permute-start | bytes 1572872 | tf_op jit(solution)/shard_map/ppermute | solution.py:25
  5.1 19.2 %collective-permute-start.1 = (bf16[32,4,16,128]{3,2,1,0:T(8,128)(2,1)S(1)}, bf16[32,4,16,128]{3,2,1,0:T(8,128)(2,1)S(1)}, u32[]{:S(2)}, u32[]{:S(2)}) collective-permute-start(bf16[32,4,16,128]{3,2,1,0:T(8,128)(2,1)S(1)} %get-tuple-element.17), channel_id=1, source_target_pairs={{1,0},{2,1},{3,2},{4,3},{5,4},{6,5},{7,6},{8,7},{9,8},{10,9},{11,1... | collective-permute-start | bytes 1572872 | tf_op jit(solution)/shard_map/ppermute | solution.py:26
  13.9 7.9 %collective-permute-start.3 = (f32[5,16,128]{2,1,0:T(8,128)S(1)}, f32[5,16,128]{2,1,0:T(8,128)S(1)}, u32[]{:S(2)}, u32[]{:S(2)}) collective-permute-start(f32[5,16,128]{2,1,0:T(8,128)S(1)} %get-tuple-element.25), channel_id=1, source_target_pairs={{0,1},{1,2},{2,3},{3,4},{4,5},{5,6},{6,7},{7,8},{8,9},{9,10},{10,1... | collective-permute-start | bytes 122888 | tf_op jit(solution)/shard_map/ppermute | solution.py:34
  17.6 5.3 %collective-permute-start.5 = (f32[5,16,128]{2,1,0:T(8,128)S(1)}, f32[5,16,128]{2,1,0:T(8,128)S(1)}, u32[]{:S(2)}, u32[]{:S(2)}) collective-permute-start(f32[5,16,128]{2,1,0:T(8,128)S(1)} %get-tuple-element.26), channel_id=1, source_target_pairs={{1,0},{2,1},{3,2},{4,3},{5,4},{6,5},{7,6},{8,7},{9,8},{10,9},{11,1... | collective-permute-start | bytes 122888 | tf_op jit(solution)/shard_map/ppermute | solution.py:34
  21.8 4.2 %copy-start.2 = (f32[5,16,128]{2,1,0:T(8,128)}, f32[5,16,128]{2,1,0:T(8,128)S(1)}, u32[]{:S(2)}) copy-start(f32[5,16,128]{2,1,0:T(8,128)S(1)} %collective-permute-done.3) | copy-start | bytes 122884
  22.9 3.1 %copy-start.4 = (f32[5,16,128]{2,1,0:T(8,128)}, f32[5,16,128]{2,1,0:T(8,128)S(1)}, u32[]{:S(2)}) copy-start(f32[5,16,128]{2,1,0:T(8,128)S(1)} %collective-permute-done.5) | copy-start | bytes 122884
  29.3 3.3 %copy-start.1 = (bf16[3,128,288]{1,2,0:T(8,128)(2,1)S(1)}, bf16[3,128,288]{1,2,0:T(8,128)(2,1)}, u32[]{:S(2)}) copy-start(bf16[3,128,288]{1,2,0:T(8,128)(2,1)} %param.10) | copy-start | bytes 663556
  56.9 4.2 %copy-start.6 = (f32[4,6]{1,0:T(4,128)S(1)}, f32[4,6]{1,0:T(4,128)}, u32[]{:S(2)}) copy-start(f32[4,6]{1,0:T(4,128)} %param.14) | copy-start | bytes 292
  68.3 13.4 %slice-start = ((f32[5,16,128]{2,1,0:T(8,128)}), f32[4,16,128]{2,1,0:T(8,128)S(1)}, s32[]{:S(2)}) async-start(f32[5,16,128]{2,1,0:T(8,128)} %copy-done.2), calls=%async_computation | async-start | bytes 65536 | tf_op jit(solution)/shard_map/slice | solution.py:153
  68.3 13.4 %slice-start.1 = ((f32[5,16,128]{2,1,0:T(8,128)}), f32[4,16,128]{2,1,0:T(8,128)S(1)}, s32[]{:S(2)}) async-start(f32[5,16,128]{2,1,0:T(8,128)} %copy-done.4), calls=%async_computation.1 | async-start | bytes 65536 | tf_op jit(solution)/shard_map/slice | solution.py:154
  68.4 13.5 %copy-start.3 = (f32[5,16,128]{2,1,0:T(8,128)S(1)}, f32[5,16,128]{2,1,0:T(8,128)}, u32[]{:S(2)}) copy-start(f32[5,16,128]{2,1,0:T(8,128)} %copy-done.2) | copy-start | bytes 122884
  68.4 13.5 %copy-start.5 = (f32[5,16,128]{2,1,0:T(8,128)S(1)}, f32[5,16,128]{2,1,0:T(8,128)}, u32[]{:S(2)}) copy-start(f32[5,16,128]{2,1,0:T(8,128)} %copy-done.4) | copy-start | bytes 122884
  76.6 7.2 %collective-permute-start.2 = (f32[6,5,16,128]{3,1,2,0:T(8,128)S(1)}, f32[6,5,16,128]{3,1,2,0:T(8,128)S(1)}, u32[]{:S(2)}, u32[]{:S(2)}) collective-permute-start(f32[6,5,16,128]{3,1,2,0:T(8,128)S(1)} %get-tuple-element.15), channel_id=1, source_target_pairs={{0,1},{1,2},{2,3},{3,4},{4,5},{5,6},{6,7},{7,8},{8,9},{9,10},{10,1... | collective-permute-start | bytes 737288 | tf_op jit(solution)/shard_map/ppermute | solution.py:34
  79.1 12.3 %collective-permute-start.4 = (f32[6,5,16,128]{3,1,2,0:T(8,128)S(1)}, f32[6,5,16,128]{3,1,2,0:T(8,128)S(1)}, u32[]{:S(2)}, u32[]{:S(2)}) collective-permute-start(f32[6,5,16,128]{3,1,2,0:T(8,128)S(1)} %get-tuple-element.16), channel_id=1, source_target_pairs={{1,0},{2,1},{3,2},{4,3},{5,4},{6,5},{7,6},{8,7},{9,8},{10,9},{11,1... | collective-permute-start | bytes 737288 | tf_op jit(solution)/shard_map/ppermute | solution.py:34
where the time goes:
time: 93.7 us; the launch traced here: 93.2 us
  local copies, waits for them, and re-layouts  32.7 us (35%)
  matrix products  20.3 us (22%)
  starting transfers between devices  16.4 us (18%)
  waiting for transfers between devices  10.6 us (11%)
  other arithmetic  8.29 us (9%)
  between operations  5.03 us (5%)
    dot_general x6, matrix products, patch_scores(): jnp.dot(conv_weight[depth_tap], sliced, preferred_element_type=jnp.float32)  13.4 us
    ppermute x4, starting transfers between devices, from_behind(): lax.ppermute(value, axis, [(source, source + steps) for source in range(l...  10.7 us
    ppermute x4, waiting for transfers between devices, from_behind(): lax.ppermute(value, axis, [(source, source + steps) for source in range(l...  10.6 us
    slice x2, local copies, waits for them, and re-layouts, patch_scores(): sliced = stacked[:, depth_tap:depth_tap + length].reshape(9 * channels, -1)  8.17 us
    unnamed x34, local copies, waits for them, and re-layouts  7.19 us
    dynamic_update_slice x2, local copies, waits for them, and re-layouts, local(): lax.dynamic_update_slice_in_dim(placed_probs, class_probs, patch_start, 1)  6.91 us
    dot_general x2, matrix products, patch_scores(): jnp.einsum('fkc,fcv->fkv', head_weight.astype(jnp.float32), activated.res...  6.31 us
    select_n x1, other arithmetic, patch_scores(): activated = jnp.where(normed > 0, normed, 0.01 * normed)  4.13 us
  transfers between devices with their start and end apart: 6, of which 3 were waited for; matrix products, arithmetic and copies ran while one was open for 6% of the time, Pallas kernels for 0%

commit v1 on v0

v1 whole, which is shorter than its diff:
```python
import functools
import jax
import jax.numpy as jnp
from jax import lax
from jax.experimental import pallas as pl
from jax.experimental.pallas import tpu as pltpu
from jax.sharding import PartitionSpec as P

PATCHES = 2
PATCH_ROWS = 8
MARGIN = 2
RIM = 4
PATCH_X = 10
MOST_ACQ = 8
PRIOR = 0.1
EPS = 1e-05
F32 = jnp.float32
BF16 = jnp.bfloat16
MIB = 1 << 20


def vmem():
    return pl.BlockSpec(memory_space=pltpu.VMEM)


def smem():
    return pl.BlockSpec(memory_space=pltpu.SMEM)


def prep_kernel(feat, own, to_a, to_b):
    channels, planes, rows, cols = feat.shape
    even = lax.rem(lax.axis_index("slab"), 2) == 0
    a_first = jnp.where(even, planes - RIM, 0)
    b_first = jnp.where(even, 0, planes - RIM)
    for x in range(planes):
        turned = jnp.swapaxes(feat[:, x].astype(F32), 0, 1).astype(BF16)
        own[x] = turned.reshape(own.shape[1:])
    to_a[...] = own[pl.ds(a_first, RIM)]
    to_b[...] = own[pl.ds(b_first, RIM)]


def column_of(table, folds, width):
    diag = lax.broadcasted_iota(jnp.int32, (width, width), 0) == lax.broadcasted_iota(jnp.int32, (width, width), 1)
    parts = []
    for f in range(folds):
        row = jnp.broadcast_to(table[f : f + 1, :], (width, width))
        parts.append(jnp.sum(jnp.where(diag, row, 0.0), axis=1, keepdims=True))
    return jnp.concatenate(parts, 0)


def head_tables(head_w, head_b, folds, classes, channels):
    rows = classes * 2 * folds
    row = lax.broadcasted_iota(jnp.int32, (rows, classes), 0)
    cls = lax.broadcasted_iota(jnp.int32, (rows, classes), 1)
    brow = lax.broadcasted_iota(jnp.int32, (rows, classes), 0)
    lane = lax.broadcasted_iota(jnp.int32, (channels, folds * channels), 1)
    chan = lax.broadcasted_iota(jnp.int32, (channels, folds * channels), 0)
    table = jnp.zeros((rows, folds * channels), F32)
    bias = jnp.zeros((rows, 1), F32)
    for f in range(folds):
        pick = (row // (2 * folds) == cls) & (row % folds == f)
        part = jnp.dot(pick.astype(F32).astype(BF16), head_w[f], preferred_element_type=F32).astype(BF16)
        place = (lane == chan + f * channels).astype(F32).astype(BF16)
        table = table + jnp.dot(part, place, preferred_element_type=F32)
        bias = bias + jnp.sum(jnp.where(pick, jnp.broadcast_to(head_b[f : f + 1, :], (rows, classes)), 0.0), axis=1, keepdims=True)
    table = table.astype(BF16)
    return jnp.concatenate([table, table], 1), bias


def gauss(position, length):
    scaled = (position - (length - 1) / 2.0) / (length / 4.0)
    return jnp.exp(-0.5 * scaled * scaled)


def fill_taps(taps, plane, source):
    rows, channels, cols = source.shape
    lane = lax.broadcasted_iota(jnp.int32, (channels, cols), 1)
    for h in range(rows):
        value = source[h]
        wide = value.astype(F32)
        left = jnp.where(lane == 0, 0.0, pltpu.roll(wide, 1, 1)).astype(BF16)
        right = jnp.where(lane == cols - 1, 0.0, pltpu.roll(wide, cols - 1, 1)).astype(BF16)
        taps[plane, h + 1] = jnp.concatenate([left, value, right], 0)


def main_kernel(offs, mask, own, from_a, from_b, wt, gain, nbias, head_w, head_b, kept, to_a, to_b, taps, w_all, conv, placed, shift, sums, squares):
    planes = own.shape[0]
    folds, classes, channels = head_w.shape
    outs = folds * channels
    cols = own.shape[-1]
    span = planes + 2 * RIM
    zero_plane = span
    even = lax.rem(lax.axis_index("slab"), 2) == 0
    a_base = jnp.where(even, RIM + planes, 0)
    b_base = jnp.where(even, 0, RIM + planes)
    wide_w = jnp.concatenate([wt[a].astype(F32) for a in range(3)], 0)
    w_all[...] = jnp.transpose(wide_w).astype(BF16)
    head, hbias = head_tables(head_w, head_b, folds, classes, channels)
    hbias = jnp.broadcast_to(hbias, (classes * 2 * folds, 2 * cols))
    gain_col = column_of(gain, folds, channels)
    bias_col = column_of(nbias, folds, channels)
    zero_row = jnp.zeros((3 * channels, cols), BF16)
    taps[zero_plane] = jnp.zeros(taps.shape[1:], BF16)
    sub = lax.broadcasted_iota(jnp.int32, (2 * folds, cols), 0)
    lane = lax.broadcasted_iota(jnp.int32, (2 * folds, cols), 1)
    line = gauss(sub.astype(F32), PATCH_ROWS) * gauss(lane.astype(F32), cols)
    for p in range(PATCHES):
        first = RIM - MARGIN + offs[0, p]

        def pad_rows(i, _):
            taps[i, 0] = zero_row
            taps[i, PATCH_ROWS + 1] = zero_row
            return 0

        lax.fori_loop(0, span, pad_rows, 0)

        def fill_own(i, _):
            fill_taps(taps, i + RIM, own.at[i, p])
            return 0

        def fill_rim(i, _):
            fill_taps(taps, i + a_base, from_a.at[i, p])
            fill_taps(taps, i + b_base, from_b.at[i, p])
            return 0

        lax.fori_loop(0, planes, fill_own, 0)
        lax.fori_loop(0, RIM, fill_rim, 0)
        sums[...] = jnp.zeros_like(sums)
        squares[...] = jnp.zeros_like(squares)

        def conv_plane(x, _):
            i = first + x
            below = jnp.where(x == 0, zero_plane, i - 1)
            above = jnp.where(x == PATCH_X - 1, zero_plane, i + 1)
            weights = w_all[...]
            for r in range(PATCH_ROWS // 2):
                halves = []
                for h in (r, r + PATCH_ROWS // 2):
                    halves.append(jnp.concatenate([taps[t, h : h + 3].reshape(9 * channels, cols) for t in (below, i, above)], 0))
                out = jnp.dot(weights, jnp.concatenate(halves, 1), preferred_element_type=F32)
                conv[x, r] = out
                one, two = out[:, :cols], out[:, cols:]
                if r == 0:
                    @pl.when(x == 0)
                    def _():
                        shift[...] = 0.5 * (one + two)
                base = shift[...]
                one, two = one - base, two - base
                sums[...] += one + two
                squares[...] += one * one + two * two
            return 0

        lax.fori_loop(0, PATCH_X, conv_plane, 0)
        count = float(PATCH_X * PATCH_ROWS)
        total = sums[...] * (1.0 / count)
        spread = squares[...] - total * sums[...]
        lane_mean = shift[...] + total
        mean = jnp.mean(lane_mean, axis=1, keepdims=True)
        dev = lane_mean - mean
        var = jnp.sum(spread + count * dev * dev, axis=1, keepdims=True) * (1.0 / (count * cols))
        scale = lax.rsqrt(var + EPS) * gain_col
        scale_b = jnp.broadcast_to(scale, (outs, 2 * cols))
        offset_b = jnp.broadcast_to(bias_col - mean * scale, (outs, 2 * cols))
        keep = mask[0, p].astype(F32) * 0.25
        placed[...] = jnp.zeros_like(placed)

        def finish_plane(x, _):
            lower = sub < folds
            table = [[] for _ in range(classes)]
            for r in range(PATCH_ROWS // 2):
                act = conv[x, r] * scale_b + offset_b
                act = jnp.maximum(act, 0.01 * act)
                high = act.astype(BF16)
                low = (act - high.astype(F32)).astype(BF16)
                logits = jnp.dot(head, jnp.concatenate([high, low], 0), preferred_element_type=F32) + hbias
                parts = []
                for k in range(classes):
                    both = logits[k * 2 * folds : (k + 1) * 2 * folds]
                    parts.append(jnp.where(lower, both[:, :cols], both[:, cols:]))
                top = functools.reduce(jnp.maximum, parts)
                parts = [jnp.exp(v - top) for v in parts]
                denom = 1.0 / functools.reduce(jnp.add, parts)
                for k in range(classes):
                    table[k].append(parts[k] * denom)
            window = line * (gauss(jnp.full((2 * folds, cols), x, jnp.int32).astype(F32), PATCH_X) * keep)
            for k in range(classes):
                v = table[k]
                odd = (sub % 2) == 1
                high_pair = (sub % 4) >= 2
                pairs = []
                for q in (0, 2):
                    pairs.append(jnp.where(odd, v[q + 1] + pltpu.roll(v[q + 1], 1, 0), v[q] + pltpu.roll(v[q], 7, 0)))
                full = jnp.where(high_pair, pairs[1] + pltpu.roll(pairs[1], 2, 0), pairs[0] + pltpu.roll(pairs[0], 6, 0))
                placed[first + x, k] = full * window
            return 0

        lax.fori_loop(0, PATCH_X, finish_plane, 0)
        reach = RIM + 1
        kept[p] = placed[pl.ds(RIM - 1, planes + 2)]
        a_first = jnp.where(even, planes + RIM - 1, 0)
        b_first = jnp.where(even, 0, planes + RIM - 1)
        to_a[p] = placed[pl.ds(a_first, reach)]
        to_b[p] = placed[pl.ds(b_first, reach)]


def merge_kernel(slabs, acq, kept, from_a, from_b, out, merged):
    wide = kept.shape[1]
    planes = wide - 2
    classes = kept.shape[2]
    rows, cols = kept.shape[3:]
    slab = lax.axis_index("slab")
    even = lax.rem(slab, 2) == 0
    a_base = jnp.where(even, wide - RIM - 1, 0)
    b_base = jnp.where(even, 0, wide - RIM - 1)
    shape = (rows, cols)
    count = jnp.full(shape, acq[0], jnp.int32).astype(F32)
    anchor = jnp.full(shape, slab * planes, jnp.int32).astype(F32)
    step = planes / jnp.maximum(count - 1.0, 1.0)
    for p in range(PATCHES):
        merged[...] = kept[p]
        merged[pl.ds(a_base, RIM + 1)] += from_a[p]
        merged[pl.ds(b_base, RIM + 1)] += from_b[p]
        table = []
        for j in range(wide):
            parts = [merged[j, k] for k in range(classes)]
            scale = 1.0 / (functools.reduce(jnp.add, parts) + PRIOR)
            parts[0] = parts[0] + PRIOR
            table.append([v * scale for v in parts])
        for s in range(MOST_ACQ):
            place = jnp.clip(anchor + (s * step - 0.5), 0.0, float(slabs * planes - 1)) - anchor
            used = (s < count).astype(F32)
            gains = [jnp.maximum(0.0, 1.0 - jnp.abs(place - (j - 1.0))) * used for j in range(wide)]
            for k in range(classes):
                out[k, s, p * rows : (p + 1) * rows] = functools.reduce(jnp.add, [gains[j] * table[j][k] for j in range(wide)])


def local(slabs, features, conv_weight, norm_gain, norm_bias, head_weight, head_bias, patch_offsets, fg_mask, acq_counts):
    channels, planes, row_total, cols = features.shape
    folds, classes, _ = head_weight.shape
    outs = folds * channels
    pairs_a = [(i, i ^ 1) for i in range(slabs) if (i ^ 1) < slabs]
    pairs_b = [(i, ((i + 1) ^ 1) - 1) for i in range(slabs) if 0 <= ((i + 1) ^ 1) - 1 < slabs]
    cell = (PATCHES, PATCH_ROWS, channels, cols)
    params = pltpu.CompilerParams(vmem_limit_bytes=40 * MIB)
    own, to_a, to_b = pl.pallas_call(
        prep_kernel,
        out_shape=[jax.ShapeDtypeStruct((n,) + cell, BF16) for n in (planes, RIM, RIM)],
        in_specs=[vmem()],
        out_specs=[vmem()] * 3,
        compiler_params=params,
        name="prep",
    )(features)
    from_b = lax.ppermute(to_b, "slab", pairs_b)
    from_a = lax.ppermute(to_a, "slab", pairs_a)
    wide = planes + 2
    tile = (classes, PATCH_ROWS, cols)
    span = planes + 2 * RIM
    kept, send_a, send_b = pl.pallas_call(
        main_kernel,
        out_shape=[jax.ShapeDtypeStruct((PATCHES, n) + tile, F32) for n in (wide, RIM + 1, RIM + 1)],
        in_specs=[smem()] * 2 + [vmem()] * 8,
        out_specs=[vmem()] * 3,
        scratch_shapes=[
            pltpu.VMEM((span + 1, PATCH_ROWS + 2, 3 * channels, cols), BF16),
            pltpu.VMEM((outs, 27 * channels), BF16),
            pltpu.VMEM((PATCH_X, PATCH_ROWS // 2, outs, 2 * cols), F32),
            pltpu.VMEM((span,) + tile, F32),
            pltpu.VMEM((outs, cols), F32),
            pltpu.VMEM((outs, cols), F32),
            pltpu.VMEM((outs, cols), F32),
        ],
        compiler_params=params,
        name="main",
    )(patch_offsets, fg_mask, own, from_a, from_b, jnp.swapaxes(conv_weight, 1, 2), norm_gain, norm_bias, head_weight, head_bias)
    got_b = lax.ppermute(send_b, "slab", pairs_b)
    got_a = lax.ppermute(send_a, "slab", pairs_a)
    return pl.pallas_call(
        functools.partial(merge_kernel, slabs),
        out_shape=jax.ShapeDtypeStruct((classes, MOST_ACQ, row_total, cols), F32),
        in_specs=[smem()] + [vmem()] * 3,
        out_specs=vmem(),
        scratch_shapes=[pltpu.VMEM((wide,) + tile, F32)],
        compiler_params=params,
        name="merge",
    )(acq_counts, kept, got_a, got_b)


def solution(mesh):
    part = ("brain", "slab")
    in_specs = (P(None, part, None, None), P(), P(), P(), P(), P(), P(part, None), P(part, None), P(part))
    body = functools.partial(local, mesh.shape["slab"])
    return jax.shard_map(body, mesh=mesh, in_specs=in_specs, out_specs=P(None, part, None, None), check_vma=False)
```

time: 93.7 us -> 55.5 us (0.59)
  local copies, waits for them, and re-layouts: 32.7 us -> 1.81 us
  Pallas kernels: 0 us -> 26.4 us
  matrix products: 20.3 us -> 0 us
  starting transfers between devices: 16.4 us -> 6.92 us
  waiting for transfers between devices: 10.6 us -> 19.4 us
  other arithmetic: 8.29 us -> 0 us
  between operations: 5.03 us -> 0.76 us
    pallas_call x0 -> x3, Pallas kernels: none -> 26.4 us  [the longest x1 24.9 us: local(): pl.pallas_call(main_kernel, out_shape=[jax.ShapeDtypeStruct((PATCHES, n)...]
    dot_general x9 -> x0, matrix products: 20.3 us -> none  [the longest x6 13.4 us: patch_scores(): jnp.dot(conv_weight[depth_tap], sliced, preferred_element_type=jnp.float32)]
    slice x14 -> x0, local copies, waits for them, and re-layouts: 15 us -> none  [the longest x2 8.17 us: patch_scores(): sliced = stacked[:, depth_tap:depth_tap + length].reshape(9 * channels, -1)]
    ppermute x6 -> x4, starting transfers between devices: 16.4 us -> 6.92 us  [the longest x1 3.06 us: local(): got_b = lax.ppermute(send_b, 'slab', pairs_b)]
    ppermute x6 -> x4, waiting for transfers between devices: 10.6 us -> 19.4 us  [the longest x1 13 us: local(): from_b = lax.ppermute(to_b, 'slab', pairs_b)]
    dynamic_update_slice x2 -> x0, local copies, waits for them, and re-layouts: 6.91 us -> none  [local(): lax.dynamic_update_slice_in_dim(placed_probs, class_probs, patch_start, 1)]
    unnamed x34 -> x17, local copies, waits for them, and re-layouts: 7.19 us -> 1.81 us
    select_n x1 -> x0, other arithmetic: 4.13 us -> none  [patch_scores(): activated = jnp.where(normed > 0, normed, 0.01 * normed)]
  transfers between devices with their start and end apart: 6 -> 4, of which waited for: 3 -> 2; matrix products, arithmetic and copies ran while one was open for 6% -> 0% of each run, Pallas kernels for 0% -> 0%
where the time goes in v1:
time: 55.5 us; the launch traced here: 55.3 us
  Pallas kernels  26.4 us (48%)
  waiting for transfers between devices  19.4 us (35%)
  starting transfers between devices  6.92 us (12%)
  local copies, waits for them, and re-layouts  1.81 us (3%)
  between operations  0.76 us (1%)
    pallas_call x1, Pallas kernels, local(): pl.pallas_call(main_kernel, out_shape=[jax.ShapeDtypeStruct((PATCHES, n)...  24.9 us
    ppermute x1, waiting for transfers between devices, local(): from_b = lax.ppermute(to_b, 'slab', pairs_b)  13 us
    ppermute x1, waiting for transfers between devices, local(): got_b = lax.ppermute(send_b, 'slab', pairs_b)  6.43 us
    ppermute x1, starting transfers between devices, local(): got_b = lax.ppermute(send_b, 'slab', pairs_b)  3.06 us
    ppermute x1, starting transfers between devices, local(): from_b = lax.ppermute(to_b, 'slab', pairs_b)  3.05 us
    unnamed x17, local copies, waits for them, and re-layouts  1.81 us
  transfers between devices with their start and end apart: 4, of which 2 were waited for; matrix products, arithmetic and copies ran while one was open for 0% of the time, Pallas kernels for 0%

profile of v1, /device:TPU:11, one launch (start us, length us, event | category | flops | bytes accessed | tf_op | source)
XLA Modules:
  0.0 55.3 jit_solution(7032123411432074595)
XLA Ops:
  0.0 0.0 copy-start
  0.0 1.1 %copy-done = bf16[32,6,16,128]{3,2,1,0:T(8,128)(2,1)S(1)} copy-done((bf16[32,6,16,128]{3,2,1,0:T(8,128)(2,1)S(1)}, bf16[32,6,16,128]{3,2,1,0:T(8,128)(2,1)}, u32[]{:S(2)}) %copy-start) | copy-done | bytes 786456
  1.1 0.0 copy-start.7
  1.1 0.0 copy-start.1
  1.1 0.5 prep.1
  1.6 0.7 %collective-permute-start = (bf16[4,2,8,32,128]{4,3,2,1,0:T(8,128)(2,1)S(1)}, bf16[4,2,8,32,128]{4,3,2,1,0:T(8,128)(2,1)S(1)}, u32[]{:S(2)}, u32[]{:S(2)}) collective-permute-start(bf16[4,2,8,32,128]{4,3,2,1,0:T(8,128)(2,1)S(1)} %get-tuple-element.12), channel_id=1, source_target_pairs={{0,1},{1,0},{2,3},{3,2},{4,5},{5,4},{6,7},{7,6},{8,9},{9,8},{10,11... | collective-permute-start | bytes 1572872 | tf_op jit(solution)/shard_map/ppermute | solution.py:254
  2.3 3.0 %collective-permute-start.1 = (bf16[4,2,8,32,128]{4,3,2,1,0:T(8,128)(2,1)S(1)}, bf16[4,2,8,32,128]{4,3,2,1,0:T(8,128)(2,1)S(1)}, u32[]{:S(2)}, u32[]{:S(2)}) collective-permute-start(bf16[4,2,8,32,128]{4,3,2,1,0:T(8,128)(2,1)S(1)} %get-tuple-element.13), channel_id=1, source_target_pairs={{1,2},{2,1},{3,4},{4,3},{5,6},{6,5},{7,8},{8,7},{9,10},{10,9},{11,... | collective-permute-start | bytes 1572872 | tf_op jit(solution)/shard_map/ppermute | solution.py:253
  5.4 0.0 copy-done.7
  5.4 0.0 copy-start.3
  5.4 0.0 copy-start.4
  5.4 0.0 copy-start.2
  5.4 0.0 collective-permute-done.from_a
  5.5 13.0 %collective-permute-done.1.from_b = bf16[4,2,8,32,128]{4,3,2,1,0:T(8,128)(2,1)S(1)} collective-permute-done((bf16[4,2,8,32,128]{4,3,2,1,0:T(8,128)(2,1)S(1)}, bf16[4,2,8,32,128]{4,3,2,1,0:T(8,128)(2,1)S(1)}, u32[]{:S(2)}, u32[]{:S(2)}) %collective-permute-start.1) | collective-permute-done | bytes 524320 | tf_op jit(solution)/shard_map/ppermute | solution.py:253
  18.4 0.0 copy-start.5
  18.4 0.0 copy-start.6
  18.4 0.0 copy-done.1
  18.4 0.0 copy-done.3
  18.5 0.0 copy-done.4
  18.5 0.0 copy-done.2
  18.5 0.6 %copy-done.5 = s32[1,2]{1,0:T(1,128)S(1)} copy-done((s32[1,2]{1,0:T(1,128)S(1)}, s32[1,2]{1,0:T(1,128)}, u32[]{:S(2)}) %copy-start.5) | copy-done | bytes 32
  19.1 0.0 copy-done.6
  19.1 24.9 %main.1 = (f32[2,8,6,8,128]{4,3,2,1,0:T(8,128)S(1)}, f32[2,5,6,8,128]{4,3,2,1,0:T(8,128)S(1)}, f32[2,5,6,8,128]{4,3,2,1,0:T(8,128)S(1)}) custom-call(s32[1,2]{1,0:T(1,128)S(1)} %copy-done.5, s32[1,2]{1,0:T(1,128)S(1)} %copy-done.6, bf16[6,2,8,32,128]{4,3,2,1,0:T(8,128)(2,1)S(1)} %get-tuple-element.11.own, ...), custom_call_target="tpu_custom_call" | custom-call | tf_op jit(solution)/shard_map/main/pallas_call | solution.py:258
  44.0 0.1 collective-permute-start.2
  44.0 3.1 %collective-permute-start.3 = (f32[2,5,6,8,128]{4,3,2,1,0:T(8,128)S(1)}, f32[2,5,6,8,128]{4,3,2,1,0:T(8,128)S(1)}, u32[]{:S(2)}, u32[]{:S(2)}) collective-permute-start(f32[2,5,6,8,128]{4,3,2,1,0:T(8,128)S(1)} %get-tuple-element.16), channel_id=1, source_target_pairs={{1,2},{2,1},{3,4},{4,3},{5,6},{6,5},{7,8},{8,7},{9,10},{10,9},{11,... | collective-permute-start | bytes 737288 | tf_op jit(solution)/shard_map/ppermute | solution.py:275
  47.8 0.0 collective-permute-done.2.from_a
  47.8 6.4 %collective-permute-done.3.from_b = f32[2,5,6,8,128]{4,3,2,1,0:T(8,128)S(1)} collective-permute-done((f32[2,5,6,8,128]{4,3,2,1,0:T(8,128)S(1)}, f32[2,5,6,8,128]{4,3,2,1,0:T(8,128)S(1)}, u32[]{:S(2)}, u32[]{:S(2)}) %collective-permute-start.3) | collective-permute-done | bytes 245792 | tf_op jit(solution)/shard_map/ppermute | solution.py:275
  54.2 1.1 %merge.1 = f32[6,8,16,128]{3,2,1,0:T(8,128)} custom-call(s32[1]{0:T(128)S(6)} %copy.11.acq, f32[2,8,6,8,128]{4,3,2,1,0:T(8,128)S(1)} %get-tuple-element.14.kept, f32[2,5,6,8,128]{4,3,2,1,0:T(8,128)S(1)} %collective-permute-done.2.from_a, f32[2,5,6,8,128]{4,3,2,1,0:T(8,128)S(1)} %collective-permute-done.3.from_b), custom_call_target="tpu_custom_call" | custom-call | tf_op jit(solution)/shard_map/merge/pallas_call | solution.py:277
  (1 shorter events, 0.0 us)
Async XLA Ops:
  0.0 1.1 %copy-start = (bf16[32,6,16,128]{3,2,1,0:T(8,128)(2,1)S(1)}, bf16[32,6,16,128]{3,2,1,0:T(8,128)(2,1)}, u32[]{:S(2)}) copy-start(bf16[32,6,16,128]{3,2,1,0:T(8,128)(2,1)} %feat.1) | copy-start | bytes 2359300
  1.1 4.3 %copy-start.7 = (bf16[4,6,32]{2,0,1:T(4,128)(2,1)S(1)}, bf16[4,6,32]{2,0,1:T(4,128)(2,1)}, u32[]{:S(2)}) copy-start(bf16[4,6,32]{2,0,1:T(4,128)(2,1)} %param.13) | copy-start | bytes 4612
  1.1 17.3 %copy-start.1 = (bf16[3,128,288]{1,2,0:T(8,128)(2,1)S(1)}, bf16[3,128,288]{1,2,0:T(8,128)(2,1)}, u32[]{:S(2)}) copy-start(bf16[3,128,288]{1,2,0:T(8,128)(2,1)} %param.10) | copy-start | bytes 663556
  1.6 3.9 %collective-permute-start = (bf16[4,2,8,32,128]{4,3,2,1,0:T(8,128)(2,1)S(1)}, bf16[4,2,8,32,128]{4,3,2,1,0:T(8,128)(2,1)S(1)}, u32[]{:S(2)}, u32[]{:S(2)}) collective-permute-start(bf16[4,2,8,32,128]{4,3,2,1,0:T(8,128)(2,1)S(1)} %get-tuple-element.12), channel_id=1, source_target_pairs={{0,1},{1,0},{2,3},{3,2},{4,5},{5,4},{6,7},{7,6},{8,9},{9,8},{10,11... | collective-permute-start | bytes 1572872 | tf_op jit(solution)/shard_map/ppermute | solution.py:254
  2.3 16.1 %collective-permute-start.1 = (bf16[4,2,8,32,128]{4,3,2,1,0:T(8,128)(2,1)S(1)}, bf16[4,2,8,32,128]{4,3,2,1,0:T(8,128)(2,1)S(1)}, u32[]{:S(2)}, u32[]{:S(2)}) collective-permute-start(bf16[4,2,8,32,128]{4,3,2,1,0:T(8,128)(2,1)S(1)} %get-tuple-element.13), channel_id=1, source_target_pairs={{1,2},{2,1},{3,4},{4,3},{5,6},{6,5},{7,8},{8,7},{9,10},{10,9},{11,... | collective-permute-start | bytes 1572872 | tf_op jit(solution)/shard_map/ppermute | solution.py:253
  5.4 13.1 %copy-start.3 = (f32[4,32]{1,0:T(4,128)S(1)}, f32[4,32]{1,0:T(4,128)}, u32[]{:S(2)}) copy-start(f32[4,32]{1,0:T(4,128)} %nbias.1) | copy-start | bytes 1540
  5.4 13.0 %copy-start.4 = (f32[4,6]{1,0:T(4,128)S(1)}, f32[4,6]{1,0:T(4,128)}, u32[]{:S(2)}) copy-start(f32[4,6]{1,0:T(4,128)} %head_b.1) | copy-start | bytes 292
  5.4 13.0 %copy-start.2 = (f32[4,32]{1,0:T(4,128)S(1)}, f32[4,32]{1,0:T(4,128)}, u32[]{:S(2)}) copy-start(f32[4,32]{1,0:T(4,128)} %gain.1) | copy-start | bytes 1540
  18.4 0.7 %copy-start.5 = (s32[1,2]{1,0:T(1,128)S(1)}, s32[1,2]{1,0:T(1,128)}, u32[]{:S(2)}) copy-start(s32[1,2]{1,0:T(1,128)} %offs.1) | copy-start | bytes 28
  18.4 0.7 %copy-start.6 = (s32[1,2]{1,0:T(1,128)S(1)}, s32[1,2]{1,0:T(1,128)}, u32[]{:S(2)}) copy-start(s32[1,2]{1,0:T(1,128)} %mask.1) | copy-start | bytes 28
  44.0 3.8 %collective-permute-start.2 = (f32[2,5,6,8,128]{4,3,2,1,0:T(8,128)S(1)}, f32[2,5,6,8,128]{4,3,2,1,0:T(8,128)S(1)}, u32[]{:S(2)}, u32[]{:S(2)}) collective-permute-start(f32[2,5,6,8,128]{4,3,2,1,0:T(8,128)S(1)} %get-tuple-element.15), channel_id=1, source_target_pairs={{0,1},{1,0},{2,3},{3,2},{4,5},{5,4},{6,7},{7,6},{8,9},{9,8},{10,11... | collective-permute-start | bytes 737288 | tf_op jit(solution)/shard_map/ppermute | solution.py:276
  44.0 10.1 %collective-permute-start.3 = (f32[2,5,6,8,128]{4,3,2,1,0:T(8,128)S(1)}, f32[2,5,6,8,128]{4,3,2,1,0:T(8,128)S(1)}, u32[]{:S(2)}, u32[]{:S(2)}) collective-permute-start(f32[2,5,6,8,128]{4,3,2,1,0:T(8,128)S(1)} %get-tuple-element.16), channel_id=1, source_target_pairs={{1,2},{2,1},{3,4},{4,3},{5,6},{6,5},{7,8},{8,7},{9,10},{10,9},{11,... | collective-permute-start | bytes 737288 | tf_op jit(solution)/shard_map/ppermute | solution.py:275

commit v2 on v1

v2 whole, which is shorter than its diff:
```python
import functools
import jax
import jax.numpy as jnp
from jax import lax
from jax.experimental import pallas as pl
from jax.experimental.pallas import tpu as pltpu
from jax.sharding import PartitionSpec as P

PATCHES = 2
PATCH_ROWS = 8
MARGIN = 2
RIM = 4
PATCH_X = 10
MOST_ACQ = 8
PRIOR = 0.1
EPS = 1e-05
F32 = jnp.float32
BF16 = jnp.bfloat16
MIB = 1 << 20


def vmem():
    return pl.BlockSpec(memory_space=pltpu.VMEM)


def smem():
    return pl.BlockSpec(memory_space=pltpu.SMEM)


def prep_kernel(feat, own, to_a, *to_b):
    channels, planes, rows, cols = feat.shape
    even = lax.rem(lax.axis_index("slab"), 2) == 0
    a_first = jnp.where(even, planes - RIM, 0)
    b_first = jnp.where(even, 0, planes - RIM)
    for x in range(planes):
        turned = jnp.swapaxes(feat[:, x].astype(F32), 0, 1).astype(BF16)
        for p in range(PATCHES):
            own[p, x] = turned[p * PATCH_ROWS : (p + 1) * PATCH_ROWS]
    for p in range(PATCHES):
        to_a[p] = own[p, pl.ds(a_first, RIM)]
        to_b[p][...] = own[p, pl.ds(b_first, RIM)]


def column_of(table, folds, width):
    diag = lax.broadcasted_iota(jnp.int32, (width, width), 0) == lax.broadcasted_iota(jnp.int32, (width, width), 1)
    parts = []
    for f in range(folds):
        row = jnp.broadcast_to(table[f : f + 1, :], (width, width))
        parts.append(jnp.sum(jnp.where(diag, row, 0.0), axis=1, keepdims=True))
    return jnp.concatenate(parts, 0)


def head_tables(head_w, head_b, folds, classes, channels):
    rows = classes * 2 * folds
    row = lax.broadcasted_iota(jnp.int32, (rows, classes), 0)
    cls = lax.broadcasted_iota(jnp.int32, (rows, classes), 1)
    brow = lax.broadcasted_iota(jnp.int32, (rows, classes), 0)
    lane = lax.broadcasted_iota(jnp.int32, (channels, folds * channels), 1)
    chan = lax.broadcasted_iota(jnp.int32, (channels, folds * channels), 0)
    table = jnp.zeros((rows, folds * channels), F32)
    bias = jnp.zeros((rows, 1), F32)
    for f in range(folds):
        pick = (row // (2 * folds) == cls) & (row % folds == f)
        part = jnp.dot(pick.astype(F32).astype(BF16), head_w[f], preferred_element_type=F32).astype(BF16)
        place = (lane == chan + f * channels).astype(F32).astype(BF16)
        table = table + jnp.dot(part, place, preferred_element_type=F32)
        bias = bias + jnp.sum(jnp.where(pick, jnp.broadcast_to(head_b[f : f + 1, :], (rows, classes)), 0.0), axis=1, keepdims=True)
    table = table.astype(BF16)
    return jnp.concatenate([table, table], 1), bias


def gauss(position, length):
    scaled = (position - (length - 1) / 2.0) / (length / 4.0)
    return jnp.exp(-0.5 * scaled * scaled)


def fill_taps(taps, plane, source):
    rows, channels, cols = source.shape
    lane = lax.broadcasted_iota(jnp.int32, (channels, cols), 1)
    for h in range(rows):
        value = source[h]
        wide = value.astype(F32)
        left = jnp.where(lane == 0, 0.0, pltpu.roll(wide, 1, 1)).astype(BF16)
        right = jnp.where(lane == cols - 1, 0.0, pltpu.roll(wide, cols - 1, 1)).astype(BF16)
        taps[plane, h + 1] = jnp.concatenate([left, value, right], 0)


def conv_planes(first, begin, end, fresh, taps, w_all, conv, stats):
    zero_plane = taps.shape[0] - 1
    cols = taps.shape[-1]

    def one_plane(x):
        i = first + x
        below = jnp.where(x == 0, zero_plane, i - 1)
        above = jnp.where(x == PATCH_X - 1, zero_plane, i + 1)
        weights = w_all[...]
        for r in range(PATCH_ROWS // 2):
            halves = []
            for h in (r, r + PATCH_ROWS // 2):
                halves.append(jnp.concatenate([taps[t, h : h + 3].reshape(-1, cols) for t in (below, i, above)], 0))
            out = jnp.dot(weights, jnp.concatenate(halves, 1), preferred_element_type=F32)
            conv[x, r] = out
            one, two = out[:, :cols], out[:, cols:]
            base = stats[0]
            if fresh and r == 0:
                base = jnp.where(x == begin, 0.5 * (one + two), base)
                stats[0] = base
            one, two = one - base, two - base
            stats[1] += one + two
            stats[2] += one * one + two * two

    def two_planes(y, _):
        one_plane(begin + 2 * y)
        one_plane(begin + 2 * y + 1)
        return 0

    def last_plane(y, _):
        one_plane(end - 1)
        return 0

    total = end - begin
    lax.fori_loop(0, total // 2, two_planes, 0)
    lax.fori_loop(0, lax.rem(total, 2), last_plane, 0)


def patch_plan(offs, p, planes):
    even = lax.rem(lax.axis_index("slab"), 2) == 0
    first = RIM - MARGIN + offs[0, p]
    foreign = jnp.where(even, RIM - first, first + PATCH_X - RIM - planes)
    foreign = foreign + jnp.minimum(foreign, 1)
    return even, first, jnp.where(even, foreign, 0), jnp.where(even, PATCH_X, PATCH_X - foreign)


def pre_kernel(offs, own, from_a, wt, gain, nbias, head_w, head_b, taps0, taps1, conv0, conv1, stats0, stats1, w_all, head, hbias, scales):
    planes = own.shape[1]
    folds, classes, channels = head_w.shape
    outs = folds * channels
    cols = own.shape[-1]
    span = planes + 2 * RIM
    even = lax.rem(lax.axis_index("slab"), 2) == 0
    a_base = jnp.where(even, RIM + planes, 0)
    wide_w = jnp.concatenate([wt[a].astype(F32) for a in range(3)], 0)
    w_all[...] = jnp.transpose(wide_w).astype(BF16)
    table, bias = head_tables(head_w, head_b, folds, classes, channels)
    head[...] = table
    hbias[...] = jnp.broadcast_to(bias, hbias.shape)
    scales[0] = jnp.broadcast_to(column_of(gain, folds, channels), (outs, cols))
    scales[1] = jnp.broadcast_to(column_of(nbias, folds, channels), (outs, cols))
    zero_row = jnp.zeros((3 * channels, cols), BF16)
    for p, (taps, conv, stats) in enumerate(((taps0, conv0, stats0), (taps1, conv1, stats1))):
        taps[span] = jnp.zeros(taps.shape[1:], BF16)

        def pad_rows(i, _):
            taps[i, 0] = zero_row
            taps[i, PATCH_ROWS + 1] = zero_row
            return 0

        def fill_own(i, _):
            fill_taps(taps, i + RIM, own.at[p, i])
            return 0

        def fill_a(i, _):
            fill_taps(taps, i + a_base, from_a.at[p, i])
            return 0

        lax.fori_loop(0, span, pad_rows, 0)
        lax.fori_loop(0, planes, fill_own, 0)
        lax.fori_loop(0, RIM, fill_a, 0)
        stats[...] = jnp.zeros_like(stats)
        _, first, begin, end = patch_plan(offs, p, planes)
        conv_planes(first, begin, end, True, taps, w_all, conv, stats)


def post_kernel(p, offs, mask, from_b, taps_in, conv_in, stats_in, w_all, head, hbias, scales, kept, to_a, to_b, taps, conv, stats, placed):
    planes = kept.shape[0] - 2
    span = taps.shape[0] - 1
    classes = kept.shape[1]
    outs, cols = stats.shape[1:]
    folds = head.shape[0] // classes // 2
    even, first, begin, end = patch_plan(offs, p, planes)
    b_base = jnp.where(even, 0, RIM + planes)

    def fill_b(i, _):
        fill_taps(taps, i + b_base, from_b.at[i])
        return 0

    lax.fori_loop(0, RIM, fill_b, 0)
    conv_planes(first, jnp.where(even, 0, end), jnp.where(even, begin, PATCH_X), False, taps, w_all, conv, stats)
    count = float(PATCH_X * PATCH_ROWS)
    total = stats[1] * (1.0 / count)
    spread = stats[2] - total * stats[1]
    lane_mean = stats[0] + total
    mean = jnp.mean(lane_mean, axis=1, keepdims=True)
    dev = lane_mean - mean
    var = jnp.sum(spread + count * dev * dev, axis=1, keepdims=True) * (1.0 / (count * cols))
    scale = lax.rsqrt(var + EPS) * scales[0, :, :1]
    scale_b = jnp.broadcast_to(scale, (outs, 2 * cols))
    offset_b = jnp.broadcast_to(scales[1, :, :1] - mean * scale, (outs, 2 * cols))
    keep = mask[0, p].astype(F32) * (1.0 / folds)
    placed[...] = jnp.zeros_like(placed)
    sub = lax.broadcasted_iota(jnp.int32, (2 * folds, cols), 0)
    lane = lax.broadcasted_iota(jnp.int32, (2 * folds, cols), 1)
    line = gauss(sub.astype(F32), PATCH_ROWS) * gauss(lane.astype(F32), cols)

    def finish_plane(x, _):
        lower = sub < folds
        table = [[] for _ in range(classes)]
        for r in range(PATCH_ROWS // 2):
            act = conv[x, r] * scale_b + offset_b
            act = jnp.maximum(act, 0.01 * act)
            high = act.astype(BF16)
            low = (act - high.astype(F32)).astype(BF16)
            logits = jnp.dot(head[...], jnp.concatenate([high, low], 0), preferred_element_type=F32) + hbias[...]
            parts = []
            for k in range(classes):
                both = logits[k * 2 * folds : (k + 1) * 2 * folds]
                parts.append(jnp.where(lower, both[:, :cols], both[:, cols:]))
            top = functools.reduce(jnp.maximum, parts)
            parts = [jnp.exp(v - top) for v in parts]
            denom = 1.0 / functools.reduce(jnp.add, parts)
            for k in range(classes):
                table[k].append(parts[k] * denom)
        window = line * (gauss(jnp.full((2 * folds, cols), x, jnp.int32).astype(F32), PATCH_X) * keep)
        odd = (sub % 2) == 1
        high_pair = (sub % 4) >= 2
        for k in range(classes):
            v = table[k]
            pairs = []
            for q in (0, 2):
                pairs.append(jnp.where(odd, v[q + 1] + pltpu.roll(v[q + 1], 1, 0), v[q] + pltpu.roll(v[q], 7, 0)))
            full = jnp.where(high_pair, pairs[1] + pltpu.roll(pairs[1], 2, 0), pairs[0] + pltpu.roll(pairs[0], 6, 0))
            placed[first + x, k] = full * window
        return 0

    lax.fori_loop(0, PATCH_X, finish_plane, 0)
    reach = RIM + 1
    kept[...] = placed[pl.ds(RIM - 1, planes + 2)]
    to_a[...] = placed[pl.ds(jnp.where(even, planes + RIM - 1, 0), reach)]
    to_b[...] = placed[pl.ds(jnp.where(even, 0, planes + RIM - 1), reach)]


def merge_kernel(slabs, acq, *refs):
    ins, out, merged = refs[:-2], refs[-2], refs[-1]
    wide = ins[0].shape[0]
    planes = wide - 2
    classes, rows, cols = ins[0].shape[1:]
    slab = lax.axis_index("slab")
    even = lax.rem(slab, 2) == 0
    a_base = jnp.where(even, wide - RIM - 1, 0)
    b_base = jnp.where(even, 0, wide - RIM - 1)
    shape = (rows, cols)
    count = jnp.full(shape, acq[0], jnp.int32).astype(F32)
    anchor = jnp.full(shape, slab * planes, jnp.int32).astype(F32)
    step = planes / jnp.maximum(count - 1.0, 1.0)
    for p in range(PATCHES):
        kept, from_a, from_b = ins[3 * p : 3 * p + 3]
        merged[...] = kept[...]
        merged[pl.ds(a_base, RIM + 1)] += from_a[...]
        merged[pl.ds(b_base, RIM + 1)] += from_b[...]
        table = []
        for j in range(wide):
            parts = [merged[j, k] for k in range(classes)]
            scale = 1.0 / (functools.reduce(jnp.add, parts) + PRIOR)
            parts[0] = parts[0] + PRIOR
            table.append([v * scale for v in parts])
        for s in range(MOST_ACQ):
            place = jnp.clip(anchor + (s * step - 0.5), 0.0, float(slabs * planes - 1)) - anchor
            used = (s < count).astype(F32)
            gains = [jnp.maximum(0.0, 1.0 - jnp.abs(place - (j - 1.0))) * used for j in range(wide)]
            for k in range(classes):
                out[k, s, p * rows : (p + 1) * rows] = functools.reduce(jnp.add, [gains[j] * table[j][k] for j in range(wide)])


def local(slabs, features, conv_weight, norm_gain, norm_bias, head_weight, head_bias, patch_offsets, fg_mask, acq_counts):
    channels, planes, row_total, cols = features.shape
    folds, classes, _ = head_weight.shape
    outs = folds * channels
    pairs_a = [(i, i ^ 1) for i in range(slabs) if (i ^ 1) < slabs]
    pairs_b = [(i, ((i + 1) ^ 1) - 1) for i in range(slabs) if 0 <= ((i + 1) ^ 1) - 1 < slabs]
    shaped = jax.ShapeDtypeStruct
    cell = (PATCH_ROWS, channels, cols)
    params = pltpu.CompilerParams(vmem_limit_bytes=24 * MIB)
    own, to_a, *to_b = pl.pallas_call(
        prep_kernel,
        out_shape=[shaped((PATCHES, planes) + cell, BF16), shaped((PATCHES, RIM) + cell, BF16)] + [shaped((RIM,) + cell, BF16)] * PATCHES,
        in_specs=[vmem()],
        out_specs=[vmem()] * (2 + PATCHES),
        compiler_params=params,
        name="prep",
    )(features)
    from_a = lax.ppermute(to_a, "slab", pairs_a)
    from_b = [lax.ppermute(v, "slab", pairs_b) for v in to_b]
    wide = planes + 2
    tile = (classes, PATCH_ROWS, cols)
    span = planes + 2 * RIM
    taps_shape = shaped((span + 1, PATCH_ROWS + 2, 3 * channels, cols), BF16)
    conv_shape = shaped((PATCH_X, PATCH_ROWS // 2, outs, 2 * cols), F32)
    stats_shape = shaped((3, outs, cols), F32)
    table_shapes = [shaped((outs, 27 * channels), BF16), shaped((classes * 2 * folds, 2 * outs), BF16), shaped((classes * 2 * folds, 2 * cols), F32), shaped((2, outs, cols), F32)]
    made = pl.pallas_call(
        pre_kernel,
        out_shape=[taps_shape] * 2 + [conv_shape] * 2 + [stats_shape] * 2 + table_shapes,
        in_specs=[smem()] + [vmem()] * 7,
        out_specs=[vmem()] * 10,
        compiler_params=params,
        name="pre",
    )(patch_offsets, own, from_a, jnp.swapaxes(conv_weight, 1, 2), norm_gain, norm_bias, head_weight, head_bias)
    merged_in = []
    for p in range(PATCHES):
        kept, send_a, send_b, *_ = pl.pallas_call(
            functools.partial(post_kernel, p),
            out_shape=[shaped((n,) + tile, F32) for n in (wide, RIM + 1, RIM + 1)] + [taps_shape, conv_shape, stats_shape],
            in_specs=[smem()] * 2 + [vmem()] * 8,
            out_specs=[vmem()] * 6,
            input_output_aliases={3: 3, 4: 4, 5: 5},
            scratch_shapes=[pltpu.VMEM((span,) + tile, F32)],
            compiler_params=params,
            name=f"post{p}",
        )(patch_offsets, fg_mask, from_b[p], made[p], made[2 + p], made[4 + p], *made[6:])
        merged_in += [kept, lax.ppermute(send_a, "slab", pairs_a), lax.ppermute(send_b, "slab", pairs_b)]
    return pl.pallas_call(
        functools.partial(merge_kernel, slabs),
        out_shape=shaped((classes, MOST_ACQ, row_total, cols), F32),
        in_specs=[smem()] + [vmem()] * (3 * PATCHES),
        out_specs=vmem(),
        scratch_shapes=[pltpu.VMEM((wide,) + tile, F32)],
        compiler_params=params,
        name="merge",
    )(acq_counts, *merged_in)


def solution(mesh):
    part = ("brain", "slab")
    in_specs = (P(None, part, None, None), P(), P(), P(), P(), P(), P(part, None), P(part, None), P(part))
    body = functools.partial(local, mesh.shape["slab"])
    return jax.shard_map(body, mesh=mesh, in_specs=in_specs, out_specs=P(None, part, None, None), check_vma=False)
```

time: 55.5 us -> 47.2 us (0.85)
  waiting for transfers between devices: 19.4 us -> 4.11 us
  starting transfers between devices: 6.92 us -> 14.4 us
  Pallas kernels: 26.4 us -> 21.2 us
  local copies, waits for them, and re-layouts: 1.81 us -> 6.11 us
    ppermute x3 -> x6, waiting for transfers between devices: 19.4 us -> 4.11 us  [the longest x2 4.1 us: local(): lax.ppermute(send_b, 'slab', pairs_b)]
    ppermute x3 -> x6, starting transfers between devices: 6.17 us -> 13.6 us  [the longest x2 5.93 us: local(): lax.ppermute(send_b, 'slab', pairs_b)]
    pallas_call x3 -> x5, Pallas kernels: 26.4 us -> 21.2 us  [the longest x2 11.4 us: local(): pl.pallas_call(functools.partial(post_kernel, p), out_shape=[shaped((n,)...]
    unnamed x17 -> x15, local copies, waits for them, and re-layouts: 1.81 us -> 6.11 us
  transfers between devices with their start and end apart: 4 -> 7, of which waited for: 2 -> 1; matrix products, arithmetic and copies ran while one was open for 0% -> 1% of each run, Pallas kernels for 0% -> 42%
where the time goes in v2:
time: 47.2 us; the launch traced here: 46.6 us
  Pallas kernels  21.2 us (45%)
  starting transfers between devices  14.4 us (31%)
  local copies, waits for them, and re-layouts  6.11 us (13%)
  waiting for transfers between devices  4.11 us (9%)
  between operations  0.77 us (2%)
    pallas_call x2, Pallas kernels, local(): pl.pallas_call(functools.partial(post_kernel, p), out_shape=[shaped((n,)...  11.4 us
    pallas_call x1, Pallas kernels, local(): pl.pallas_call(pre_kernel, out_shape=[taps_shape] * 2 + [conv_shape] * 2...  8.29 us
    unnamed x15, local copies, waits for them, and re-layouts  6.11 us
    ppermute x2, starting transfers between devices, local(): lax.ppermute(send_b, 'slab', pairs_b)  5.93 us
    ppermute x2, starting transfers between devices, local(): from_b = [lax.ppermute(v, 'slab', pairs_b) for v in to_b]  5.55 us
    ppermute x2, waiting for transfers between devices, local(): lax.ppermute(send_b, 'slab', pairs_b)  4.1 us
    ppermute x2, starting transfers between devices, local(): lax.ppermute(send_a, 'slab', pairs_a)  2.16 us
    pallas_call x1, Pallas kernels, local(): pl.pallas_call(functools.partial(merge_kernel, slabs), out_shape=shaped((...  1.1 us
  transfers between devices with their start and end apart: 7, of which 1 were waited for; matrix products, arithmetic and copies ran while one was open for 1% of the time, Pallas kernels for 42%

profile of v2, /device:TPU:11, one launch (start us, length us, event | category | flops | bytes accessed | tf_op | source)
XLA Modules:
  0.0 46.6 jit_solution(14717053448928645675)
XLA Ops:
  0.0 0.0 copy-start
  0.0 1.1 %copy-done = bf16[32,6,16,128]{3,2,1,0:T(8,128)(2,1)S(1)} copy-done((bf16[32,6,16,128]{3,2,1,0:T(8,128)(2,1)S(1)}, bf16[32,6,16,128]{3,2,1,0:T(8,128)(2,1)}, u32[]{:S(2)}) %copy-start) | copy-done | bytes 786456
  1.1 0.4 prep.1
  1.6 0.7 %collective-permute-start.1 = (bf16[2,4,8,32,128]{4,3,2,1,0:T(8,128)(2,1)S(1)}, bf16[2,4,8,32,128]{4,3,2,1,0:T(8,128)(2,1)S(1)}, u32[]{:S(2)}, u32[]{:S(2)}) collective-permute-start(bf16[2,4,8,32,128]{4,3,2,1,0:T(8,128)(2,1)S(1)} %get-tuple-element.27), channel_id=1, source_target_pairs={{0,1},{1,0},{2,3},{3,2},{4,5},{5,4},{6,7},{7,6},{8,9},{9,8},{10,11... | collective-permute-start | bytes 1572872 | tf_op jit(solution)/shard_map/ppermute | solution.py:291
  2.3 3.0 %collective-permute-start.4 = (bf16[4,8,32,128]{3,2,1,0:T(8,128)(2,1)S(1)}, bf16[4,8,32,128]{3,2,1,0:T(8,128)(2,1)S(1)}, u32[]{:S(2)}, u32[]{:S(2)}) collective-permute-start(bf16[4,8,32,128]{3,2,1,0:T(8,128)(2,1)S(1)} %get-tuple-element.38), channel_id=1, source_target_pairs={{1,2},{2,1},{3,4},{4,3},{5,6},{6,5},{7,8},{8,7},{9,10},{10,9},{11,... | collective-permute-start | bytes 786440 | tf_op jit(solution)/shard_map/ppermute | solution.py:292
  5.4 2.5 %collective-permute-start = (bf16[4,8,32,128]{3,2,1,0:T(8,128)(2,1)S(1)}, bf16[4,8,32,128]{3,2,1,0:T(8,128)(2,1)S(1)}, u32[]{:S(2)}, u32[]{:S(2)}) collective-permute-start(bf16[4,8,32,128]{3,2,1,0:T(8,128)(2,1)S(1)} %get-tuple-element.25), channel_id=1, source_target_pairs={{1,2},{2,1},{3,4},{4,3},{5,6},{6,5},{7,8},{8,7},{9,10},{10,9},{11,... | collective-permute-start | bytes 786440 | tf_op jit(solution)/shard_map/ppermute | solution.py:292
  7.9 0.7 %copy.16.head_w = bf16[4,6,32]{2,1,0:T(8,128)(2,1)S(1)} copy(bf16[4,6,32]{2,0,1:T(4,128)(2,1)} %param.13) | data formatting | bytes 3072 | tf_op args[4]
  8.6 0.0 collective-permute-done.1.from_a
  8.6 0.0 copy-start.1
  8.6 0.9 %copy-done.1 = bf16[3,128,288]{1,2,0:T(8,128)(2,1)S(1)} copy-done((bf16[3,128,288]{1,2,0:T(8,128)(2,1)S(1)}, bf16[3,128,288]{1,2,0:T(8,128)(2,1)}, u32[]{:S(2)}) %copy-start.1) | copy-done | bytes 221208
  9.5 0.0 copy-start.2
  9.5 0.7 %copy-done.2 = s32[1,2]{1,0:T(1,128)S(1)} copy-done((s32[1,2]{1,0:T(1,128)S(1)}, s32[1,2]{1,0:T(1,128)}, u32[]{:S(2)}) %copy-start.2) | copy-done | bytes 32
  10.2 0.0 copy-start.3
  10.2 0.7 %copy-done.3 = f32[4,32]{1,0:T(4,128)S(1)} copy-done((f32[4,32]{1,0:T(4,128)S(1)}, f32[4,32]{1,0:T(4,128)}, u32[]{:S(2)}) %copy-start.3) | copy-done | bytes 536
  10.9 0.0 copy-start.4
  10.9 0.7 %copy-done.4 = f32[4,32]{1,0:T(4,128)S(1)} copy-done((f32[4,32]{1,0:T(4,128)S(1)}, f32[4,32]{1,0:T(4,128)}, u32[]{:S(2)}) %copy-start.4) | copy-done | bytes 536
  11.6 0.0 copy-start.5
  11.6 0.7 %copy-done.5 = f32[4,6]{1,0:T(4,128)S(1)} copy-done((f32[4,6]{1,0:T(4,128)S(1)}, f32[4,6]{1,0:T(4,128)}, u32[]{:S(2)}) %copy-start.5) | copy-done | bytes 120
  12.2 8.3 %pre.1 = (bf16[15,10,96,128]{3,2,1,0:T(8,128)(2,1)S(1)}, bf16[15,10,96,128]{3,2,1,0:T(8,128)(2,1)S(1)}, f32[10,4,128,256]{3,2,1,0:T(8,128)S(1)}, f32[10,4,128,25...) custom-call(s32[1,2]{1,0:T(1,128)S(1)} %copy-done.2, ...), custom_call_target="tpu_custom_call" | custom-call | tf_op jit(solution)/shard_map/pre/pallas_call | solution.py:300
  20.5 0.0 collective-permute-done.4.from_b
  20.5 0.0 copy-start.6
  20.6 0.6 %copy-done.6 = s32[1,2]{1,0:T(1,128)S(1)} copy-done((s32[1,2]{1,0:T(1,128)S(1)}, s32[1,2]{1,0:T(1,128)}, u32[]{:S(2)}) %copy-start.6) | copy-done | bytes 32
  21.2 6.3 %post1.1 = (f32[8,6,8,128]{3,2,1,0:T(8,128)S(1)}, f32[5,6,8,128]{3,2,1,0:T(8,128)S(1)}, f32[5,6,8,128]{3,2,1,0:T(8,128)S(1)}, bf16[15,10,96,128]{3,2,1,0:T(8,128...) custom-call(s32[1,2]{1,0:T(1,128)S(1)} %copy-done.2, ...), custom_call_target="tpu_custom_call", output_to_operand_aliasing={{3}: (3, {}), {4}: (4, {}), {5}: (5, {})} | custom-call | tf_op jit(solution)/shard_map/post1/pallas_call | solution.py:310
  27.5 0.1 collective-permute-start.5
  27.5 3.2 %collective-permute-start.6 = (f32[5,6,8,128]{3,2,1,0:T(8,128)S(1)}, f32[5,6,8,128]{3,2,1,0:T(8,128)S(1)}, u32[]{:S(2)}, u32[]{:S(2)}) collective-permute-start(f32[5,6,8,128]{3,2,1,0:T(8,128)S(1)} %get-tuple-element.44), channel_id=1, source_target_pairs={{1,2},{2,1},{3,4},{4,3},{5,6},{6,5},{7,8},{8,7},{9,10},{10,9},{11,... | collective-permute-start | bytes 368648 | tf_op jit(solution)/shard_map/ppermute | solution.py:320
  30.8 0.0 collective-permute-done.from_b
  30.8 5.1 %post0.1 = (f32[8,6,8,128]{3,2,1,0:T(8,128)S(1)}, f32[5,6,8,128]{3,2,1,0:T(8,128)S(1)}, f32[5,6,8,128]{3,2,1,0:T(8,128)S(1)}, bf16[15,10,96,128]{3,2,1,0:T(8,128...) custom-call(s32[1,2]{1,0:T(1,128)S(1)} %copy-done.2, ...), custom_call_target="tpu_custom_call", output_to_operand_aliasing={{3}: (3, {}), {4}: (4, {}), {5}: (5, {})} | custom-call | tf_op jit(solution)/shard_map/post0/pallas_call | solution.py:310
  35.9 2.1 %collective-permute-start.2 = (f32[5,6,8,128]{3,2,1,0:T(8,128)S(1)}, f32[5,6,8,128]{3,2,1,0:T(8,128)S(1)}, u32[]{:S(2)}, u32[]{:S(2)}) collective-permute-start(f32[5,6,8,128]{3,2,1,0:T(8,128)S(1)} %get-tuple-element.36), channel_id=1, source_target_pairs={{0,1},{1,0},{2,3},{3,2},{4,5},{5,4},{6,7},{7,6},{8,9},{9,8},{10,11... | collective-permute-start | bytes 368648 | tf_op jit(solution)/shard_map/ppermute | solution.py:320
  38.0 2.7 %collective-permute-start.3 = (f32[5,6,8,128]{3,2,1,0:T(8,128)S(1)}, f32[5,6,8,128]{3,2,1,0:T(8,128)S(1)}, u32[]{:S(2)}, u32[]{:S(2)}) collective-permute-start(f32[5,6,8,128]{3,2,1,0:T(8,128)S(1)} %get-tuple-element.37), channel_id=1, source_target_pairs={{1,2},{2,1},{3,4},{4,3},{5,6},{6,5},{7,8},{8,7},{9,10},{10,9},{11,... | collective-permute-start | bytes 368648 | tf_op jit(solution)/shard_map/ppermute | solution.py:320
  41.4 0.0 collective-permute-done.5.refs_4_
  41.4 0.0 collective-permute-done.6.refs_5_
  41.4 0.0 collective-permute-done.2.refs_1_
  41.4 4.1 %collective-permute-done.3.refs_2_ = f32[5,6,8,128]{3,2,1,0:T(8,128)S(1)} collective-permute-done((f32[5,6,8,128]{3,2,1,0:T(8,128)S(1)}, f32[5,6,8,128]{3,2,1,0:T(8,128)S(1)}, u32[]{:S(2)}, u32[]{:S(2)}) %collective-permute-start.3) | collective-permute-done | bytes 122912 | tf_op jit(solution)/shard_map/ppermute | solution.py:320
  45.5 1.1 %merge.1 = f32[6,8,16,128]{3,2,1,0:T(8,128)} custom-call(s32[1]{0:T(128)S(6)} %copy.23.acq, f32[8,6,8,128]{3,2,1,0:T(8,128)S(1)} %get-tuple-element.35.refs_0_, f32[5,6,8,128]{3,2,1,0:T(8,128)S(1)} %collective-permute-done.2.refs_1_, f32[5,6,8,128]{3,2,1,0:T(8,128)S(1)} %collective-permute-done.3.refs_2_, f32[8,6,8,128]{3,2,1,0:T(8,128)S(1)} %get-tuple-element.42.refs_3_, ...), custom_call_target="tpu_custom_call" | custom-call | tf_op jit(solution)/shard_map/merge/pallas_call | solution.py:321
Async XLA Ops:
  0.0 1.1 %copy-start = (bf16[32,6,16,128]{3,2,1,0:T(8,128)(2,1)S(1)}, bf16[32,6,16,128]{3,2,1,0:T(8,128)(2,1)}, u32[]{:S(2)}) copy-start(bf16[32,6,16,128]{3,2,1,0:T(8,128)(2,1)} %feat.1) | copy-start | bytes 2359300
  1.6 7.0 %collective-permute-start.1 = (bf16[2,4,8,32,128]{4,3,2,1,0:T(8,128)(2,1)S(1)}, bf16[2,4,8,32,128]{4,3,2,1,0:T(8,128)(2,1)S(1)}, u32[]{:S(2)}, u32[]{:S(2)}) collective-permute-start(bf16[2,4,8,32,128]{4,3,2,1,0:T(8,128)(2,1)S(1)} %get-tuple-element.27), channel_id=1, source_target_pairs={{0,1},{1,0},{2,3},{3,2},{4,5},{5,4},{6,7},{7,6},{8,9},{9,8},{10,11... | collective-permute-start | bytes 1572872 | tf_op jit(solution)/shard_map/ppermute | solution.py:291
  2.3 18.2 %collective-permute-start.4 = (bf16[4,8,32,128]{3,2,1,0:T(8,128)(2,1)S(1)}, bf16[4,8,32,128]{3,2,1,0:T(8,128)(2,1)S(1)}, u32[]{:S(2)}, u32[]{:S(2)}) collective-permute-start(bf16[4,8,32,128]{3,2,1,0:T(8,128)(2,1)S(1)} %get-tuple-element.38), channel_id=1, source_target_pairs={{1,2},{2,1},{3,4},{4,3},{5,6},{6,5},{7,8},{8,7},{9,10},{10,9},{11,... | collective-permute-start | bytes 786440 | tf_op jit(solution)/shard_map/ppermute | solution.py:292
  5.4 25.4 %collective-permute-start = (bf16[4,8,32,128]{3,2,1,0:T(8,128)(2,1)S(1)}, bf16[4,8,32,128]{3,2,1,0:T(8,128)(2,1)S(1)}, u32[]{:S(2)}, u32[]{:S(2)}) collective-permute-start(bf16[4,8,32,128]{3,2,1,0:T(8,128)(2,1)S(1)} %get-tuple-element.25), channel_id=1, source_target_pairs={{1,2},{2,1},{3,4},{4,3},{5,6},{6,5},{7,8},{8,7},{9,10},{10,9},{11,... | collective-permute-start | bytes 786440 | tf_op jit(solution)/shard_map/ppermute | solution.py:292
  8.6 0.9 %copy-start.1 = (bf16[3,128,288]{1,2,0:T(8,128)(2,1)S(1)}, bf16[3,128,288]{1,2,0:T(8,128)(2,1)}, u32[]{:S(2)}) copy-start(bf16[3,128,288]{1,2,0:T(8,128)(2,1)} %param.10) | copy-start | bytes 663556
  9.5 0.7 %copy-start.2 = (s32[1,2]{1,0:T(1,128)S(1)}, s32[1,2]{1,0:T(1,128)}, u32[]{:S(2)}) copy-start(s32[1,2]{1,0:T(1,128)} %offs.5) | copy-start | bytes 28
  10.2 0.7 %copy-start.3 = (f32[4,32]{1,0:T(4,128)S(1)}, f32[4,32]{1,0:T(4,128)}, u32[]{:S(2)}) copy-start(f32[4,32]{1,0:T(4,128)} %gain.1) | copy-start | bytes 1540
  10.9 0.7 %copy-start.4 = (f32[4,32]{1,0:T(4,128)S(1)}, f32[4,32]{1,0:T(4,128)}, u32[]{:S(2)}) copy-start(f32[4,32]{1,0:T(4,128)} %nbias.1) | copy-start | bytes 1540
  11.6 0.7 %copy-start.5 = (f32[4,6]{1,0:T(4,128)S(1)}, f32[4,6]{1,0:T(4,128)}, u32[]{:S(2)}) copy-start(f32[4,6]{1,0:T(4,128)} %head_b.1) | copy-start | bytes 292
  20.5 0.7 %copy-start.6 = (s32[1,2]{1,0:T(1,128)S(1)}, s32[1,2]{1,0:T(1,128)}, u32[]{:S(2)}) copy-start(s32[1,2]{1,0:T(1,128)} %mask.3) | copy-start | bytes 28
  27.5 13.9 %collective-permute-start.5 = (f32[5,6,8,128]{3,2,1,0:T(8,128)S(1)}, f32[5,6,8,128]{3,2,1,0:T(8,128)S(1)}, u32[]{:S(2)}, u32[]{:S(2)}) collective-permute-start(f32[5,6,8,128]{3,2,1,0:T(8,128)S(1)} %get-tuple-element.43), channel_id=1, source_target_pairs={{0,1},{1,0},{2,3},{3,2},{4,5},{5,4},{6,7},{7,6},{8,9},{9,8},{10,11... | collective-permute-start | bytes 368648 | tf_op jit(solution)/shard_map/ppermute | solution.py:320
  27.5 13.8 %collective-permute-start.6 = (f32[5,6,8,128]{3,2,1,0:T(8,128)S(1)}, f32[5,6,8,128]{3,2,1,0:T(8,128)S(1)}, u32[]{:S(2)}, u32[]{:S(2)}) collective-permute-start(f32[5,6,8,128]{3,2,1,0:T(8,128)S(1)} %get-tuple-element.44), channel_id=1, source_target_pairs={{1,2},{2,1},{3,4},{4,3},{5,6},{6,5},{7,8},{8,7},{9,10},{10,9},{11,... | collective-permute-start | bytes 368648 | tf_op jit(solution)/shard_map/ppermute | solution.py:320
  35.9 5.5 %collective-permute-start.2 = (f32[5,6,8,128]{3,2,1,0:T(8,128)S(1)}, f32[5,6,8,128]{3,2,1,0:T(8,128)S(1)}, u32[]{:S(2)}, u32[]{:S(2)}) collective-permute-start(f32[5,6,8,128]{3,2,1,0:T(8,128)S(1)} %get-tuple-element.36), channel_id=1, source_target_pairs={{0,1},{1,0},{2,3},{3,2},{4,5},{5,4},{6,7},{7,6},{8,9},{9,8},{10,11... | collective-permute-start | bytes 368648 | tf_op jit(solution)/shard_map/ppermute | solution.py:320
  38.0 7.5 %collective-permute-start.3 = (f32[5,6,8,128]{3,2,1,0:T(8,128)S(1)}, f32[5,6,8,128]{3,2,1,0:T(8,128)S(1)}, u32[]{:S(2)}, u32[]{:S(2)}) collective-permute-start(f32[5,6,8,128]{3,2,1,0:T(8,128)S(1)} %get-tuple-element.37), channel_id=1, source_target_pairs={{1,2},{2,1},{3,4},{4,3},{5,6},{6,5},{7,8},{8,7},{9,10},{10,9},{11,... | collective-permute-start | bytes 368648 | tf_op jit(solution)/shard_map/ppermute | solution.py:320

commit v3 on v2

--- a/solution.py
+++ b/solution.py
@@ -27,18 +27,29 @@
     return pl.BlockSpec(memory_space=pltpu.SMEM)
 
 
-def prep_kernel(feat, own, to_a, *to_b):
+def prep_kernel(*refs):
+    small = (len(refs) - 3 - 2 - PATCHES) // 2
+    feat, small_in, rest = refs[0], refs[1 : 1 + small], refs[1 + small :]
+    (own, to_a), to_b, small_out = rest[:2], rest[2 : 2 + PATCHES], rest[2 + PATCHES : 2 + PATCHES + small]
+    held, sems = rest[2 + PATCHES + small :]
     channels, planes, rows, cols = feat.shape
+    copies = [pltpu.make_async_copy(feat.at[:, x], held.at[x], sems.at[x]) for x in range(planes)]
+    copies += [pltpu.make_async_copy(a, b, sems.at[planes + i]) for i, (a, b) in enumerate(zip(small_in, small_out))]
+    for copy in copies:
+        copy.start()
     even = lax.rem(lax.axis_index("slab"), 2) == 0
     a_first = jnp.where(even, planes - RIM, 0)
     b_first = jnp.where(even, 0, planes - RIM)
     for x in range(planes):
-        turned = jnp.swapaxes(feat[:, x].astype(F32), 0, 1).astype(BF16)
+        copies[x].wait()
+        turned = jnp.swapaxes(held[x].astype(F32), 0, 1).astype(BF16)
         for p in range(PATCHES):
             own[p, x] = turned[p * PATCH_ROWS : (p + 1) * PATCH_ROWS]
     for p in range(PATCHES):
         to_a[p] = own[p, pl.ds(a_first, RIM)]
         to_b[p][...] = own[p, pl.ds(b_first, RIM)]
+    for copy in copies[planes:]:
+        copy.wait()
 
 
 def column_of(table, folds, width):
@@ -51,21 +62,24 @@
 
 
 def head_tables(head_w, head_b, folds, classes, channels):
-    rows = classes * 2 * folds
+    rows, outs = classes * 2 * folds, folds * channels
+    lane = lax.broadcasted_iota(jnp.int32, (channels, outs), 1)
+    chan = lax.broadcasted_iota(jnp.int32, (channels, outs), 0)
+    spread = (lane % channels == chan).astype(F32).astype(BF16)
+    tall = []
+    for k in range(classes):
+        tall += [head_w[k].astype(F32)] * 2
+    tall = jnp.concatenate(tall, 0).astype(BF16)
+    table = jnp.dot(tall, spread, preferred_element_type=F32)
+    row = lax.broadcasted_iota(jnp.int32, (rows, outs), 0)
+    col = lax.broadcasted_iota(jnp.int32, (rows, outs), 1)
+    table = jnp.where(row % folds == col // channels, table, 0.0).astype(BF16)
     row = lax.broadcasted_iota(jnp.int32, (rows, classes), 0)
     cls = lax.broadcasted_iota(jnp.int32, (rows, classes), 1)
-    brow = lax.broadcasted_iota(jnp.int32, (rows, classes), 0)
-    lane = lax.broadcasted_iota(jnp.int32, (channels, folds * channels), 1)
-    chan = lax.broadcasted_iota(jnp.int32, (channels, folds * channels), 0)
-    table = jnp.zeros((rows, folds * channels), F32)
     bias = jnp.zeros((rows, 1), F32)
     for f in range(folds):
         pick = (row // (2 * folds) == cls) & (row % folds == f)
-        part = jnp.dot(pick.astype(F32).astype(BF16), head_w[f], preferred_element_type=F32).astype(BF16)
-        place = (lane == chan + f * channels).astype(F32).astype(BF16)
-        table = table + jnp.dot(part, place, preferred_element_type=F32)
         bias = bias + jnp.sum(jnp.where(pick, jnp.broadcast_to(head_b[f : f + 1, :], (rows, classes)), 0.0), axis=1, keepdims=True)
-    table = table.astype(BF16)
     return jnp.concatenate([table, table], 1), bias
 
 
@@ -133,14 +147,15 @@
 
 def pre_kernel(offs, own, from_a, wt, gain, nbias, head_w, head_b, taps0, taps1, conv0, conv1, stats0, stats1, w_all, head, hbias, scales):
     planes = own.shape[1]
-    folds, classes, channels = head_w.shape
+    classes, folds, channels = head_w.shape
     outs = folds * channels
     cols = own.shape[-1]
     span = planes + 2 * RIM
     even = lax.rem(lax.axis_index("slab"), 2) == 0
     a_base = jnp.where(even, RIM + planes, 0)
-    wide_w = jnp.concatenate([wt[a].astype(F32) for a in range(3)], 0)
-    w_all[...] = jnp.transpose(wide_w).astype(BF16)
+    eye = (lax.broadcasted_iota(jnp.int32, (outs, outs), 0) == lax.broadcasted_iota(jnp.int32, (outs, outs), 1)).astype(F32).astype(BF16)
+    wide_w = jnp.concatenate([wt[a] for a in range(3)], 0)
+    w_all[...] = lax.dot_general(eye, wide_w, (((1,), (1,)), ((), ())), preferred_element_type=F32).astype(BF16)
     table, bias = head_tables(head_w, head_b, folds, classes, channels)
     head[...] = table
     hbias[...] = jnp.broadcast_to(bias, hbias.shape)
@@ -164,17 +179,17 @@
             return 0
 
         lax.fori_loop(0, span, pad_rows, 0)
-        lax.fori_loop(0, planes, fill_own, 0)
-        lax.fori_loop(0, RIM, fill_a, 0)
+        lax.fori_loop(0, planes, fill_own, 0, unroll=2)
+        lax.fori_loop(0, RIM, fill_a, 0, unroll=2)
         stats[...] = jnp.zeros_like(stats)
         _, first, begin, end = patch_plan(offs, p, planes)
         conv_planes(first, begin, end, True, taps, w_all, conv, stats)
 
 
-def post_kernel(p, offs, mask, from_b, taps_in, conv_in, stats_in, w_all, head, hbias, scales, kept, to_a, to_b, taps, conv, stats, placed):
-    planes = kept.shape[0] - 2
-    span = taps.shape[0] - 1
-    classes = kept.shape[1]
+def post_kernel(p, offs, mask, from_b, taps_in, conv_in, stats_in, w_all, head, hbias, scales, *refs):
+    kept, to_a, to_b, taps, conv, stats, placed = refs[-7:]
+    planes = kept.shape[1] - 2
+    classes = kept.shape[2]
     outs, cols = stats.shape[1:]
     folds = head.shape[0] // classes // 2
     even, first, begin, end = patch_plan(offs, p, planes)
@@ -184,7 +199,7 @@
         fill_taps(taps, i + b_base, from_b.at[i])
         return 0
 
-    lax.fori_loop(0, RIM, fill_b, 0)
+    lax.fori_loop(0, RIM, fill_b, 0, unroll=2)
     conv_planes(first, jnp.where(even, 0, end), jnp.where(even, begin, PATCH_X), False, taps, w_all, conv, stats)
     count = float(PATCH_X * PATCH_ROWS)
     total = stats[1] * (1.0 / count)
@@ -232,18 +247,17 @@
             placed[first + x, k] = full * window
         return 0
 
-    lax.fori_loop(0, PATCH_X, finish_plane, 0)
+    lax.fori_loop(0, PATCH_X, finish_plane, 0, unroll=2)
     reach = RIM + 1
-    kept[...] = placed[pl.ds(RIM - 1, planes + 2)]
-    to_a[...] = placed[pl.ds(jnp.where(even, planes + RIM - 1, 0), reach)]
-    to_b[...] = placed[pl.ds(jnp.where(even, 0, planes + RIM - 1), reach)]
-
-
-def merge_kernel(slabs, acq, *refs):
-    ins, out, merged = refs[:-2], refs[-2], refs[-1]
-    wide = ins[0].shape[0]
+    kept[p] = placed[pl.ds(RIM - 1, planes + 2)]
+    to_a[p] = placed[pl.ds(jnp.where(even, planes + RIM - 1, 0), reach)]
+    to_b[p] = placed[pl.ds(jnp.where(even, 0, planes + RIM - 1), reach)]
+
+
+def merge_kernel(slabs, acq, kept, from_a, from_b, out, merged):
+    wide = kept.shape[1]
     planes = wide - 2
-    classes, rows, cols = ins[0].shape[1:]
+    classes, rows, cols = kept.shape[2:]
     slab = lax.axis_index("slab")
     even = lax.rem(slab, 2) == 0
     a_base = jnp.where(even, wide - RIM - 1, 0)
@@ -253,10 +267,9 @@
     anchor = jnp.full(shape, slab * planes, jnp.int32).astype(F32)
     step = planes / jnp.maximum(count - 1.0, 1.0)
     for p in range(PATCHES):
-        kept, from_a, from_b = ins[3 * p : 3 * p + 3]
-        merged[...] = kept[...]
-        merged[pl.ds(a_base, RIM + 1)] += from_a[...]
-        merged[pl.ds(b_base, RIM + 1)] += from_b[...]
+        merged[...] = kept[p]
+        merged[pl.ds(a_base, RIM + 1)] += from_a[p]
+        merged[pl.ds(b_base, RIM + 1)] += from_b[p]
         table = []
         for j in range(wide):
             parts = [merged[j, k] for k in range(classes)]
@@ -280,14 +293,19 @@
     shaped = jax.ShapeDtypeStruct
     cell = (PATCH_ROWS, channels, cols)
     params = pltpu.CompilerParams(vmem_limit_bytes=24 * MIB)
-    own, to_a, *to_b = pl.pallas_call(
+    small = [jnp.swapaxes(conv_weight, 1, 2), norm_gain, norm_bias, jnp.swapaxes(head_weight, 0, 1), head_bias, patch_offsets, fg_mask]
+    own, to_a, *rest = pl.pallas_call(
         prep_kernel,
-        out_shape=[shaped((PATCHES, planes) + cell, BF16), shaped((PATCHES, RIM) + cell, BF16)] + [shaped((RIM,) + cell, BF16)] * PATCHES,
-        in_specs=[vmem()],
-        out_specs=[vmem()] * (2 + PATCHES),
+        out_shape=[shaped((PATCHES, planes) + cell, BF16), shaped((PATCHES, RIM) + cell, BF16)]
+        + [shaped((RIM,) + cell, BF16)] * PATCHES
+        + [shaped(v.shape, v.dtype) for v in small],
+        in_specs=[pl.BlockSpec(memory_space=pltpu.HBM)] * (1 + len(small)),
+        out_specs=[vmem()] * (2 + PATCHES + len(small)),
+        scratch_shapes=[pltpu.VMEM((planes, channels, row_total, cols), BF16), pltpu.SemaphoreType.DMA((planes + len(small),))],
         compiler_params=params,
         name="prep",
-    )(features)
+    )(*[pltpu.with_memory_space_constraint(v, pltpu.HBM) for v in (features, *small)])
+    to_b, (conv_weight, norm_gain, norm_bias, head_weight, head_bias, patch_offsets, fg_mask) = rest[:PATCHES], rest[PATCHES:]
     from_a = lax.ppermute(to_a, "slab", pairs_a)
     from_b = [lax.ppermute(v, "slab", pairs_b) for v in to_b]
     wide = planes + 2
@@ -304,29 +322,30 @@
         out_specs=[vmem()] * 10,
         compiler_params=params,
         name="pre",
-    )(patch_offsets, own, from_a, jnp.swapaxes(conv_weight, 1, 2), norm_gain, norm_bias, head_weight, head_bias)
-    merged_in = []
+    )(patch_offsets, own, from_a, conv_weight, norm_gain, norm_bias, head_weight, head_bias)
+    sends = []
+    send_shapes = [shaped((PATCHES, n) + tile, F32) for n in (wide, RIM + 1, RIM + 1)]
     for p in range(PATCHES):
-        kept, send_a, send_b, *_ = pl.pallas_call(
+        sends = pl.pallas_call(
             functools.partial(post_kernel, p),
-            out_shape=[shaped((n,) + tile, F32) for n in (wide, RIM + 1, RIM + 1)] + [taps_shape, conv_shape, stats_shape],
-            in_specs=[smem()] * 2 + [vmem()] * 8,
+            out_shape=send_shapes + [taps_shape, conv_shape, stats_shape],
+            in_specs=[smem()] * 2 + [vmem()] * (8 + len(sends)),
             out_specs=[vmem()] * 6,
-            input_output_aliases={3: 3, 4: 4, 5: 5},
+            input_output_aliases={3: 3, 4: 4, 5: 5} | {10 + i: i for i in range(len(sends))},
             scratch_shapes=[pltpu.VMEM((span,) + tile, F32)],
             compiler_params=params,
             name=f"post{p}",
-        )(patch_offsets, fg_mask, from_b[p], made[p], made[2 + p], made[4 + p], *made[6:])
-        merged_in += [kept, lax.ppermute(send_a, "slab", pairs_a), lax.ppermute(send_b, "slab", pairs_b)]
+        )(patch_offsets, fg_mask, from_b[p], made[p], made[2 + p], made[4 + p], *made[6:], *sends)[:3]
+    kept, send_a, send_b = sends
     return pl.pallas_call(
         functools.partial(merge_kernel, slabs),
         out_shape=shaped((classes, MOST_ACQ, row_total, cols), F32),
-        in_specs=[smem()] + [vmem()] * (3 * PATCHES),
+        in_specs=[smem()] + [vmem()] * 3,
         out_specs=vmem(),
         scratch_shapes=[pltpu.VMEM((wide,) + tile, F32)],
         compiler_params=params,
         name="merge",
-    )(acq_counts, *merged_in)
+    )(acq_counts, kept, lax.ppermute(send_a, "slab", pairs_a), lax.ppermute(send_b, "slab", pairs_b))
 
 
 def solution(mesh):

time: 47.2 us -> 37.6 us (0.80)
  local copies, waits for them, and re-layouts: 6.11 us -> 0 us
  starting transfers between devices: 14.4 us -> 10.6 us
  waiting for transfers between devices: 4.11 us -> 5.98 us
  Pallas kernels: 21.2 us -> 19.7 us
    unnamed x15 -> x0, local copies, waits for them, and re-layouts: 6.11 us -> none
    ppermute x2 -> x1, starting transfers between devices: 5.93 us -> 3.5 us  [local(): lax.ppermute(send_b, 'slab', pairs_b)]
    pallas_call x2, Pallas kernels: 11.4 us -> 9.27 us  [local(): pl.pallas_call(functools.partial(post_kernel, p), out_shape=send_shapes +...]
    ppermute x2 -> x1, waiting for transfers between devices: 4.1 us -> 5.97 us  [local(): lax.ppermute(send_b, 'slab', pairs_b)]
    ppermute x2 -> x1, starting transfers between devices: 2.16 us -> 0.82 us  [local(): lax.ppermute(send_a, 'slab', pairs_a)]
    pallas_call x1, Pallas kernels: 0.45 us -> 1.47 us  [local(): pl.pallas_call(prep_kernel, out_shape=[shaped((PATCHES, planes) + cell, B...]
  transfers between devices with their start and end apart: 7 -> 5, of which waited for: 1 -> 1; matrix products, arithmetic and copies ran while one was open for 1% -> 0% of each run, Pallas kernels for 42% -> 34%
where the time goes in v3:
time: 37.6 us; the launch traced here: 37 us
  Pallas kernels  19.7 us (52%)
  starting transfers between devices  10.6 us (28%)
  waiting for transfers between devices  5.98 us (16%)
  between operations  0.74 us (2%)
    pallas_call x2, Pallas kernels, local(): pl.pallas_call(functools.partial(post_kernel, p), out_shape=send_shapes +...  9.27 us
    pallas_call x1, Pallas kernels, local(): pl.pallas_call(pre_kernel, out_shape=[taps_shape] * 2 + [conv_shape] * 2...  7.85 us
    ppermute x1, waiting for transfers between devices, local(): lax.ppermute(send_b, 'slab', pairs_b)  5.97 us
    ppermute x2, starting transfers between devices, local(): from_b = [lax.ppermute(v, 'slab', pairs_b) for v in to_b]  5.55 us
    ppermute x1, starting transfers between devices, local(): lax.ppermute(send_b, 'slab', pairs_b)  3.5 us
    pallas_call x1, Pallas kernels, local(): pl.pallas_call(prep_kernel, out_shape=[shaped((PATCHES, planes) + cell, B...  1.47 us
    pallas_call x1, Pallas kernels, local(): pl.pallas_call(functools.partial(merge_kernel, slabs), out_shape=shaped((...  1.1 us
    ppermute x1, starting transfers between devices, local(): lax.ppermute(send_a, 'slab', pairs_a)  0.82 us
  transfers between devices with their start and end apart: 5, of which 1 were waited for; matrix products, arithmetic and copies ran while one was open for 0% of the time, Pallas kernels for 34%

profile of v3, /device:TPU:11, one launch (start us, length us, event | category | flops | bytes accessed | tf_op | source)
XLA Modules:
  0.0 37.0 jit_solution(5887184726039994252)
XLA Ops:
  0.0 1.5 %prep.1 = (bf16[2,6,8,32,128]{4,3,2,1,0:T(8,128)(2,1)S(1)}, bf16[2,4,8,32,128]{4,3,2,1,0:T(8,128)(2,1)S(1)}, bf16[4,8,32,128]{3,2,1,0:T(8,128)(2,1)S(1)}, bf16[4...) custom-call(bf16[32,6,16,128]{3,2,1,0:T(8,128)(2,1)} %refs_0_.1, ...), custom_call_target="tpu_custom_call" | custom-call | tf_op jit(solution)/shard_map/prep/pallas_call | solution.py:297
  1.5 0.7 %collective-permute-start.1 = (bf16[2,4,8,32,128]{4,3,2,1,0:T(8,128)(2,1)S(1)}, bf16[2,4,8,32,128]{4,3,2,1,0:T(8,128)(2,1)S(1)}, u32[]{:S(2)}, u32[]{:S(2)}) collective-permute-start(bf16[2,4,8,32,128]{4,3,2,1,0:T(8,128)(2,1)S(1)} %get-tuple-element.36), channel_id=1, source_target_pairs={{0,1},{1,0},{2,3},{3,2},{4,5},{5,4},{6,7},{7,6},{8,9},{9,8},{10,11... | collective-permute-start | bytes 1572872 | tf_op jit(solution)/shard_map/ppermute | solution.py:309
  2.2 3.0 %collective-permute-start.2 = (bf16[4,8,32,128]{3,2,1,0:T(8,128)(2,1)S(1)}, bf16[4,8,32,128]{3,2,1,0:T(8,128)(2,1)S(1)}, u32[]{:S(2)}, u32[]{:S(2)}) collective-permute-start(bf16[4,8,32,128]{3,2,1,0:T(8,128)(2,1)S(1)} %get-tuple-element.49), channel_id=1, source_target_pairs={{1,2},{2,1},{3,4},{4,3},{5,6},{6,5},{7,8},{8,7},{9,10},{10,9},{11,... | collective-permute-start | bytes 786440 | tf_op jit(solution)/shard_map/ppermute | solution.py:310
  5.3 2.5 %collective-permute-start = (bf16[4,8,32,128]{3,2,1,0:T(8,128)(2,1)S(1)}, bf16[4,8,32,128]{3,2,1,0:T(8,128)(2,1)S(1)}, u32[]{:S(2)}, u32[]{:S(2)}) collective-permute-start(bf16[4,8,32,128]{3,2,1,0:T(8,128)(2,1)S(1)} %get-tuple-element.34), channel_id=1, source_target_pairs={{1,2},{2,1},{3,4},{4,3},{5,6},{6,5},{7,8},{8,7},{9,10},{10,9},{11,... | collective-permute-start | bytes 786440 | tf_op jit(solution)/shard_map/ppermute | solution.py:310
  7.8 0.0 collective-permute-done.1.from_a
  7.8 7.9 %pre.1 = (bf16[15,10,96,128]{3,2,1,0:T(8,128)(2,1)S(1)}, bf16[15,10,96,128]{3,2,1,0:T(8,128)(2,1)S(1)}, f32[10,4,128,256]{3,2,1,0:T(8,128)S(1)}, f32[10,4,128,25...) custom-call(s32[1,2]{1,0:T(1,128)S(1)} %get-tuple-element.32.offs, ...), custom_call_target="tpu_custom_call" | custom-call | tf_op jit(solution)/shard_map/pre/pallas_call | solution.py:318
  15.7 0.0 collective-permute-done.2.from_b
  15.7 4.7 %post0.1 = (f32[2,8,6,8,128]{4,3,2,1,0:T(8,128)S(1)}, f32[2,5,6,8,128]{4,3,2,1,0:T(8,128)S(1)}, f32[2,5,6,8,128]{4,3,2,1,0:T(8,128)S(1)}, bf16[15,10,96,128]{3,2...) custom-call(s32[1,2]{1,0:T(1,128)S(1)} %get-tuple-element.32.offs, ...), custom_call_target="tpu_custom_call", output_to_operand_aliasing={{3}: (3, {}), {4}: (4, {}), {5}: (5, {})} | custom-call | tf_op jit(solution)/shard_map/post0/pallas_call | solution.py:329
  20.3 0.0 collective-permute-done.from_b
  20.3 4.6 %post1.1 = (f32[2,8,6,8,128]{4,3,2,1,0:T(8,128)S(1)}, f32[2,5,6,8,128]{4,3,2,1,0:T(8,128)S(1)}, f32[2,5,6,8,128]{4,3,2,1,0:T(8,128)S(1)}, bf16[15,10,96,128]{3,2...) custom-call(s32[1,2]{1,0:T(1,128)S(1)} %get-tuple-element.32.offs, ...), custom_call_target="tpu_custom_call", output_to_operand_aliasing={{3}: (3, {}), {4}: (4, {}), {5}: (5, {}), {0}: (10, {}), {1... | custom-call | tf_op jit(solution)/shard_map/post1/pallas_call | solution.py:329
  25.0 0.8 %collective-permute-start.3 = (f32[2,5,6,8,128]{4,3,2,1,0:T(8,128)S(1)}, f32[2,5,6,8,128]{4,3,2,1,0:T(8,128)S(1)}, u32[]{:S(2)}, u32[]{:S(2)}) collective-permute-start(f32[2,5,6,8,128]{4,3,2,1,0:T(8,128)S(1)} %get-tuple-element.57), channel_id=1, source_target_pairs={{0,1},{1,0},{2,3},{3,2},{4,5},{5,4},{6,7},{7,6},{8,9},{9,8},{10,11... | collective-permute-start | bytes 737288 | tf_op jit(solution)/shard_map/ppermute | solution.py:348
  25.8 3.5 %collective-permute-start.4 = (f32[2,5,6,8,128]{4,3,2,1,0:T(8,128)S(1)}, f32[2,5,6,8,128]{4,3,2,1,0:T(8,128)S(1)}, u32[]{:S(2)}, u32[]{:S(2)}) collective-permute-start(f32[2,5,6,8,128]{4,3,2,1,0:T(8,128)S(1)} %get-tuple-element.58), channel_id=1, source_target_pairs={{1,2},{2,1},{3,4},{4,3},{5,6},{6,5},{7,8},{8,7},{9,10},{10,9},{11,... | collective-permute-start | bytes 737288 | tf_op jit(solution)/shard_map/ppermute | solution.py:348
  30.0 0.0 collective-permute-done.3.from_a
  30.0 6.0 %collective-permute-done.4.from_b = f32[2,5,6,8,128]{4,3,2,1,0:T(8,128)S(1)} collective-permute-done((f32[2,5,6,8,128]{4,3,2,1,0:T(8,128)S(1)}, f32[2,5,6,8,128]{4,3,2,1,0:T(8,128)S(1)}, u32[]{:S(2)}, u32[]{:S(2)}) %collective-permute-start.4) | collective-permute-done | bytes 245792 | tf_op jit(solution)/shard_map/ppermute | solution.py:348
  35.9 1.1 %merge.1 = f32[6,8,16,128]{3,2,1,0:T(8,128)} custom-call(s32[1]{0:T(128)S(6)} %copy.28.acq, f32[2,8,6,8,128]{4,3,2,1,0:T(8,128)S(1)} %get-tuple-element.56.kept, f32[2,5,6,8,128]{4,3,2,1,0:T(8,128)S(1)} %collective-permute-done.3.from_a, f32[2,5,6,8,128]{4,3,2,1,0:T(8,128)S(1)} %collective-permute-done.4.from_b), custom_call_target="tpu_custom_call" | custom-call | tf_op jit(solution)/shard_map/merge/pallas_call | solution.py:340
Async XLA Ops:
  1.5 6.3 %collective-permute-start.1 = (bf16[2,4,8,32,128]{4,3,2,1,0:T(8,128)(2,1)S(1)}, bf16[2,4,8,32,128]{4,3,2,1,0:T(8,128)(2,1)S(1)}, u32[]{:S(2)}, u32[]{:S(2)}) collective-permute-start(bf16[2,4,8,32,128]{4,3,2,1,0:T(8,128)(2,1)S(1)} %get-tuple-element.36), channel_id=1, source_target_pairs={{0,1},{1,0},{2,3},{3,2},{4,5},{5,4},{6,7},{7,6},{8,9},{9,8},{10,11... | collective-permute-start | bytes 1572872 | tf_op jit(solution)/shard_map/ppermute | solution.py:309
  2.2 13.4 %collective-permute-start.2 = (bf16[4,8,32,128]{3,2,1,0:T(8,128)(2,1)S(1)}, bf16[4,8,32,128]{3,2,1,0:T(8,128)(2,1)S(1)}, u32[]{:S(2)}, u32[]{:S(2)}) collective-permute-start(bf16[4,8,32,128]{3,2,1,0:T(8,128)(2,1)S(1)} %get-tuple-element.49), channel_id=1, source_target_pairs={{1,2},{2,1},{3,4},{4,3},{5,6},{6,5},{7,8},{8,7},{9,10},{10,9},{11,... | collective-permute-start | bytes 786440 | tf_op jit(solution)/shard_map/ppermute | solution.py:310
  5.3 15.1 %collective-permute-start = (bf16[4,8,32,128]{3,2,1,0:T(8,128)(2,1)S(1)}, bf16[4,8,32,128]{3,2,1,0:T(8,128)(2,1)S(1)}, u32[]{:S(2)}, u32[]{:S(2)}) collective-permute-start(bf16[4,8,32,128]{3,2,1,0:T(8,128)(2,1)S(1)} %get-tuple-element.34), channel_id=1, source_target_pairs={{1,2},{2,1},{3,4},{4,3},{5,6},{6,5},{7,8},{8,7},{9,10},{10,9},{11,... | collective-permute-start | bytes 786440 | tf_op jit(solution)/shard_map/ppermute | solution.py:310
  25.0 5.0 %collective-permute-start.3 = (f32[2,5,6,8,128]{4,3,2,1,0:T(8,128)S(1)}, f32[2,5,6,8,128]{4,3,2,1,0:T(8,128)S(1)}, u32[]{:S(2)}, u32[]{:S(2)}) collective-permute-start(f32[2,5,6,8,128]{4,3,2,1,0:T(8,128)S(1)} %get-tuple-element.57), channel_id=1, source_target_pairs={{0,1},{1,0},{2,3},{3,2},{4,5},{5,4},{6,7},{7,6},{8,9},{9,8},{10,11... | collective-permute-start | bytes 737288 | tf_op jit(solution)/shard_map/ppermute | solution.py:348
  25.8 10.1 %collective-permute-start.4 = (f32[2,5,6,8,128]{4,3,2,1,0:T(8,128)S(1)}, f32[2,5,6,8,128]{4,3,2,1,0:T(8,128)S(1)}, u32[]{:S(2)}, u32[]{:S(2)}) collective-permute-start(f32[2,5,6,8,128]{4,3,2,1,0:T(8,128)S(1)} %get-tuple-element.58), channel_id=1, source_target_pairs={{1,2},{2,1},{3,4},{4,3},{5,6},{6,5},{7,8},{8,7},{9,10},{10,9},{11,... | collective-permute-start | bytes 737288 | tf_op jit(solution)/shard_map/ppermute | solution.py:348

commit v4 on v3

--- a/solution.py
+++ b/solution.py
@@ -17,6 +17,7 @@
 F32 = jnp.float32
 BF16 = jnp.bfloat16
 MIB = 1 << 20
+UNIT = 32767.0
 
 
 def vmem():
@@ -250,11 +251,12 @@
     lax.fori_loop(0, PATCH_X, finish_plane, 0, unroll=2)
     reach = RIM + 1
     kept[p] = placed[pl.ds(RIM - 1, planes + 2)]
-    to_a[p] = placed[pl.ds(jnp.where(even, planes + RIM - 1, 0), reach)]
-    to_b[p] = placed[pl.ds(jnp.where(even, 0, planes + RIM - 1), reach)]
-
-
-def merge_kernel(slabs, acq, kept, from_a, from_b, out, merged):
+    for send, begin in ((to_a, jnp.where(even, planes + RIM - 1, 0)), (to_b, jnp.where(even, 0, planes + RIM - 1))):
+        for j in range(reach):
+            send[p, j] = (placed[begin + j] * UNIT + 0.5).astype(jnp.int32).astype(jnp.int16)
+
+
+def merge_kernel(slabs, acq, kept, from_a, from_b, out, merged, held, sems):
     wide = kept.shape[1]
     planes = wide - 2
     classes, rows, cols = kept.shape[2:]
@@ -267,21 +269,31 @@
     anchor = jnp.full(shape, slab * planes, jnp.int32).astype(F32)
     step = planes / jnp.maximum(count - 1.0, 1.0)
     for p in range(PATCHES):
-        merged[...] = kept[p]
-        merged[pl.ds(a_base, RIM + 1)] += from_a[p]
-        merged[pl.ds(b_base, RIM + 1)] += from_b[p]
-        table = []
+        merged[p] = kept[p]
+        for base, got in ((a_base, from_a), (b_base, from_b)):
+            for j in range(RIM + 1):
+                merged[p, base + j] += got[p, j].astype(jnp.int32).astype(F32) * (1.0 / UNIT)
         for j in range(wide):
-            parts = [merged[j, k] for k in range(classes)]
+            parts = [merged[p, j, k] for k in range(classes)]
             scale = 1.0 / (functools.reduce(jnp.add, parts) + PRIOR)
             parts[0] = parts[0] + PRIOR
-            table.append([v * scale for v in parts])
-        for s in range(MOST_ACQ):
-            place = jnp.clip(anchor + (s * step - 0.5), 0.0, float(slabs * planes - 1)) - anchor
-            used = (s < count).astype(F32)
-            gains = [jnp.maximum(0.0, 1.0 - jnp.abs(place - (j - 1.0))) * used for j in range(wide)]
             for k in range(classes):
-                out[k, s, p * rows : (p + 1) * rows] = functools.reduce(jnp.add, [gains[j] * table[j][k] for j in range(wide)])
+                merged[p, j, k] = parts[k] * scale
+    gains = []
+    for s in range(MOST_ACQ):
+        place = jnp.clip(anchor + (s * step - 0.5), 0.0, float(slabs * planes - 1)) - anchor
+        used = (s < count).astype(F32)
+        gains.append([jnp.maximum(0.0, 1.0 - jnp.abs(place - (j - 1.0))) * used for j in range(wide)])
+    copies = []
+    for k in range(classes):
+        for p in range(PATCHES):
+            column = [merged[p, j, k] for j in range(wide)]
+            for s in range(MOST_ACQ):
+                held[k, s, p * rows : (p + 1) * rows] = functools.reduce(jnp.add, [g * v for g, v in zip(gains[s], column)])
+        copies.append(pltpu.make_async_copy(held.at[k], out.at[k], sems.at[k]))
+        copies[-1].start()
+    for copy in copies:
+        copy.wait()
 
 
 def local(slabs, features, conv_weight, norm_gain, norm_bias, head_weight, head_bias, patch_offsets, fg_mask, acq_counts):
@@ -324,7 +336,7 @@
         name="pre",
     )(patch_offsets, own, from_a, conv_weight, norm_gain, norm_bias, head_weight, head_bias)
     sends = []
-    send_shapes = [shaped((PATCHES, n) + tile, F32) for n in (wide, RIM + 1, RIM + 1)]
+    send_shapes = [shaped((PATCHES, n) + tile, t) for n, t in ((wide, F32), (RIM + 1, jnp.int16), (RIM + 1, jnp.int16))]
     for p in range(PATCHES):
         sends = pl.pallas_call(
             functools.partial(post_kernel, p),
@@ -341,8 +353,12 @@
         functools.partial(merge_kernel, slabs),
         out_shape=shaped((classes, MOST_ACQ, row_total, cols), F32),
         in_specs=[smem()] + [vmem()] * 3,
-        out_specs=vmem(),
-        scratch_shapes=[pltpu.VMEM((wide,) + tile, F32)],
+        out_specs=pl.BlockSpec(memory_space=pltpu.HBM),
+        scratch_shapes=[
+            pltpu.VMEM((PATCHES, wide) + tile, F32),
+            pltpu.VMEM((classes, MOST_ACQ, row_total, cols), F32),
+            pltpu.SemaphoreType.DMA((classes,)),
+        ],
         compiler_params=params,
         name="merge",
     )(acq_counts, kept, lax.ppermute(send_a, "slab", pairs_a), lax.ppermute(send_b, "slab", pairs_b))

time: 37.6 us -> 34.8 us (0.926)
  waiting for transfers between devices: 5.98 us -> 3.52 us
    ppermute x1, waiting for transfers between devices: 5.97 us -> 3.5 us  [local(): lax.ppermute(send_b, 'slab', pairs_b)]
  transfers between devices with their start and end apart: 5 -> 5, of which waited for: 1 -> 1; matrix products, arithmetic and copies ran while one was open for 0% -> 0% of each run, Pallas kernels for 34% -> 36%
where the time goes in v4:
time: 34.8 us; the launch traced here: 34.5 us
  Pallas kernels  19.6 us (56%)
  starting transfers between devices  10.6 us (30%)
  waiting for transfers between devices  3.52 us (10%)
  between operations  0.74 us (2%)
    pallas_call x2, Pallas kernels, local(): pl.pallas_call(functools.partial(post_kernel, p), out_shape=send_shapes +...  8.9 us
    pallas_call x1, Pallas kernels, local(): pl.pallas_call(pre_kernel, out_shape=[taps_shape] * 2 + [conv_shape] * 2...  8.14 us
    ppermute x2, starting transfers between devices, local(): from_b = [lax.ppermute(v, 'slab', pairs_b) for v in to_b]  5.55 us
    ppermute x1, waiting for transfers between devices, local(): lax.ppermute(send_b, 'slab', pairs_b)  3.5 us
    ppermute x1, starting transfers between devices, local(): lax.ppermute(send_b, 'slab', pairs_b)  3.33 us
    pallas_call x1, Pallas kernels, local(): pl.pallas_call(prep_kernel, out_shape=[shaped((PATCHES, planes) + cell, B...  1.47 us
    pallas_call x1, Pallas kernels, local(): pl.pallas_call(functools.partial(merge_kernel, slabs), out_shape=shaped((...  1.1 us
    ppermute x1, starting transfers between devices, local(): lax.ppermute(send_a, 'slab', pairs_a)  0.99 us
  transfers between devices with their start and end apart: 5, of which 1 were waited for; matrix products, arithmetic and copies ran while one was open for 0% of the time, Pallas kernels for 36%

profile of v4, /device:TPU:11, one launch (start us, length us, event | category | flops | bytes accessed | tf_op | source)
XLA Modules:
  0.0 34.5 jit_solution(5179560906696958973)
XLA Ops:
  0.0 1.5 %prep.1 = (bf16[2,6,8,32,128]{4,3,2,1,0:T(8,128)(2,1)S(1)}, bf16[2,4,8,32,128]{4,3,2,1,0:T(8,128)(2,1)S(1)}, bf16[4,8,32,128]{3,2,1,0:T(8,128)(2,1)S(1)}, bf16[4...) custom-call(bf16[32,6,16,128]{3,2,1,0:T(8,128)(2,1)} %refs_0_.1, ...), custom_call_target="tpu_custom_call" | custom-call | tf_op jit(solution)/shard_map/prep/pallas_call | solution.py:309
  1.5 0.7 %collective-permute-start.1 = (bf16[2,4,8,32,128]{4,3,2,1,0:T(8,128)(2,1)S(1)}, bf16[2,4,8,32,128]{4,3,2,1,0:T(8,128)(2,1)S(1)}, u32[]{:S(2)}, u32[]{:S(2)}) collective-permute-start(bf16[2,4,8,32,128]{4,3,2,1,0:T(8,128)(2,1)S(1)} %get-tuple-element.36), channel_id=1, source_target_pairs={{0,1},{1,0},{2,3},{3,2},{4,5},{5,4},{6,7},{7,6},{8,9},{9,8},{10,11... | collective-permute-start | bytes 1572872 | tf_op jit(solution)/shard_map/ppermute | solution.py:321
  2.2 3.0 %collective-permute-start.2 = (bf16[4,8,32,128]{3,2,1,0:T(8,128)(2,1)S(1)}, bf16[4,8,32,128]{3,2,1,0:T(8,128)(2,1)S(1)}, u32[]{:S(2)}, u32[]{:S(2)}) collective-permute-start(bf16[4,8,32,128]{3,2,1,0:T(8,128)(2,1)S(1)} %get-tuple-element.49), channel_id=1, source_target_pairs={{1,2},{2,1},{3,4},{4,3},{5,6},{6,5},{7,8},{8,7},{9,10},{10,9},{11,... | collective-permute-start | bytes 786440 | tf_op jit(solution)/shard_map/ppermute | solution.py:322
  5.3 2.5 %collective-permute-start = (bf16[4,8,32,128]{3,2,1,0:T(8,128)(2,1)S(1)}, bf16[4,8,32,128]{3,2,1,0:T(8,128)(2,1)S(1)}, u32[]{:S(2)}, u32[]{:S(2)}) collective-permute-start(bf16[4,8,32,128]{3,2,1,0:T(8,128)(2,1)S(1)} %get-tuple-element.34), channel_id=1, source_target_pairs={{1,2},{2,1},{3,4},{4,3},{5,6},{6,5},{7,8},{8,7},{9,10},{10,9},{11,... | collective-permute-start | bytes 786440 | tf_op jit(solution)/shard_map/ppermute | solution.py:322
  7.8 0.0 collective-permute-done.1.from_a
  7.8 8.1 %pre.1 = (bf16[15,10,96,128]{3,2,1,0:T(8,128)(2,1)S(1)}, bf16[15,10,96,128]{3,2,1,0:T(8,128)(2,1)S(1)}, f32[10,4,128,256]{3,2,1,0:T(8,128)S(1)}, f32[10,4,128,25...) custom-call(s32[1,2]{1,0:T(1,128)S(1)} %get-tuple-element.32.offs, ...), custom_call_target="tpu_custom_call" | custom-call | tf_op jit(solution)/shard_map/pre/pallas_call | solution.py:330
  15.9 0.0 collective-permute-done.2.from_b
  16.0 4.2 %post0.1 = (f32[2,8,6,8,128]{4,3,2,1,0:T(8,128)S(1)}, s16[2,5,6,8,128]{4,3,2,1,0:T(8,128)(2,1)S(1)}, s16[2,5,6,8,128]{4,3,2,1,0:T(8,128)(2,1)S(1)}, bf16[15,10,9...) custom-call(s32[1,2]{1,0:T(1,128)S(1)} %get-tuple-element.32.offs, ...), custom_call_target="tpu_custom_call", output_to_operand_aliasing={{3}: (3, {}), {4}: (4, {}), {5}: (5, {})} | custom-call | tf_op jit(solution)/shard_map/post0/pallas_call | solution.py:341
  20.2 0.0 collective-permute-done.from_b
  20.2 4.7 %post1.1 = (f32[2,8,6,8,128]{4,3,2,1,0:T(8,128)S(1)}, s16[2,5,6,8,128]{4,3,2,1,0:T(8,128)(2,1)S(1)}, s16[2,5,6,8,128]{4,3,2,1,0:T(8,128)(2,1)S(1)}, bf16[15,10,9...) custom-call(s32[1,2]{1,0:T(1,128)S(1)} %get-tuple-element.32.offs, ...), custom_call_target="tpu_custom_call", output_to_operand_aliasing={{3}: (3, {}), {4}: (4, {}), {5}: (5, {}), {0}: (10, {}), {1... | custom-call | tf_op jit(solution)/shard_map/post1/pallas_call | solution.py:341
  24.9 1.0 %collective-permute-start.3 = (s16[2,5,6,8,128]{4,3,2,1,0:T(8,128)(2,1)S(1)}, s16[2,5,6,8,128]{4,3,2,1,0:T(8,128)(2,1)S(1)}, u32[]{:S(2)}, u32[]{:S(2)}) collective-permute-start(s16[2,5,6,8,128]{4,3,2,1,0:T(8,128)(2,1)S(1)} %get-tuple-element.57), channel_id=1, source_target_pairs={{0,1},{1,0},{2,3},{3,2},{4,5},{5,4},{6,7},{7,6},{8,9},{9,8},{10,11... | collective-permute-start | bytes 368648 | tf_op jit(solution)/shard_map/ppermute | solution.py:364
  25.9 3.3 %collective-permute-start.4 = (s16[2,5,6,8,128]{4,3,2,1,0:T(8,128)(2,1)S(1)}, s16[2,5,6,8,128]{4,3,2,1,0:T(8,128)(2,1)S(1)}, u32[]{:S(2)}, u32[]{:S(2)}) collective-permute-start(s16[2,5,6,8,128]{4,3,2,1,0:T(8,128)(2,1)S(1)} %get-tuple-element.58), channel_id=1, source_target_pairs={{1,2},{2,1},{3,4},{4,3},{5,6},{6,5},{7,8},{8,7},{9,10},{10,9},{11,... | collective-permute-start | bytes 368648 | tf_op jit(solution)/shard_map/ppermute | solution.py:364
  29.9 0.0 collective-permute-done.3.from_a
  29.9 3.5 %collective-permute-done.4.from_b = s16[2,5,6,8,128]{4,3,2,1,0:T(8,128)(2,1)S(1)} collective-permute-done((s16[2,5,6,8,128]{4,3,2,1,0:T(8,128)(2,1)S(1)}, s16[2,5,6,8,128]{4,3,2,1,0:T(8,128)(2,1)S(1)}, u32[]{:S(2)}, u32[]{:S(2)}) %collective-permute-start.4) | collective-permute-done | bytes 122912 | tf_op jit(solution)/shard_map/ppermute | solution.py:364
  33.4 1.1 %merge.1 = f32[6,8,16,128]{3,2,1,0:T(8,128)} custom-call(s32[1]{0:T(128)S(6)} %copy.28.acq, f32[2,8,6,8,128]{4,3,2,1,0:T(8,128)S(1)} %get-tuple-element.56.kept, s16[2,5,6,8,128]{4,3,2,1,0:T(8,128)(2,1)S(1)} %collective-permute-done.3.from_a, s16[2,5,6,8,128]{4,3,2,1,0:T(8,128)(2,1)S(1)} %collective-permute-done.4.from_b), custom_call_target="tpu_custom_call" | custom-call | tf_op jit(solution)/shard_map/merge/pallas_call | solution.py:352
Async XLA Ops:
  1.5 6.3 %collective-permute-start.1 = (bf16[2,4,8,32,128]{4,3,2,1,0:T(8,128)(2,1)S(1)}, bf16[2,4,8,32,128]{4,3,2,1,0:T(8,128)(2,1)S(1)}, u32[]{:S(2)}, u32[]{:S(2)}) collective-permute-start(bf16[2,4,8,32,128]{4,3,2,1,0:T(8,128)(2,1)S(1)} %get-tuple-element.36), channel_id=1, source_target_pairs={{0,1},{1,0},{2,3},{3,2},{4,5},{5,4},{6,7},{7,6},{8,9},{9,8},{10,11... | collective-permute-start | bytes 1572872 | tf_op jit(solution)/shard_map/ppermute | solution.py:321
  2.2 13.7 %collective-permute-start.2 = (bf16[4,8,32,128]{3,2,1,0:T(8,128)(2,1)S(1)}, bf16[4,8,32,128]{3,2,1,0:T(8,128)(2,1)S(1)}, u32[]{:S(2)}, u32[]{:S(2)}) collective-permute-start(bf16[4,8,32,128]{3,2,1,0:T(8,128)(2,1)S(1)} %get-tuple-element.49), channel_id=1, source_target_pairs={{1,2},{2,1},{3,4},{4,3},{5,6},{6,5},{7,8},{8,7},{9,10},{10,9},{11,... | collective-permute-start | bytes 786440 | tf_op jit(solution)/shard_map/ppermute | solution.py:322
  5.3 14.9 %collective-permute-start = (bf16[4,8,32,128]{3,2,1,0:T(8,128)(2,1)S(1)}, bf16[4,8,32,128]{3,2,1,0:T(8,128)(2,1)S(1)}, u32[]{:S(2)}, u32[]{:S(2)}) collective-permute-start(bf16[4,8,32,128]{3,2,1,0:T(8,128)(2,1)S(1)} %get-tuple-element.34), channel_id=1, source_target_pairs={{1,2},{2,1},{3,4},{4,3},{5,6},{6,5},{7,8},{8,7},{9,10},{10,9},{11,... | collective-permute-start | bytes 786440 | tf_op jit(solution)/shard_map/ppermute | solution.py:322
  24.9 5.0 %collective-permute-start.3 = (s16[2,5,6,8,128]{4,3,2,1,0:T(8,128)(2,1)S(1)}, s16[2,5,6,8,128]{4,3,2,1,0:T(8,128)(2,1)S(1)}, u32[]{:S(2)}, u32[]{:S(2)}) collective-permute-start(s16[2,5,6,8,128]{4,3,2,1,0:T(8,128)(2,1)S(1)} %get-tuple-element.57), channel_id=1, source_target_pairs={{0,1},{1,0},{2,3},{3,2},{4,5},{5,4},{6,7},{7,6},{8,9},{9,8},{10,11... | collective-permute-start | bytes 368648 | tf_op jit(solution)/shard_map/ppermute | solution.py:364
  25.9 7.5 %collective-permute-start.4 = (s16[2,5,6,8,128]{4,3,2,1,0:T(8,128)(2,1)S(1)}, s16[2,5,6,8,128]{4,3,2,1,0:T(8,128)(2,1)S(1)}, u32[]{:S(2)}, u32[]{:S(2)}) collective-permute-start(s16[2,5,6,8,128]{4,3,2,1,0:T(8,128)(2,1)S(1)} %get-tuple-element.58), channel_id=1, source_target_pairs={{1,2},{2,1},{3,4},{4,3},{5,6},{6,5},{7,8},{8,7},{9,10},{10,9},{11,... | collective-permute-start | bytes 368648 | tf_op jit(solution)/shard_map/ppermute | solution.py:364

commit v5 on v4

--- a/solution.py
+++ b/solution.py
@@ -100,29 +100,32 @@
         taps[plane, h + 1] = jnp.concatenate([left, value, right], 0)
 
 
-def conv_planes(first, begin, end, fresh, taps, w_all, conv, stats):
+def conv_plane(x, first, fresh, taps, w_all, conv, stats):
     zero_plane = taps.shape[0] - 1
     cols = taps.shape[-1]
-
+    i = first + x
+    below = jnp.where(x == 0, zero_plane, i - 1)
+    above = jnp.where(x == PATCH_X - 1, zero_plane, i + 1)
+    weights = w_all[...]
+    for r in range(PATCH_ROWS // 2):
+        halves = []
+        for h in (r, r + PATCH_ROWS // 2):
+            halves.append(jnp.concatenate([taps[t, h : h + 3].reshape(-1, cols) for t in (below, i, above)], 0))
+        out = jnp.dot(weights, jnp.concatenate(halves, 1), preferred_element_type=F32)
+        conv[x, r] = out
+        one, two = out[:, :cols], out[:, cols:]
+        base = stats[0]
+        if fresh is not None and r == 0:
+            base = jnp.where(fresh, 0.5 * (one + two), base)
+            stats[0] = base
+        one, two = one - base, two - base
+        stats[1] += one + two
+        stats[2] += one * one + two * two
+
+
+def conv_planes(first, begin, end, fresh, *refs):
     def one_plane(x):
-        i = first + x
-        below = jnp.where(x == 0, zero_plane, i - 1)
-        above = jnp.where(x == PATCH_X - 1, zero_plane, i + 1)
-        weights = w_all[...]
-        for r in range(PATCH_ROWS // 2):
-            halves = []
-            for h in (r, r + PATCH_ROWS // 2):
-                halves.append(jnp.concatenate([taps[t, h : h + 3].reshape(-1, cols) for t in (below, i, above)], 0))
-            out = jnp.dot(weights, jnp.concatenate(halves, 1), preferred_element_type=F32)
-            conv[x, r] = out
-            one, two = out[:, :cols], out[:, cols:]
-            base = stats[0]
-            if fresh and r == 0:
-                base = jnp.where(x == begin, 0.5 * (one + two), base)
-                stats[0] = base
-            one, two = one - base, two - base
-            stats[1] += one + two
-            stats[2] += one * one + two * two
+        conv_plane(x, first, x == begin if fresh else None, *refs)
 
     def two_planes(y, _):
         one_plane(begin + 2 * y)
@@ -146,7 +149,7 @@
     return even, first, jnp.where(even, foreign, 0), jnp.where(even, PATCH_X, PATCH_X - foreign)
 
 
-def pre_kernel(offs, own, from_a, wt, gain, nbias, head_w, head_b, taps0, taps1, conv0, conv1, stats0, stats1, w_all, head, hbias, scales):
+def pre_kernel(offs, own, from_a, wt, gain, nbias, head_w, head_b, taps0, taps1, conv0, stats0, w_all, head, hbias, scales):
     planes = own.shape[1]
     classes, folds, channels = head_w.shape
     outs = folds * channels
@@ -163,7 +166,7 @@
     scales[0] = jnp.broadcast_to(column_of(gain, folds, channels), (outs, cols))
     scales[1] = jnp.broadcast_to(column_of(nbias, folds, channels), (outs, cols))
     zero_row = jnp.zeros((3 * channels, cols), BF16)
-    for p, (taps, conv, stats) in enumerate(((taps0, conv0, stats0), (taps1, conv1, stats1))):
+    for p, taps in enumerate((taps0, taps1)):
         taps[span] = jnp.zeros(taps.shape[1:], BF16)
 
         def pad_rows(i, _):
@@ -182,26 +185,24 @@
         lax.fori_loop(0, span, pad_rows, 0)
         lax.fori_loop(0, planes, fill_own, 0, unroll=2)
         lax.fori_loop(0, RIM, fill_a, 0, unroll=2)
-        stats[...] = jnp.zeros_like(stats)
-        _, first, begin, end = patch_plan(offs, p, planes)
-        conv_planes(first, begin, end, True, taps, w_all, conv, stats)
-
-
-def post_kernel(p, offs, mask, from_b, taps_in, conv_in, stats_in, w_all, head, hbias, scales, *refs):
-    kept, to_a, to_b, taps, conv, stats, placed = refs[-7:]
-    planes = kept.shape[1] - 2
-    classes = kept.shape[2]
-    outs, cols = stats.shape[1:]
-    folds = head.shape[0] // classes // 2
-    even, first, begin, end = patch_plan(offs, p, planes)
-    b_base = jnp.where(even, 0, RIM + planes)
-
-    def fill_b(i, _):
-        fill_taps(taps, i + b_base, from_b.at[i])
-        return 0
-
-    lax.fori_loop(0, RIM, fill_b, 0, unroll=2)
-    conv_planes(first, jnp.where(even, 0, end), jnp.where(even, begin, PATCH_X), False, taps, w_all, conv, stats)
+    stats0[...] = jnp.zeros_like(stats0)
+    _, first, begin, end = patch_plan(offs, 0, planes)
+    conv_planes(first, begin, end, True, taps0, w_all, conv0, stats0)
+
+
+def fill_b(even, from_b, taps):
+    planes = taps.shape[0] - 1 - 2 * RIM
+    base = jnp.where(even, 0, RIM + planes)
+
+    def fill(i, _):
+        fill_taps(taps, i + base, from_b.at[i])
+        return 0
+
+    lax.fori_loop(0, RIM, fill, 0, unroll=2)
+
+
+def settle(stats, scales, norm):
+    cols = stats.shape[-1]
     count = float(PATCH_X * PATCH_ROWS)
     total = stats[1] * (1.0 / count)
     spread = stats[2] - total * stats[1]
@@ -209,57 +210,106 @@
     mean = jnp.mean(lane_mean, axis=1, keepdims=True)
     dev = lane_mean - mean
     var = jnp.sum(spread + count * dev * dev, axis=1, keepdims=True) * (1.0 / (count * cols))
-    scale = lax.rsqrt(var + EPS) * scales[0, :, :1]
-    scale_b = jnp.broadcast_to(scale, (outs, 2 * cols))
-    offset_b = jnp.broadcast_to(scales[1, :, :1] - mean * scale, (outs, 2 * cols))
-    keep = mask[0, p].astype(F32) * (1.0 / folds)
-    placed[...] = jnp.zeros_like(placed)
-    sub = lax.broadcasted_iota(jnp.int32, (2 * folds, cols), 0)
-    lane = lax.broadcasted_iota(jnp.int32, (2 * folds, cols), 1)
+    scale = lax.rsqrt(var + EPS) * scales[0]
+    norm[0] = scale
+    norm[1] = scales[1] - mean * scale
+
+
+def clear_rest(first, placed):
+    for q in range(placed.shape[0] - PATCH_X):
+        placed[jnp.where(q < first, q, q + PATCH_X)] = jnp.zeros(placed.shape[1:], F32)
+
+
+def finish_plane(x, first, keep, conv, norm, head, hbias, placed):
+    classes, rows, cols = placed.shape[1:]
+    folds = rows // 2
+    sub = lax.broadcasted_iota(jnp.int32, (rows, cols), 0)
+    lane = lax.broadcasted_iota(jnp.int32, (rows, cols), 1)
+    lower = sub < folds
+    scale, offset = (jnp.concatenate([norm[i], norm[i]], 1) for i in range(2))
+    table = [[] for _ in range(classes)]
+    for r in range(PATCH_ROWS // 2):
+        act = conv[x, r] * scale + offset
+        act = jnp.maximum(act, 0.01 * act)
+        high = act.astype(BF16)
+        low = (act - high.astype(F32)).astype(BF16)
+        logits = jnp.dot(head[...], jnp.concatenate([high, low], 0), preferred_element_type=F32) + hbias[...]
+        parts = []
+        for k in range(classes):
+            both = logits[k * rows : (k + 1) * rows]
+            parts.append(jnp.where(lower, both[:, :cols], both[:, cols:]))
+        top = functools.reduce(jnp.maximum, parts)
+        parts = [jnp.exp(v - top) for v in parts]
+        denom = 1.0 / functools.reduce(jnp.add, parts)
+        for k in range(classes):
+            table[k].append(parts[k] * denom)
     line = gauss(sub.astype(F32), PATCH_ROWS) * gauss(lane.astype(F32), cols)
-
-    def finish_plane(x, _):
-        lower = sub < folds
-        table = [[] for _ in range(classes)]
-        for r in range(PATCH_ROWS // 2):
-            act = conv[x, r] * scale_b + offset_b
-            act = jnp.maximum(act, 0.01 * act)
-            high = act.astype(BF16)
-            low = (act - high.astype(F32)).astype(BF16)
-            logits = jnp.dot(head[...], jnp.concatenate([high, low], 0), preferred_element_type=F32) + hbias[...]
-            parts = []
-            for k in range(classes):
-                both = logits[k * 2 * folds : (k + 1) * 2 * folds]
-                parts.append(jnp.where(lower, both[:, :cols], both[:, cols:]))
-            top = functools.reduce(jnp.maximum, parts)
-            parts = [jnp.exp(v - top) for v in parts]
-            denom = 1.0 / functools.reduce(jnp.add, parts)
-            for k in range(classes):
-                table[k].append(parts[k] * denom)
-        window = line * (gauss(jnp.full((2 * folds, cols), x, jnp.int32).astype(F32), PATCH_X) * keep)
-        odd = (sub % 2) == 1
-        high_pair = (sub % 4) >= 2
-        for k in range(classes):
-            v = table[k]
-            pairs = []
-            for q in (0, 2):
-                pairs.append(jnp.where(odd, v[q + 1] + pltpu.roll(v[q + 1], 1, 0), v[q] + pltpu.roll(v[q], 7, 0)))
-            full = jnp.where(high_pair, pairs[1] + pltpu.roll(pairs[1], 2, 0), pairs[0] + pltpu.roll(pairs[0], 6, 0))
-            placed[first + x, k] = full * window
-        return 0
-
-    lax.fori_loop(0, PATCH_X, finish_plane, 0, unroll=2)
-    reach = RIM + 1
-    kept[p] = placed[pl.ds(RIM - 1, planes + 2)]
+    window = line * (gauss(jnp.full((rows, cols), x, jnp.int32).astype(F32), PATCH_X) * keep)
+    odd = (sub % 2) == 1
+    high_pair = (sub % 4) >= 2
+    for k in range(classes):
+        v = table[k]
+        pairs = []
+        for q in (0, 2):
+            pairs.append(jnp.where(odd, v[q + 1] + pltpu.roll(v[q + 1], 1, 0), v[q] + pltpu.roll(v[q], 7, 0)))
+        full = jnp.where(high_pair, pairs[1] + pltpu.roll(pairs[1], 2, 0), pairs[0] + pltpu.roll(pairs[0], 6, 0))
+        placed[first + x, k] = full * window
+
+
+def mid_kernel(offs, mask, from_b, taps0_in, conv0_in, stats0_in, taps1, w_all, head, hbias, scales, placed, norm, conv1, stats1, taps0, conv0, stats0):
+    planes = taps0.shape[0] - 1 - 2 * RIM
+    folds = placed.shape[2] // 2
+    even, first0, begin, end = patch_plan(offs, 0, planes)
+    fill_b(even, from_b, taps0)
+    conv_planes(first0, jnp.where(even, 0, end), jnp.where(even, begin, PATCH_X), False, taps0, w_all, conv0, stats0)
+    settle(stats0, scales, norm)
+    clear_rest(first0, placed)
+    stats1[...] = jnp.zeros_like(stats1)
+    keep = mask[0, 0].astype(F32) * (1.0 / folds)
+    _, first1, begin, end = patch_plan(offs, 1, planes)
+
+    def both(y, _):
+        finish_plane(y, first0, keep, conv0, norm, head, hbias, placed)
+        conv_plane(begin + y, first1, y == 0, taps1, w_all, conv1, stats1)
+        return 0
+
+    lax.fori_loop(0, end - begin, both, 0)
+
+
+def post_kernel(offs, mask, from_b, conv0, norm0, w_all, head, hbias, scales, taps1_in, conv1_in, stats1_in, placed0_in, placed0, placed1, to_a, to_b, taps1, conv1, stats1, norm1):
+    planes = taps1.shape[0] - 1 - 2 * RIM
+    folds = placed1.shape[2] // 2
+    even, first0, _, _ = patch_plan(offs, 0, planes)
+    _, first1, begin, end = patch_plan(offs, 1, planes)
+    fill_b(even, from_b, taps1)
+    keep0, keep1 = (mask[0, p].astype(F32) * (1.0 / folds) for p in range(PATCHES))
+    done = end - begin
+    waiting = jnp.where(even, 0, end)
+
+    def both(y, _):
+        finish_plane(done + y, first0, keep0, conv0, norm0, head, hbias, placed0)
+        conv_plane(waiting + y, first1, None, taps1, w_all, conv1, stats1)
+        return 0
+
+    lax.fori_loop(0, PATCH_X - done, both, 0)
+    settle(stats1, scales, norm1)
+    clear_rest(first1, placed1)
+
+    def finish(x, _):
+        finish_plane(x, first1, keep1, conv1, norm1, head, hbias, placed1)
+        return 0
+
+    lax.fori_loop(0, PATCH_X, finish, 0, unroll=2)
     for send, begin in ((to_a, jnp.where(even, planes + RIM - 1, 0)), (to_b, jnp.where(even, 0, planes + RIM - 1))):
-        for j in range(reach):
-            send[p, j] = (placed[begin + j] * UNIT + 0.5).astype(jnp.int32).astype(jnp.int16)
-
-
-def merge_kernel(slabs, acq, kept, from_a, from_b, out, merged, held, sems):
-    wide = kept.shape[1]
-    planes = wide - 2
-    classes, rows, cols = kept.shape[2:]
+        for p, placed in enumerate((placed0, placed1)):
+            for j in range(RIM + 1):
+                send[p, j] = (placed[begin + j] * UNIT + 0.5).astype(jnp.int32).astype(jnp.int16)
+
+
+def merge_kernel(slabs, acq, placed0, placed1, from_a, from_b, out, merged, held, sems):
+    planes = placed0.shape[0] - 2 * RIM
+    wide = planes + 2
+    classes, rows, cols = placed0.shape[1:]
     slab = lax.axis_index("slab")
     even = lax.rem(slab, 2) == 0
     a_base = jnp.where(even, wide - RIM - 1, 0)
@@ -268,8 +318,8 @@
     count = jnp.full(shape, acq[0], jnp.int32).astype(F32)
     anchor = jnp.full(shape, slab * planes, jnp.int32).astype(F32)
     step = planes / jnp.maximum(count - 1.0, 1.0)
-    for p in range(PATCHES):
-        merged[p] = kept[p]
+    for p, placed in enumerate((placed0, placed1)):
+        merged[p] = placed[RIM - 1 : RIM - 1 + wide]
         for base, got in ((a_base, from_a), (b_base, from_b)):
             for j in range(RIM + 1):
                 merged[p, base + j] += got[p, j].astype(jnp.int32).astype(F32) * (1.0 / UNIT)
@@ -327,32 +377,40 @@
     conv_shape = shaped((PATCH_X, PATCH_ROWS // 2, outs, 2 * cols), F32)
     stats_shape = shaped((3, outs, cols), F32)
     table_shapes = [shaped((outs, 27 * channels), BF16), shaped((classes * 2 * folds, 2 * outs), BF16), shaped((classes * 2 * folds, 2 * cols), F32), shaped((2, outs, cols), F32)]
-    made = pl.pallas_call(
+    placed_shape = shaped((span,) + tile, F32)
+    norm_shape = shaped((2, outs, cols), F32)
+    send_shape = shaped((PATCHES, RIM + 1) + tile, jnp.int16)
+    taps0, taps1, conv0, stats0, *tables = pl.pallas_call(
         pre_kernel,
-        out_shape=[taps_shape] * 2 + [conv_shape] * 2 + [stats_shape] * 2 + table_shapes,
+        out_shape=[taps_shape, taps_shape, conv_shape, stats_shape] + table_shapes,
         in_specs=[smem()] + [vmem()] * 7,
-        out_specs=[vmem()] * 10,
+        out_specs=[vmem()] * 8,
         compiler_params=params,
         name="pre",
     )(patch_offsets, own, from_a, conv_weight, norm_gain, norm_bias, head_weight, head_bias)
-    sends = []
-    send_shapes = [shaped((PATCHES, n) + tile, t) for n, t in ((wide, F32), (RIM + 1, jnp.int16), (RIM + 1, jnp.int16))]
-    for p in range(PATCHES):
-        sends = pl.pallas_call(
-            functools.partial(post_kernel, p),
-            out_shape=send_shapes + [taps_shape, conv_shape, stats_shape],
-            in_specs=[smem()] * 2 + [vmem()] * (8 + len(sends)),
-            out_specs=[vmem()] * 6,
-            input_output_aliases={3: 3, 4: 4, 5: 5} | {10 + i: i for i in range(len(sends))},
-            scratch_shapes=[pltpu.VMEM((span,) + tile, F32)],
-            compiler_params=params,
-            name=f"post{p}",
-        )(patch_offsets, fg_mask, from_b[p], made[p], made[2 + p], made[4 + p], *made[6:], *sends)[:3]
-    kept, send_a, send_b = sends
+    placed0, norm0, conv1, stats1, _, conv0, _ = pl.pallas_call(
+        mid_kernel,
+        out_shape=[placed_shape, norm_shape, conv_shape, stats_shape, taps_shape, conv_shape, stats_shape],
+        in_specs=[smem()] * 2 + [vmem()] * 9,
+        out_specs=[vmem()] * 7,
+        input_output_aliases={3: 4, 4: 5, 5: 6},
+        compiler_params=params,
+        name="mid",
+    )(patch_offsets, fg_mask, from_b[0], taps0, conv0, stats0, taps1, *tables)
+    placed0, placed1, send_a, send_b, *_ = pl.pallas_call(
+        post_kernel,
+        out_shape=[placed_shape, placed_shape, send_shape, send_shape, taps_shape, conv_shape, stats_shape],
+        in_specs=[smem()] * 2 + [vmem()] * 11,
+        out_specs=[vmem()] * 7,
+        input_output_aliases={12: 0, 9: 4, 10: 5, 11: 6},
+        scratch_shapes=[pltpu.VMEM(norm_shape.shape, F32)],
+        compiler_params=params,
+        name="post",
+    )(patch_offsets, fg_mask, from_b[1], conv0, norm0, *tables, taps1, conv1, stats1, placed0)
     return pl.pallas_call(
         functools.partial(merge_kernel, slabs),
         out_shape=shaped((classes, MOST_ACQ, row_total, cols), F32),
-        in_specs=[smem()] + [vmem()] * 3,
+        in_specs=[smem()] + [vmem()] * 4,
         out_specs=pl.BlockSpec(memory_space=pltpu.HBM),
         scratch_shapes=[
             pltpu.VMEM((PATCHES, wide) + tile, F32),
@@ -361,7 +419,7 @@
         ],
         compiler_params=params,
         name="merge",
-    )(acq_counts, kept, lax.ppermute(send_a, "slab", pairs_a), lax.ppermute(send_b, "slab", pairs_b))
+    )(acq_counts, placed0, placed1, lax.ppermute(send_a, "slab", pairs_a), lax.ppermute(send_b, "slab", pairs_b))
 
 
 def solution(mesh):

time: 34.8 us -> 37 us (1.063)
  the two profiles are of different devices: /device:TPU:11 before, /device:TPU:17 now
where the time goes in v5:
time: 37 us; the launch traced here: 36.8 us
  Pallas kernels  19.6 us (53%)
  starting transfers between devices  9.45 us (26%)
  waiting for transfers between devices  7.02 us (19%)
  between operations  0.74 us (2%)
    pallas_call x1, Pallas kernels, local(): pl.pallas_call(mid_kernel, out_shape=[placed_shape, norm_shape, conv_shap...  7.98 us
    ppermute x2, starting transfers between devices, local(): from_b = [lax.ppermute(v, 'slab', pairs_b) for v in to_b]  5.55 us
    pallas_call x1, Pallas kernels, local(): pl.pallas_call(post_kernel, out_shape=[placed_shape, placed_shape, send_s...  4.58 us
    pallas_call x1, Pallas kernels, local(): pl.pallas_call(pre_kernel, out_shape=[taps_shape, taps_shape, conv_shape,...  4.47 us
    ppermute x1, waiting for transfers between devices, local(): lax.ppermute(send_b, 'slab', pairs_b)  3.77 us
    ppermute x2, waiting for transfers between devices, local(): from_b = [lax.ppermute(v, 'slab', pairs_b) for v in to_b]  3.25 us
    ppermute x1, starting transfers between devices, local(): lax.ppermute(send_b, 'slab', pairs_b)  3.08 us
    pallas_call x1, Pallas kernels, local(): pl.pallas_call(prep_kernel, out_shape=[shaped((PATCHES, planes) + cell, B...  1.47 us
  transfers between devices with their start and end apart: 5, of which 2 were waited for; matrix products, arithmetic and copies ran while one was open for 0% of the time, Pallas kernels for 34%

profile of v5, /device:TPU:17, one launch (start us, length us, event | category | flops | bytes accessed | tf_op | source)
XLA Modules:
  0.0 36.8 jit_solution(3881670432226014601)
XLA Ops:
  0.0 1.5 %prep.1 = (bf16[2,6,8,32,128]{4,3,2,1,0:T(8,128)(2,1)S(1)}, bf16[2,4,8,32,128]{4,3,2,1,0:T(8,128)(2,1)S(1)}, bf16[4,8,32,128]{3,2,1,0:T(8,128)(2,1)S(1)}, bf16[4...) custom-call(bf16[32,6,16,128]{3,2,1,0:T(8,128)(2,1)} %refs_0_.1, ...), custom_call_target="tpu_custom_call" | custom-call | tf_op jit(solution)/shard_map/prep/pallas_call | solution.py:359
  1.5 0.7 %collective-permute-start.2 = (bf16[2,4,8,32,128]{4,3,2,1,0:T(8,128)(2,1)S(1)}, bf16[2,4,8,32,128]{4,3,2,1,0:T(8,128)(2,1)S(1)}, u32[]{:S(2)}, u32[]{:S(2)}) collective-permute-start(bf16[2,4,8,32,128]{4,3,2,1,0:T(8,128)(2,1)S(1)} %get-tuple-element.38), channel_id=1, source_target_pairs={{0,1},{1,0},{2,3},{3,2},{4,5},{5,4},{6,7},{7,6},{8,9},{9,8},{10,11... | collective-permute-start | bytes 1572872 | tf_op jit(solution)/shard_map/ppermute | solution.py:371
  2.2 3.0 %collective-permute-start.1 = (bf16[4,8,32,128]{3,2,1,0:T(8,128)(2,1)S(1)}, bf16[4,8,32,128]{3,2,1,0:T(8,128)(2,1)S(1)}, u32[]{:S(2)}, u32[]{:S(2)}) collective-permute-start(bf16[4,8,32,128]{3,2,1,0:T(8,128)(2,1)S(1)} %get-tuple-element.36), channel_id=1, source_target_pairs={{1,2},{2,1},{3,4},{4,3},{5,6},{6,5},{7,8},{8,7},{9,10},{10,9},{11,... | collective-permute-start | bytes 786440 | tf_op jit(solution)/shard_map/ppermute | solution.py:372
  5.3 2.5 %collective-permute-start = (bf16[4,8,32,128]{3,2,1,0:T(8,128)(2,1)S(1)}, bf16[4,8,32,128]{3,2,1,0:T(8,128)(2,1)S(1)}, u32[]{:S(2)}, u32[]{:S(2)}) collective-permute-start(bf16[4,8,32,128]{3,2,1,0:T(8,128)(2,1)S(1)} %get-tuple-element.35), channel_id=1, source_target_pairs={{1,2},{2,1},{3,4},{4,3},{5,6},{6,5},{7,8},{8,7},{9,10},{10,9},{11,... | collective-permute-start | bytes 786440 | tf_op jit(solution)/shard_map/ppermute | solution.py:372
  7.8 0.0 collective-permute-done.2.from_a
  7.8 4.5 %pre.1 = (bf16[15,10,96,128]{3,2,1,0:T(8,128)(2,1)S(1)}, bf16[15,10,96,128]{3,2,1,0:T(8,128)(2,1)S(1)}, f32[10,4,128,256]{3,2,1,0:T(8,128)S(1)}, f32[3,128,128]{...) custom-call(s32[1,2]{1,0:T(1,128)S(1)} %get-tuple-element.33.offs, ...), custom_call_target="tpu_custom_call" | custom-call | tf_op jit(solution)/shard_map/pre/pallas_call | solution.py:383
  12.3 3.2 %collective-permute-done.1.from_b = bf16[4,8,32,128]{3,2,1,0:T(8,128)(2,1)S(1)} collective-permute-done((bf16[4,8,32,128]{3,2,1,0:T(8,128)(2,1)S(1)}, bf16[4,8,32,128]{3,2,1,0:T(8,128)(2,1)S(1)}, u32[]{:S(2)}, u32[]{:S(2)}) %collective-permute-start.1) | collective-permute-done | bytes 262176 | tf_op jit(solution)/shard_map/ppermute | solution.py:372
  15.5 8.0 %mid.1 = (f32[14,6,8,128]{3,2,1,0:T(8,128)S(1)}, f32[2,128,128]{2,1,0:T(8,128)S(1)}, f32[10,4,128,256]{3,2,1,0:T(8,128)S(1)}, f32[3,128,128]{2,1,0:T(8,128)S(1)}...) custom-call(s32[1,2]{1,0:T(1,128)S(1)} %get-tuple-element.33.offs, ...), custom_call_target="tpu_custom_call", output_to_operand_aliasing={{4}: (3, {}), {5}: (4, {}), {6}: (5, {})} | custom-call | tf_op jit(solution)/shard_map/mid/pallas_call | solution.py:391
  23.5 0.0 collective-permute-done.from_b
  23.5 4.6 %post.1 = (f32[14,6,8,128]{3,2,1,0:T(8,128)S(1)}, f32[14,6,8,128]{3,2,1,0:T(8,128)S(1)}, s16[2,5,6,8,128]{4,3,2,1,0:T(8,128)(2,1)S(1)}, s16[2,5,6,8,128]{4,3,2,1...) custom-call(s32[1,2]{1,0:T(1,128)S(1)} %get-tuple-element.33.offs, ...), custom_call_target="tpu_custom_call", output_to_operand_aliasing={{0}: (12, {}), {4}: (9, {}), {5}: (10, {}), {6}: (11, {})} | custom-call | tf_op jit(solution)/shard_map/post/pallas_call | solution.py:400
  28.1 0.1 collective-permute-start.3
  28.2 3.1 %collective-permute-start.4 = (s16[2,5,6,8,128]{4,3,2,1,0:T(8,128)(2,1)S(1)}, s16[2,5,6,8,128]{4,3,2,1,0:T(8,128)(2,1)S(1)}, u32[]{:S(2)}, u32[]{:S(2)}) collective-permute-start(s16[2,5,6,8,128]{4,3,2,1,0:T(8,128)(2,1)S(1)} %get-tuple-element.60), channel_id=1, source_target_pairs={{1,2},{2,1},{3,4},{4,3},{5,6},{6,5},{7,8},{8,7},{9,10},{10,9},{11,... | collective-permute-start | bytes 368648 | tf_op jit(solution)/shard_map/ppermute | solution.py:422
  31.9 0.0 collective-permute-done.3.from_a
  31.9 3.8 %collective-permute-done.4.from_b = s16[2,5,6,8,128]{4,3,2,1,0:T(8,128)(2,1)S(1)} collective-permute-done((s16[2,5,6,8,128]{4,3,2,1,0:T(8,128)(2,1)S(1)}, s16[2,5,6,8,128]{4,3,2,1,0:T(8,128)(2,1)S(1)}, u32[]{:S(2)}, u32[]{:S(2)}) %collective-permute-start.4) | collective-permute-done | bytes 122912 | tf_op jit(solution)/shard_map/ppermute | solution.py:422
  35.7 1.1 %merge.1 = f32[6,8,16,128]{3,2,1,0:T(8,128)} custom-call(s32[1]{0:T(128)S(6)} %copy.24.acq, f32[14,6,8,128]{3,2,1,0:T(8,128)S(1)} %get-tuple-element.57.placed0, f32[14,6,8,128]{3,2,1,0:T(8,128)S(1)} %get-tuple-element.58.placed1, s16[2,5,6,8,128]{4,3,2,1,0:T(8,128)(2,1)S(1)} %collective-permute-done.3.from_a, ...), custom_call_target="tpu_custom_call" | custom-call | tf_op jit(solution)/shard_map/merge/pallas_call | solution.py:410
Async XLA Ops:
  1.5 6.3 %collective-permute-start.2 = (bf16[2,4,8,32,128]{4,3,2,1,0:T(8,128)(2,1)S(1)}, bf16[2,4,8,32,128]{4,3,2,1,0:T(8,128)(2,1)S(1)}, u32[]{:S(2)}, u32[]{:S(2)}) collective-permute-start(bf16[2,4,8,32,128]{4,3,2,1,0:T(8,128)(2,1)S(1)} %get-tuple-element.38), channel_id=1, source_target_pairs={{0,1},{1,0},{2,3},{3,2},{4,5},{5,4},{6,7},{7,6},{8,9},{9,8},{10,11... | collective-permute-start | bytes 1572872 | tf_op jit(solution)/shard_map/ppermute | solution.py:371
  2.2 13.3 %collective-permute-start.1 = (bf16[4,8,32,128]{3,2,1,0:T(8,128)(2,1)S(1)}, bf16[4,8,32,128]{3,2,1,0:T(8,128)(2,1)S(1)}, u32[]{:S(2)}, u32[]{:S(2)}) collective-permute-start(bf16[4,8,32,128]{3,2,1,0:T(8,128)(2,1)S(1)} %get-tuple-element.36), channel_id=1, source_target_pairs={{1,2},{2,1},{3,4},{4,3},{5,6},{6,5},{7,8},{8,7},{9,10},{10,9},{11,... | collective-permute-start | bytes 786440 | tf_op jit(solution)/shard_map/ppermute | solution.py:372
  5.3 18.2 %collective-permute-start = (bf16[4,8,32,128]{3,2,1,0:T(8,128)(2,1)S(1)}, bf16[4,8,32,128]{3,2,1,0:T(8,128)(2,1)S(1)}, u32[]{:S(2)}, u32[]{:S(2)}) collective-permute-start(bf16[4,8,32,128]{3,2,1,0:T(8,128)(2,1)S(1)} %get-tuple-element.35), channel_id=1, source_target_pairs={{1,2},{2,1},{3,4},{4,3},{5,6},{6,5},{7,8},{8,7},{9,10},{10,9},{11,... | collective-permute-start | bytes 786440 | tf_op jit(solution)/shard_map/ppermute | solution.py:372
  28.1 3.8 %collective-permute-start.3 = (s16[2,5,6,8,128]{4,3,2,1,0:T(8,128)(2,1)S(1)}, s16[2,5,6,8,128]{4,3,2,1,0:T(8,128)(2,1)S(1)}, u32[]{:S(2)}, u32[]{:S(2)}) collective-permute-start(s16[2,5,6,8,128]{4,3,2,1,0:T(8,128)(2,1)S(1)} %get-tuple-element.59), channel_id=1, source_target_pairs={{0,1},{1,0},{2,3},{3,2},{4,5},{5,4},{6,7},{7,6},{8,9},{9,8},{10,11... | collective-permute-start | bytes 368648 | tf_op jit(solution)/shard_map/ppermute | solution.py:422
  28.2 7.5 %collective-permute-start.4 = (s16[2,5,6,8,128]{4,3,2,1,0:T(8,128)(2,1)S(1)}, s16[2,5,6,8,128]{4,3,2,1,0:T(8,128)(2,1)S(1)}, u32[]{:S(2)}, u32[]{:S(2)}) collective-permute-start(s16[2,5,6,8,128]{4,3,2,1,0:T(8,128)(2,1)S(1)} %get-tuple-element.60), channel_id=1, source_target_pairs={{1,2},{2,1},{3,4},{4,3},{5,6},{6,5},{7,8},{8,7},{9,10},{10,9},{11,... | collective-permute-start | bytes 368648 | tf_op jit(solution)/shard_map/ppermute | solution.py:422

commit v6 on v5

--- a/solution.py
+++ b/solution.py
@@ -17,6 +17,7 @@
 F32 = jnp.float32
 BF16 = jnp.bfloat16
 MIB = 1 << 20
+GROUP = 5
 UNIT = 32767.0
 
 
@@ -29,10 +30,9 @@
 
 
 def prep_kernel(*refs):
-    small = (len(refs) - 3 - 2 - PATCHES) // 2
+    small = (len(refs) - 3 - 3) // 2
     feat, small_in, rest = refs[0], refs[1 : 1 + small], refs[1 + small :]
-    (own, to_a), to_b, small_out = rest[:2], rest[2 : 2 + PATCHES], rest[2 + PATCHES : 2 + PATCHES + small]
-    held, sems = rest[2 + PATCHES + small :]
+    (own, to_a, to_b), small_out, (held, sems) = rest[:3], rest[3 : 3 + small], rest[3 + small :]
     channels, planes, rows, cols = feat.shape
     copies = [pltpu.make_async_copy(feat.at[:, x], held.at[x], sems.at[x]) for x in range(planes)]
     copies += [pltpu.make_async_copy(a, b, sems.at[planes + i]) for i, (a, b) in enumerate(zip(small_in, small_out))]
@@ -46,9 +46,9 @@
         turned = jnp.swapaxes(held[x].astype(F32), 0, 1).astype(BF16)
         for p in range(PATCHES):
             own[p, x] = turned[p * PATCH_ROWS : (p + 1) * PATCH_ROWS]
+    to_b[...] = own[0, pl.ds(b_first, RIM)]
     for p in range(PATCHES):
         to_a[p] = own[p, pl.ds(a_first, RIM)]
-        to_b[p][...] = own[p, pl.ds(b_first, RIM)]
     for copy in copies[planes:]:
         copy.wait()
 
@@ -92,12 +92,23 @@
 def fill_taps(taps, plane, source):
     rows, channels, cols = source.shape
     lane = lax.broadcasted_iota(jnp.int32, (channels, cols), 1)
+    not_first = (lane != 0).astype(F32).astype(BF16)
+    not_last = (lane != cols - 1).astype(F32).astype(BF16)
     for h in range(rows):
         value = source[h]
-        wide = value.astype(F32)
-        left = jnp.where(lane == 0, 0.0, pltpu.roll(wide, 1, 1)).astype(BF16)
-        right = jnp.where(lane == cols - 1, 0.0, pltpu.roll(wide, cols - 1, 1)).astype(BF16)
+        left = pltpu.roll(value, 1, 1) * not_first
+        right = pltpu.roll(value, cols - 1, 1) * not_last
         taps[plane, h + 1] = jnp.concatenate([left, value, right], 0)
+
+
+def run(*steps):
+    steps = list(steps)
+    while steps:
+        for step in list(steps):
+            try:
+                next(step)
+            except StopIteration:
+                steps.remove(step)
 
 
 def conv_plane(x, first, fresh, taps, w_all, conv, stats):
@@ -121,24 +132,35 @@
         one, two = one - base, two - base
         stats[1] += one + two
         stats[2] += one * one + two * two
+        yield
 
 
 def conv_planes(first, begin, end, fresh, *refs):
     def one_plane(x):
-        conv_plane(x, first, x == begin if fresh else None, *refs)
-
-    def two_planes(y, _):
-        one_plane(begin + 2 * y)
-        one_plane(begin + 2 * y + 1)
-        return 0
+        run(conv_plane(x, first, x == begin if fresh else None, *refs))
 
     def last_plane(y, _):
         one_plane(end - 1)
         return 0
 
+    def many_planes(y, _):
+        for d in range(GROUP):
+            one_plane(begin + GROUP * y + d)
+        return 0
+
     total = end - begin
-    lax.fori_loop(0, total // 2, two_planes, 0)
-    lax.fori_loop(0, lax.rem(total, 2), last_plane, 0)
+    groups = total // GROUP
+    left = lax.rem(total, GROUP)
+    lax.fori_loop(0, groups, many_planes, 0)
+    begin_left = begin + GROUP * groups
+
+    def two_planes(y, _):
+        one_plane(begin_left + 2 * y)
+        one_plane(begin_left + 2 * y + 1)
+        return 0
+
+    lax.fori_loop(0, left // 2, two_planes, 0)
+    lax.fori_loop(0, lax.rem(left, 2), last_plane, 0)
 
 
 def patch_plan(offs, p, planes):
@@ -149,7 +171,7 @@
     return even, first, jnp.where(even, foreign, 0), jnp.where(even, PATCH_X, PATCH_X - foreign)
 
 
-def pre_kernel(offs, own, from_a, wt, gain, nbias, head_w, head_b, taps0, taps1, conv0, stats0, w_all, head, hbias, scales):
+def pre_kernel(offs, own, from_a, wt, gain, nbias, head_w, head_b, to_b, taps0, taps1, conv0, stats0, w_all, head, hbias, scales):
     planes = own.shape[1]
     classes, folds, channels = head_w.shape
     outs = folds * channels
@@ -157,6 +179,7 @@
     span = planes + 2 * RIM
     even = lax.rem(lax.axis_index("slab"), 2) == 0
     a_base = jnp.where(even, RIM + planes, 0)
+    to_b[...] = own[1, pl.ds(jnp.where(even, 0, planes - RIM), RIM)]
     eye = (lax.broadcasted_iota(jnp.int32, (outs, outs), 0) == lax.broadcasted_iota(jnp.int32, (outs, outs), 1)).astype(F32).astype(BF16)
     wide_w = jnp.concatenate([wt[a] for a in range(3)], 0)
     w_all[...] = lax.dot_general(eye, wide_w, (((1,), (1,)), ((), ())), preferred_element_type=F32).astype(BF16)
@@ -243,6 +266,7 @@
         denom = 1.0 / functools.reduce(jnp.add, parts)
         for k in range(classes):
             table[k].append(parts[k] * denom)
+        yield
     line = gauss(sub.astype(F32), PATCH_ROWS) * gauss(lane.astype(F32), cols)
     window = line * (gauss(jnp.full((rows, cols), x, jnp.int32).astype(F32), PATCH_X) * keep)
     odd = (sub % 2) == 1
@@ -269,11 +293,16 @@
     _, first1, begin, end = patch_plan(offs, 1, planes)
 
     def both(y, _):
-        finish_plane(y, first0, keep, conv0, norm, head, hbias, placed)
-        conv_plane(begin + y, first1, y == 0, taps1, w_all, conv1, stats1)
-        return 0
-
-    lax.fori_loop(0, end - begin, both, 0)
+        run(conv_plane(begin + y, first1, y == 0, taps1, w_all, conv1, stats1), finish_plane(y, first0, keep, conv0, norm, head, hbias, placed))
+        return 0
+
+    def both_twice(y, _):
+        both(2 * y, 0)
+        both(2 * y + 1, 0)
+        return 0
+
+    lax.fori_loop(0, (end - begin) // 2, both_twice, 0)
+    lax.fori_loop((end - begin) // 2 * 2, end - begin, both, 0)
 
 
 def post_kernel(offs, mask, from_b, conv0, norm0, w_all, head, hbias, scales, taps1_in, conv1_in, stats1_in, placed0_in, placed0, placed1, to_a, to_b, taps1, conv1, stats1, norm1):
@@ -287,59 +316,79 @@
     waiting = jnp.where(even, 0, end)
 
     def both(y, _):
-        finish_plane(done + y, first0, keep0, conv0, norm0, head, hbias, placed0)
-        conv_plane(waiting + y, first1, None, taps1, w_all, conv1, stats1)
-        return 0
-
-    lax.fori_loop(0, PATCH_X - done, both, 0)
+        run(conv_plane(waiting + y, first1, None, taps1, w_all, conv1, stats1), finish_plane(done + y, first0, keep0, conv0, norm0, head, hbias, placed0))
+        return 0
+
+    def both_twice(y, _):
+        both(2 * y, 0)
+        both(2 * y + 1, 0)
+        return 0
+
+    left = PATCH_X - done
+    lax.fori_loop(0, left // 2, both_twice, 0)
+    lax.fori_loop(left // 2 * 2, left, both, 0)
     settle(stats1, scales, norm1)
     clear_rest(first1, placed1)
 
     def finish(x, _):
-        finish_plane(x, first1, keep1, conv1, norm1, head, hbias, placed1)
-        return 0
-
-    lax.fori_loop(0, PATCH_X, finish, 0, unroll=2)
+        run(finish_plane(x, first1, keep1, conv1, norm1, head, hbias, placed1))
+        return 0
+
+    lax.fori_loop(0, PATCH_X, finish, 0, unroll=5)
     for send, begin in ((to_a, jnp.where(even, planes + RIM - 1, 0)), (to_b, jnp.where(even, 0, planes + RIM - 1))):
         for p, placed in enumerate((placed0, placed1)):
             for j in range(RIM + 1):
                 send[p, j] = (placed[begin + j] * UNIT + 0.5).astype(jnp.int32).astype(jnp.int16)
 
 
-def merge_kernel(slabs, acq, placed0, placed1, from_a, from_b, out, merged, held, sems):
+def gather_kernel(placed0, placed1, from_a, summed):
     planes = placed0.shape[0] - 2 * RIM
     wide = planes + 2
-    classes, rows, cols = placed0.shape[1:]
+    even = lax.rem(lax.axis_index("slab"), 2) == 0
+    base = jnp.where(even, wide - RIM - 1, 0)
+    for p, placed in enumerate((placed0, placed1)):
+        summed[p] = placed[RIM - 1 : RIM - 1 + wide]
+        for j in range(RIM + 1):
+            summed[p, base + j] += from_a[p, j].astype(jnp.int32).astype(F32) * (1.0 / UNIT)
+
+
+def merge_kernel(slabs, acq, summed, from_b, out, merged, held, sems):
+    wide = summed.shape[1]
+    planes = wide - 2
+    classes, rows, cols = summed.shape[2:]
     slab = lax.axis_index("slab")
     even = lax.rem(slab, 2) == 0
-    a_base = jnp.where(even, wide - RIM - 1, 0)
-    b_base = jnp.where(even, 0, wide - RIM - 1)
+    base = jnp.where(even, 0, wide - RIM - 1)
     shape = (rows, cols)
+    gaps = jnp.maximum(acq[0] - 1, 1)
     count = jnp.full(shape, acq[0], jnp.int32).astype(F32)
     anchor = jnp.full(shape, slab * planes, jnp.int32).astype(F32)
     step = planes / jnp.maximum(count - 1.0, 1.0)
-    for p, placed in enumerate((placed0, placed1)):
-        merged[p] = placed[RIM - 1 : RIM - 1 + wide]
-        for base, got in ((a_base, from_a), (b_base, from_b)):
-            for j in range(RIM + 1):
-                merged[p, base + j] += got[p, j].astype(jnp.int32).astype(F32) * (1.0 / UNIT)
+    lowest = jnp.where(slab == 0, 0, -1)
+    firsts, gains = [], []
+    for s in range(MOST_ACQ):
+        first = lax.div(2 * planes * s + gaps, 2 * gaps) - 1
+        first = jnp.minimum(jnp.maximum(first, lowest), planes - 1)
+        place = jnp.clip(anchor + (s * step - 0.5), 0.0, float(slabs * planes - 1)) - anchor
+        used = (s < count).astype(F32)
+        near = place - jnp.full(shape, first, jnp.int32).astype(F32)
+        firsts.append(first + 1)
+        gains.append([jnp.maximum(0.0, 1.0 - jnp.abs(near - d)) * used for d in range(2)])
+    for p in range(PATCHES):
+        merged[p] = summed[p]
+        for j in range(RIM + 1):
+            merged[p, base + j] += from_b[p, j].astype(jnp.int32).astype(F32) * (1.0 / UNIT)
         for j in range(wide):
             parts = [merged[p, j, k] for k in range(classes)]
             scale = 1.0 / (functools.reduce(jnp.add, parts) + PRIOR)
             parts[0] = parts[0] + PRIOR
             for k in range(classes):
                 merged[p, j, k] = parts[k] * scale
-    gains = []
-    for s in range(MOST_ACQ):
-        place = jnp.clip(anchor + (s * step - 0.5), 0.0, float(slabs * planes - 1)) - anchor
-        used = (s < count).astype(F32)
-        gains.append([jnp.maximum(0.0, 1.0 - jnp.abs(place - (j - 1.0))) * used for j in range(wide)])
     copies = []
     for k in range(classes):
         for p in range(PATCHES):
-            column = [merged[p, j, k] for j in range(wide)]
             for s in range(MOST_ACQ):
-                held[k, s, p * rows : (p + 1) * rows] = functools.reduce(jnp.add, [g * v for g, v in zip(gains[s], column)])
+                held[k, s, p * rows : (p + 1) * rows] = gains[s][0] * merged[p, firsts[s], k] + gains[s][1] * merged[p, firsts[s] + 1, k]
         copies.append(pltpu.make_async_copy(held.at[k], out.at[k], sems.at[k]))
         copies[-1].start()
     for copy in copies:
@@ -354,22 +403,23 @@
     pairs_b = [(i, ((i + 1) ^ 1) - 1) for i in range(slabs) if 0 <= ((i + 1) ^ 1) - 1 < slabs]
     shaped = jax.ShapeDtypeStruct
     cell = (PATCH_ROWS, channels, cols)
+    halo_shape = shaped((RIM,) + cell, BF16)
     params = pltpu.CompilerParams(vmem_limit_bytes=24 * MIB)
     small = [jnp.swapaxes(conv_weight, 1, 2), norm_gain, norm_bias, jnp.swapaxes(head_weight, 0, 1), head_bias, patch_offsets, fg_mask]
     own, to_a, *rest = pl.pallas_call(
         prep_kernel,
         out_shape=[shaped((PATCHES, planes) + cell, BF16), shaped((PATCHES, RIM) + cell, BF16)]
-        + [shaped((RIM,) + cell, BF16)] * PATCHES
+        + [halo_shape]
         + [shaped(v.shape, v.dtype) for v in small],
         in_specs=[pl.BlockSpec(memory_space=pltpu.HBM)] * (1 + len(small)),
-        out_specs=[vmem()] * (2 + PATCHES + len(small)),
+        out_specs=[vmem()] * (3 + len(small)),
         scratch_shapes=[pltpu.VMEM((planes, channels, row_total, cols), BF16), pltpu.SemaphoreType.DMA((planes + len(small),))],
         compiler_params=params,
         name="prep",
     )(*[pltpu.with_memory_space_constraint(v, pltpu.HBM) for v in (features, *small)])
-    to_b, (conv_weight, norm_gain, norm_bias, head_weight, head_bias, patch_offsets, fg_mask) = rest[:PATCHES], rest[PATCHES:]
+    to_b, conv_weight, norm_gain, norm_bias, head_weight, head_bias, patch_offsets, fg_mask = rest
     from_a = lax.ppermute(to_a, "slab", pairs_a)
-    from_b = [lax.ppermute(v, "slab", pairs_b) for v in to_b]
+    from_b0 = lax.ppermute(to_b, "slab", pairs_b)
     wide = planes + 2
     tile = (classes, PATCH_ROWS, cols)
     span = planes + 2 * RIM
@@ -380,11 +430,11 @@
     placed_shape = shaped((span,) + tile, F32)
     norm_shape = shaped((2, outs, cols), F32)
     send_shape = shaped((PATCHES, RIM + 1) + tile, jnp.int16)
-    taps0, taps1, conv0, stats0, *tables = pl.pallas_call(
+    to_b, taps0, taps1, conv0, stats0, *tables = pl.pallas_call(
         pre_kernel,
-        out_shape=[taps_shape, taps_shape, conv_shape, stats_shape] + table_shapes,
+        out_shape=[halo_shape, taps_shape, taps_shape, conv_shape, stats_shape] + table_shapes,
         in_specs=[smem()] + [vmem()] * 7,
-        out_specs=[vmem()] * 8,
+        out_specs=[vmem()] * 9,
         compiler_params=params,
         name="pre",
     )(patch_offsets, own, from_a, conv_weight, norm_gain, norm_bias, head_weight, head_bias)
@@ -396,7 +446,8 @@
         input_output_aliases={3: 4, 4: 5, 5: 6},
         compiler_params=params,
         name="mid",
-    )(patch_offsets, fg_mask, from_b[0], taps0, conv0, stats0, taps1, *tables)
+    )(patch_offsets, fg_mask, from_b0, taps0, conv0, stats0, taps1, *tables)
+    from_b1 = lax.ppermute(to_b, "slab", pairs_b)
     placed0, placed1, send_a, send_b, *_ = pl.pallas_call(
         post_kernel,
         out_shape=[placed_shape, placed_shape, send_shape, send_shape, taps_shape, conv_shape, stats_shape],
@@ -406,11 +457,21 @@
         scratch_shapes=[pltpu.VMEM(norm_shape.shape, F32)],
         compiler_params=params,
         name="post",
-    )(patch_offsets, fg_mask, from_b[1], conv0, norm0, *tables, taps1, conv1, stats1, placed0)
+    )(patch_offsets, fg_mask, from_b1, conv0, norm0, *tables, taps1, conv1, stats1, placed0)
+    got_a = lax.ppermute(send_a, "slab", pairs_a)
+    got_b = lax.ppermute(send_b, "slab", pairs_b)
+    summed = pl.pallas_call(
+        gather_kernel,
+        out_shape=shaped((PATCHES, wide) + tile, F32),
+        in_specs=[vmem()] * 3,
+        out_specs=vmem(),
+        compiler_params=params,
+        name="gather",
+    )(placed0, placed1, got_a)
     return pl.pallas_call(
         functools.partial(merge_kernel, slabs),
         out_shape=shaped((classes, MOST_ACQ, row_total, cols), F32),
-        in_specs=[smem()] + [vmem()] * 4,
+        in_specs=[smem()] + [vmem()] * 2,
         out_specs=pl.BlockSpec(memory_space=pltpu.HBM),
         scratch_shapes=[
             pltpu.VMEM((PATCHES, wide) + tile, F32),
@@ -419,7 +480,7 @@
         ],
         compiler_params=params,
         name="merge",
-    )(acq_counts, placed0, placed1, lax.ppermute(send_a, "slab", pairs_a), lax.ppermute(send_b, "slab", pairs_b))
+    )(acq_counts, summed, got_b)
 
 
 def solution(mesh):

time: 37 us -> 35 us (0.946)
  the two profiles are of different devices: /device:TPU:17 before, /device:TPU:11 now
where the time goes in v6:
time: 35 us; the launch traced here: 34.3 us
  Pallas kernels  17.7 us (51%)
  starting transfers between devices  8.96 us (26%)
  waiting for transfers between devices  6.9 us (20%)
  between operations  0.73 us (2%)
    pallas_call x1, Pallas kernels, local(): pl.pallas_call(mid_kernel, out_shape=[placed_shape, norm_shape, conv_shap...  6.22 us
    ppermute x1, waiting for transfers between devices, local(): got_b = lax.ppermute(send_b, 'slab', pairs_b)  4.86 us
    pallas_call x1, Pallas kernels, local(): pl.pallas_call(pre_kernel, out_shape=[halo_shape, taps_shape, taps_shape,...  4.81 us
    pallas_call x1, Pallas kernels, local(): pl.pallas_call(post_kernel, out_shape=[placed_shape, placed_shape, send_s...  4.23 us
    ppermute x1, starting transfers between devices, local(): from_b0 = lax.ppermute(to_b, 'slab', pairs_b)  3.05 us
    ppermute x1, starting transfers between devices, local(): from_b1 = lax.ppermute(to_b, 'slab', pairs_b)  2.22 us
    ppermute x1, starting transfers between devices, local(): got_b = lax.ppermute(send_b, 'slab', pairs_b)  1.91 us
    ppermute x1, waiting for transfers between devices, local(): from_b1 = lax.ppermute(to_b, 'slab', pairs_b)  1.67 us
  transfers between devices with their start and end apart: 5, of which 3 were waited for; matrix products, arithmetic and copies ran while one was open for 0% of the time, Pallas kernels for 32%

profile of v6, /device:TPU:11, one launch (start us, length us, event | category | flops | bytes accessed | tf_op | source)
XLA Modules:
  0.0 34.3 jit_solution(3822235334938676783)
XLA Ops:
  0.0 1.5 %prep.1 = (bf16[2,6,8,32,128]{4,3,2,1,0:T(8,128)(2,1)S(1)}, bf16[2,4,8,32,128]{4,3,2,1,0:T(8,128)(2,1)S(1)}, bf16[4,8,32,128]{3,2,1,0:T(8,128)(2,1)S(1)}, bf16[3...) custom-call(bf16[32,6,16,128]{3,2,1,0:T(8,128)(2,1)} %refs_0_.1, ...), custom_call_target="tpu_custom_call" | custom-call | tf_op jit(solution)/shard_map/prep/pallas_call | solution.py:409
  1.5 0.7 %collective-permute-start = (bf16[2,4,8,32,128]{4,3,2,1,0:T(8,128)(2,1)S(1)}, bf16[2,4,8,32,128]{4,3,2,1,0:T(8,128)(2,1)S(1)}, u32[]{:S(2)}, u32[]{:S(2)}) collective-permute-start(bf16[2,4,8,32,128]{4,3,2,1,0:T(8,128)(2,1)S(1)} %get-tuple-element.36), channel_id=1, source_target_pairs={{0,1},{1,0},{2,3},{3,2},{4,5},{5,4},{6,7},{7,6},{8,9},{9,8},{10,11... | collective-permute-start | bytes 1572872 | tf_op jit(solution)/shard_map/ppermute | solution.py:421
  2.2 3.0 %collective-permute-start.2 = (bf16[4,8,32,128]{3,2,1,0:T(8,128)(2,1)S(1)}, bf16[4,8,32,128]{3,2,1,0:T(8,128)(2,1)S(1)}, u32[]{:S(2)}, u32[]{:S(2)}) collective-permute-start(bf16[4,8,32,128]{3,2,1,0:T(8,128)(2,1)S(1)} %get-tuple-element.43), channel_id=1, source_target_pairs={{1,2},{2,1},{3,4},{4,3},{5,6},{6,5},{7,8},{8,7},{9,10},{10,9},{11,... | collective-permute-start | bytes 786440 | tf_op jit(solution)/shard_map/ppermute | solution.py:422
  5.3 0.0 collective-permute-done.from_a
  5.3 4.8 %pre.1 = (bf16[4,8,32,128]{3,2,1,0:T(8,128)(2,1)S(1)}, bf16[15,10,96,128]{3,2,1,0:T(8,128)(2,1)S(1)}, bf16[15,10,96,128]{3,2,1,0:T(8,128)(2,1)S(1)}, f32[10,4,12...) custom-call(s32[1,2]{1,0:T(1,128)S(1)} %get-tuple-element.33.offs, ...), custom_call_target="tpu_custom_call" | custom-call | tf_op jit(solution)/shard_map/pre/pallas_call | solution.py:433
  10.1 2.2 %collective-permute-start.1 = (bf16[4,8,32,128]{3,2,1,0:T(8,128)(2,1)S(1)}, bf16[4,8,32,128]{3,2,1,0:T(8,128)(2,1)S(1)}, u32[]{:S(2)}, u32[]{:S(2)}) collective-permute-start(bf16[4,8,32,128]{3,2,1,0:T(8,128)(2,1)S(1)} %get-tuple-element.42), channel_id=1, source_target_pairs={{1,2},{2,1},{3,4},{4,3},{5,6},{6,5},{7,8},{8,7},{9,10},{10,9},{11,... | collective-permute-start | bytes 786440 | tf_op jit(solution)/shard_map/ppermute | solution.py:450
  12.3 0.4 %collective-permute-done.2.from_b = bf16[4,8,32,128]{3,2,1,0:T(8,128)(2,1)S(1)} collective-permute-done((bf16[4,8,32,128]{3,2,1,0:T(8,128)(2,1)S(1)}, bf16[4,8,32,128]{3,2,1,0:T(8,128)(2,1)S(1)}, u32[]{:S(2)}, u32[]{:S(2)}) %collective-permute-start.2) | collective-permute-done | bytes 262176 | tf_op jit(solution)/shard_map/ppermute | solution.py:422
  12.7 6.2 %mid.1 = (f32[14,6,8,128]{3,2,1,0:T(8,128)S(1)}, f32[2,128,128]{2,1,0:T(8,128)S(1)}, f32[10,4,128,256]{3,2,1,0:T(8,128)S(1)}, f32[3,128,128]{2,1,0:T(8,128)S(1)}...) custom-call(s32[1,2]{1,0:T(1,128)S(1)} %get-tuple-element.33.offs, ...), custom_call_target="tpu_custom_call", output_to_operand_aliasing={{4}: (3, {}), {5}: (4, {}), {6}: (5, {})} | custom-call | tf_op jit(solution)/shard_map/mid/pallas_call | solution.py:441
  18.9 1.7 %collective-permute-done.1.from_b = bf16[4,8,32,128]{3,2,1,0:T(8,128)(2,1)S(1)} collective-permute-done((bf16[4,8,32,128]{3,2,1,0:T(8,128)(2,1)S(1)}, bf16[4,8,32,128]{3,2,1,0:T(8,128)(2,1)S(1)}, u32[]{:S(2)}, u32[]{:S(2)}) %collective-permute-start.1) | collective-permute-done | bytes 262176 | tf_op jit(solution)/shard_map/ppermute | solution.py:450
  20.6 4.2 %post.1 = (f32[14,6,8,128]{3,2,1,0:T(8,128)S(1)}, f32[14,6,8,128]{3,2,1,0:T(8,128)S(1)}, s16[2,5,6,8,128]{4,3,2,1,0:T(8,128)(2,1)S(1)}, s16[2,5,6,8,128]{4,3,2,1...) custom-call(s32[1,2]{1,0:T(1,128)S(1)} %get-tuple-element.33.offs, ...), custom_call_target="tpu_custom_call", output_to_operand_aliasing={{0}: (12, {}), {4}: (9, {}), {5}: (10, {}), {6}: (11, {})} | custom-call | tf_op jit(solution)/shard_map/post/pallas_call | solution.py:451
  24.8 1.0 %collective-permute-start.3 = (s16[2,5,6,8,128]{4,3,2,1,0:T(8,128)(2,1)S(1)}, s16[2,5,6,8,128]{4,3,2,1,0:T(8,128)(2,1)S(1)}, u32[]{:S(2)}, u32[]{:S(2)}) collective-permute-start(s16[2,5,6,8,128]{4,3,2,1,0:T(8,128)(2,1)S(1)} %get-tuple-element.59), channel_id=1, source_target_pairs={{0,1},{1,0},{2,3},{3,2},{4,5},{5,4},{6,7},{7,6},{8,9},{9,8},{10,11... | collective-permute-start | bytes 368648 | tf_op jit(solution)/shard_map/ppermute | solution.py:461
  25.9 1.9 %collective-permute-start.4 = (s16[2,5,6,8,128]{4,3,2,1,0:T(8,128)(2,1)S(1)}, s16[2,5,6,8,128]{4,3,2,1,0:T(8,128)(2,1)S(1)}, u32[]{:S(2)}, u32[]{:S(2)}) collective-permute-start(s16[2,5,6,8,128]{4,3,2,1,0:T(8,128)(2,1)S(1)} %get-tuple-element.60), channel_id=1, source_target_pairs={{1,2},{2,1},{3,4},{4,3},{5,6},{6,5},{7,8},{8,7},{9,10},{10,9},{11,... | collective-permute-start | bytes 368648 | tf_op jit(solution)/shard_map/ppermute | solution.py:462
  28.4 0.0 collective-permute-done.3.from_a
  28.5 0.1 gather.1.summed
  28.5 4.9 %collective-permute-done.4.from_b = s16[2,5,6,8,128]{4,3,2,1,0:T(8,128)(2,1)S(1)} collective-permute-done((s16[2,5,6,8,128]{4,3,2,1,0:T(8,128)(2,1)S(1)}, s16[2,5,6,8,128]{4,3,2,1,0:T(8,128)(2,1)S(1)}, u32[]{:S(2)}, u32[]{:S(2)}) %collective-permute-start.4) | collective-permute-done | bytes 122912 | tf_op jit(solution)/shard_map/ppermute | solution.py:462
  33.4 1.0 %merge.1 = f32[6,8,16,128]{3,2,1,0:T(8,128)} custom-call(s32[1]{0:T(128)S(6)} %copy.24.acq, f32[2,8,6,8,128]{4,3,2,1,0:T(8,128)S(1)} %gather.1.summed, s16[2,5,6,8,128]{4,3,2,1,0:T(8,128)(2,1)S(1)} %collective-permute-done.4.from_b), custom_call_target="tpu_custom_call" | custom-call | tf_op jit(solution)/shard_map/merge/pallas_call | solution.py:471
Async XLA Ops:
  1.5 3.8 %collective-permute-start = (bf16[2,4,8,32,128]{4,3,2,1,0:T(8,128)(2,1)S(1)}, bf16[2,4,8,32,128]{4,3,2,1,0:T(8,128)(2,1)S(1)}, u32[]{:S(2)}, u32[]{:S(2)}) collective-permute-start(bf16[2,4,8,32,128]{4,3,2,1,0:T(8,128)(2,1)S(1)} %get-tuple-element.36), channel_id=1, source_target_pairs={{0,1},{1,0},{2,3},{3,2},{4,5},{5,4},{6,7},{7,6},{8,9},{9,8},{10,11... | collective-permute-start | bytes 1572872 | tf_op jit(solution)/shard_map/ppermute | solution.py:421
  2.2 10.5 %collective-permute-start.2 = (bf16[4,8,32,128]{3,2,1,0:T(8,128)(2,1)S(1)}, bf16[4,8,32,128]{3,2,1,0:T(8,128)(2,1)S(1)}, u32[]{:S(2)}, u32[]{:S(2)}) collective-permute-start(bf16[4,8,32,128]{3,2,1,0:T(8,128)(2,1)S(1)} %get-tuple-element.43), channel_id=1, source_target_pairs={{1,2},{2,1},{3,4},{4,3},{5,6},{6,5},{7,8},{8,7},{9,10},{10,9},{11,... | collective-permute-start | bytes 786440 | tf_op jit(solution)/shard_map/ppermute | solution.py:422
  10.1 10.5 %collective-permute-start.1 = (bf16[4,8,32,128]{3,2,1,0:T(8,128)(2,1)S(1)}, bf16[4,8,32,128]{3,2,1,0:T(8,128)(2,1)S(1)}, u32[]{:S(2)}, u32[]{:S(2)}) collective-permute-start(bf16[4,8,32,128]{3,2,1,0:T(8,128)(2,1)S(1)} %get-tuple-element.42), channel_id=1, source_target_pairs={{1,2},{2,1},{3,4},{4,3},{5,6},{6,5},{7,8},{8,7},{9,10},{10,9},{11,... | collective-permute-start | bytes 786440 | tf_op jit(solution)/shard_map/ppermute | solution.py:450
  24.8 3.6 %collective-permute-start.3 = (s16[2,5,6,8,128]{4,3,2,1,0:T(8,128)(2,1)S(1)}, s16[2,5,6,8,128]{4,3,2,1,0:T(8,128)(2,1)S(1)}, u32[]{:S(2)}, u32[]{:S(2)}) collective-permute-start(s16[2,5,6,8,128]{4,3,2,1,0:T(8,128)(2,1)S(1)} %get-tuple-element.59), channel_id=1, source_target_pairs={{0,1},{1,0},{2,3},{3,2},{4,5},{5,4},{6,7},{7,6},{8,9},{9,8},{10,11... | collective-permute-start | bytes 368648 | tf_op jit(solution)/shard_map/ppermute | solution.py:461
  25.9 7.5 %collective-permute-start.4 = (s16[2,5,6,8,128]{4,3,2,1,0:T(8,128)(2,1)S(1)}, s16[2,5,6,8,128]{4,3,2,1,0:T(8,128)(2,1)S(1)}, u32[]{:S(2)}, u32[]{:S(2)}) collective-permute-start(s16[2,5,6,8,128]{4,3,2,1,0:T(8,128)(2,1)S(1)} %get-tuple-element.60), channel_id=1, source_target_pairs={{1,2},{2,1},{3,4},{4,3},{5,6},{6,5},{7,8},{8,7},{9,10},{10,9},{11,... | collective-permute-start | bytes 368648 | tf_op jit(solution)/shard_map/ppermute | solution.py:462

commit v7 on v6

--- a/solution.py
+++ b/solution.py
@@ -30,9 +30,9 @@
 
 
 def prep_kernel(*refs):
-    small = (len(refs) - 3 - 3) // 2
+    small = (len(refs) - 7) // 2
     feat, small_in, rest = refs[0], refs[1 : 1 + small], refs[1 + small :]
-    (own, to_a, to_b), small_out, (held, sems) = rest[:3], rest[3 : 3 + small], rest[3 + small :]
+    (own, to_a, *to_b), small_out, (held, sems) = rest[:4], rest[4 : 4 + small], rest[4 + small :]
     channels, planes, rows, cols = feat.shape
     copies = [pltpu.make_async_copy(feat.at[:, x], held.at[x], sems.at[x]) for x in range(planes)]
     copies += [pltpu.make_async_copy(a, b, sems.at[planes + i]) for i, (a, b) in enumerate(zip(small_in, small_out))]
@@ -46,9 +46,9 @@
         turned = jnp.swapaxes(held[x].astype(F32), 0, 1).astype(BF16)
         for p in range(PATCHES):
             own[p, x] = turned[p * PATCH_ROWS : (p + 1) * PATCH_ROWS]
-    to_b[...] = own[0, pl.ds(b_first, RIM)]
     for p in range(PATCHES):
         to_a[p] = own[p, pl.ds(a_first, RIM)]
+        to_b[p][...] = own[p, pl.ds(b_first, RIM)]
     for copy in copies[planes:]:
         copy.wait()
 
@@ -171,7 +171,7 @@
     return even, first, jnp.where(even, foreign, 0), jnp.where(even, PATCH_X, PATCH_X - foreign)
 
 
-def pre_kernel(offs, own, from_a, wt, gain, nbias, head_w, head_b, to_b, taps0, taps1, conv0, stats0, w_all, head, hbias, scales):
+def pre_kernel(offs, own, from_a, wt, gain, nbias, head_w, head_b, taps0, taps1, conv0, conv1, stats0, stats1, w_all, head, hbias, scales):
     planes = own.shape[1]
     classes, folds, channels = head_w.shape
     outs = folds * channels
@@ -179,7 +179,6 @@
     span = planes + 2 * RIM
     even = lax.rem(lax.axis_index("slab"), 2) == 0
     a_base = jnp.where(even, RIM + planes, 0)
-    to_b[...] = own[1, pl.ds(jnp.where(even, 0, planes - RIM), RIM)]
     eye = (lax.broadcasted_iota(jnp.int32, (outs, outs), 0) == lax.broadcasted_iota(jnp.int32, (outs, outs), 1)).astype(F32).astype(BF16)
     wide_w = jnp.concatenate([wt[a] for a in range(3)], 0)
     w_all[...] = lax.dot_general(eye, wide_w, (((1,), (1,)), ((), ())), preferred_element_type=F32).astype(BF16)
@@ -208,9 +207,10 @@
         lax.fori_loop(0, span, pad_rows, 0)
         lax.fori_loop(0, planes, fill_own, 0, unroll=2)
         lax.fori_loop(0, RIM, fill_a, 0, unroll=2)
-    stats0[...] = jnp.zeros_like(stats0)
-    _, first, begin, end = patch_plan(offs, 0, planes)
-    conv_planes(first, begin, end, True, taps0, w_all, conv0, stats0)
+    for p, (taps, conv, stats) in enumerate(((taps0, conv0, stats0), (taps1, conv1, stats1))):
+        stats[...] = jnp.zeros_like(stats)
+        _, first, begin, end = patch_plan(offs, p, planes)
+        conv_planes(first, begin, end, True, taps, w_all, conv, stats)
 
 
 def fill_b(even, from_b, taps):
@@ -280,20 +280,48 @@
         placed[first + x, k] = full * window
 
 
-def mid_kernel(offs, mask, from_b, taps0_in, conv0_in, stats0_in, taps1, w_all, head, hbias, scales, placed, norm, conv1, stats1, taps0, conv0, stats0):
-    planes = taps0.shape[0] - 1 - 2 * RIM
+def finish_planes(begin, end, first, keep, *refs):
+    def finish(x):
+        run(finish_plane(x, first, keep, *refs))
+
+    def many(y, _):
+        for d in range(GROUP):
+            finish(begin + GROUP * y + d)
+        return 0
+
+    def one(x, _):
+        finish(x)
+        return 0
+
+    groups = (end - begin) // GROUP
+    lax.fori_loop(0, groups, many, 0)
+    lax.fori_loop(begin + GROUP * groups, end, one, 0)
+
+
+def mid_kernel(offs, mask, from_b, taps_in, conv_in, stats_in, w_all, head, hbias, scales, placed, norm, taps, conv, stats):
+    planes = taps.shape[0] - 1 - 2 * RIM
     folds = placed.shape[2] // 2
-    even, first0, begin, end = patch_plan(offs, 0, planes)
-    fill_b(even, from_b, taps0)
-    conv_planes(first0, jnp.where(even, 0, end), jnp.where(even, begin, PATCH_X), False, taps0, w_all, conv0, stats0)
-    settle(stats0, scales, norm)
-    clear_rest(first0, placed)
-    stats1[...] = jnp.zeros_like(stats1)
-    keep = mask[0, 0].astype(F32) * (1.0 / folds)
+    even, first, begin, end = patch_plan(offs, 0, planes)
+    fill_b(even, from_b, taps)
+    conv_planes(first, jnp.where(even, 0, end), jnp.where(even, begin, PATCH_X), False, taps, w_all, conv, stats)
+    settle(stats, scales, norm)
+    clear_rest(first, placed)
+    _, _, begin, end = patch_plan(offs, 1, planes)
+    finish_planes(0, end - begin, first, mask[0, 0].astype(F32) * (1.0 / folds), conv, norm, head, hbias, placed)
+
+
+def post_kernel(offs, mask, from_b, conv0, norm0, w_all, head, hbias, scales, taps_in, conv_in, stats_in, placed0_in, placed0, placed1, to_a, to_b, taps, conv, stats, norm1):
+    planes = taps.shape[0] - 1 - 2 * RIM
+    folds = placed1.shape[2] // 2
+    even, first0, _, _ = patch_plan(offs, 0, planes)
     _, first1, begin, end = patch_plan(offs, 1, planes)
+    fill_b(even, from_b, taps)
+    keep0, keep1 = (mask[0, p].astype(F32) * (1.0 / folds) for p in range(PATCHES))
+    done = end - begin
+    waiting = jnp.where(even, 0, end)
 
     def both(y, _):
-        run(conv_plane(begin + y, first1, y == 0, taps1, w_all, conv1, stats1), finish_plane(y, first0, keep, conv0, norm, head, hbias, placed))
+        run(conv_plane(waiting + y, first1, None, taps, w_all, conv, stats), finish_plane(done + y, first0, keep0, conv0, norm0, head, hbias, placed0))
         return 0
 
     def both_twice(y, _):
@@ -301,40 +329,12 @@
         both(2 * y + 1, 0)
         return 0
 
-    lax.fori_loop(0, (end - begin) // 2, both_twice, 0)
-    lax.fori_loop((end - begin) // 2 * 2, end - begin, both, 0)
-
-
-def post_kernel(offs, mask, from_b, conv0, norm0, w_all, head, hbias, scales, taps1_in, conv1_in, stats1_in, placed0_in, placed0, placed1, to_a, to_b, taps1, conv1, stats1, norm1):
-    planes = taps1.shape[0] - 1 - 2 * RIM
-    folds = placed1.shape[2] // 2
-    even, first0, _, _ = patch_plan(offs, 0, planes)
-    _, first1, begin, end = patch_plan(offs, 1, planes)
-    fill_b(even, from_b, taps1)
-    keep0, keep1 = (mask[0, p].astype(F32) * (1.0 / folds) for p in range(PATCHES))
-    done = end - begin
-    waiting = jnp.where(even, 0, end)
-
-    def both(y, _):
-        run(conv_plane(waiting + y, first1, None, taps1, w_all, conv1, stats1), finish_plane(done + y, first0, keep0, conv0, norm0, head, hbias, placed0))
-        return 0
-
-    def both_twice(y, _):
-        both(2 * y, 0)
-        both(2 * y + 1, 0)
-        return 0
-
     left = PATCH_X - done
     lax.fori_loop(0, left // 2, both_twice, 0)
     lax.fori_loop(left // 2 * 2, left, both, 0)
-    settle(stats1, scales, norm1)
+    settle(stats, scales, norm1)
     clear_rest(first1, placed1)
-
-    def finish(x, _):
-        run(finish_plane(x, first1, keep1, conv1, norm1, head, hbias, placed1))
-        return 0
-
-    lax.fori_loop(0, PATCH_X, finish, 0, unroll=5)
+    finish_planes(0, PATCH_X, first1, keep1, conv, norm1, head, hbias, placed1)
     for send, begin in ((to_a, jnp.where(even, planes + RIM - 1, 0)), (to_b, jnp.where(even, 0, planes + RIM - 1))):
         for p, placed in enumerate((placed0, placed1)):
             for j in range(RIM + 1):
@@ -409,17 +409,17 @@
     own, to_a, *rest = pl.pallas_call(
         prep_kernel,
         out_shape=[shaped((PATCHES, planes) + cell, BF16), shaped((PATCHES, RIM) + cell, BF16)]
-        + [halo_shape]
+        + [halo_shape] * PATCHES
         + [shaped(v.shape, v.dtype) for v in small],
         in_specs=[pl.BlockSpec(memory_space=pltpu.HBM)] * (1 + len(small)),
-        out_specs=[vmem()] * (3 + len(small)),
+        out_specs=[vmem()] * (2 + PATCHES + len(small)),
         scratch_shapes=[pltpu.VMEM((planes, channels, row_total, cols), BF16), pltpu.SemaphoreType.DMA((planes + len(small),))],
         compiler_params=params,
         name="prep",
     )(*[pltpu.with_memory_space_constraint(v, pltpu.HBM) for v in (features, *small)])
-    to_b, conv_weight, norm_gain, norm_bias, head_weight, head_bias, patch_offsets, fg_mask = rest
+    to_b, (conv_weight, norm_gain, norm_bias, head_weight, head_bias, patch_offsets, fg_mask) = rest[:PATCHES], rest[PATCHES:]
     from_a = lax.ppermute(to_a, "slab", pairs_a)
-    from_b0 = lax.ppermute(to_b, "slab", pairs_b)
+    from_b = [lax.ppermute(v, "slab", pairs_b) for v in to_b]
     wide = planes + 2
     tile = (classes, PATCH_ROWS, cols)
     span = planes + 2 * RIM
@@ -430,24 +430,23 @@
     placed_shape = shaped((span,) + tile, F32)
     norm_shape = shaped((2, outs, cols), F32)
     send_shape = shaped((PATCHES, RIM + 1) + tile, jnp.int16)
-    to_b, taps0, taps1, conv0, stats0, *tables = pl.pallas_call(
+    taps0, taps1, conv0, conv1, stats0, stats1, *tables = pl.pallas_call(
         pre_kernel,
-        out_shape=[halo_shape, taps_shape, taps_shape, conv_shape, stats_shape] + table_shapes,
+        out_shape=[taps_shape] * 2 + [conv_shape] * 2 + [stats_shape] * 2 + table_shapes,
         in_specs=[smem()] + [vmem()] * 7,
-        out_specs=[vmem()] * 9,
+        out_specs=[vmem()] * 10,
         compiler_params=params,
         name="pre",
     )(patch_offsets, own, from_a, conv_weight, norm_gain, norm_bias, head_weight, head_bias)
-    placed0, norm0, conv1, stats1, _, conv0, _ = pl.pallas_call(
+    placed0, norm0, _, conv0, _ = pl.pallas_call(
         mid_kernel,
-        out_shape=[placed_shape, norm_shape, conv_shape, stats_shape, taps_shape, conv_shape, stats_shape],
-        in_specs=[smem()] * 2 + [vmem()] * 9,
-        out_specs=[vmem()] * 7,
-        input_output_aliases={3: 4, 4: 5, 5: 6},
+        out_shape=[placed_shape, norm_shape, taps_shape, conv_shape, stats_shape],
+        in_specs=[smem()] * 2 + [vmem()] * 8,
+        out_specs=[vmem()] * 5,
+        input_output_aliases={3: 2, 4: 3, 5: 4},
         compiler_params=params,
         name="mid",
-    )(patch_offsets, fg_mask, from_b0, taps0, conv0, stats0, taps1, *tables)
-    from_b1 = lax.ppermute(to_b, "slab", pairs_b)
+    )(patch_offsets, fg_mask, from_b[0], taps0, conv0, stats0, *tables)
     placed0, placed1, send_a, send_b, *_ = pl.pallas_call(
         post_kernel,
         out_shape=[placed_shape, placed_shape, send_shape, send_shape, taps_shape, conv_shape, stats_shape],
@@ -457,7 +456,7 @@
         scratch_shapes=[pltpu.VMEM(norm_shape.shape, F32)],
         compiler_params=params,
         name="post",
-    )(patch_offsets, fg_mask, from_b1, conv0, norm0, *tables, taps1, conv1, stats1, placed0)
+    )(patch_offsets, fg_mask, from_b[1], conv0, norm0, *tables, taps1, conv1, stats1, placed0)
     got_a = lax.ppermute(send_a, "slab", pairs_a)
     got_b = lax.ppermute(send_b, "slab", pairs_b)
     summed = pl.pallas_call(

time: 35 us -> 33.9 us (0.969)
  waiting for transfers between devices: 6.9 us -> 4.34 us
  starting transfers between devices: 8.96 us -> 9.9 us
  Pallas kernels: 17.7 us -> 18.3 us
    ppermute x1, starting transfers between devices: 1.91 us -> 3.54 us  [local(): got_b = lax.ppermute(send_b, 'slab', pairs_b)]
    ppermute x1, waiting for transfers between devices: 4.86 us -> 3.24 us  [local(): got_b = lax.ppermute(send_b, 'slab', pairs_b)]
    ppermute x1, starting transfers between devices: 1.05 us -> 0.07 us  [local(): got_a = lax.ppermute(send_a, 'slab', pairs_a)]
    ppermute x2, waiting for transfers between devices: 2.04 us -> 1.09 us  [local(): from_b = [lax.ppermute(v, 'slab', pairs_b) for v in to_b]]
    pallas_call x1, Pallas kernels: 4.23 us -> 4.85 us  [local(): pl.pallas_call(post_kernel, out_shape=[placed_shape, placed_shape, send_s...]
  transfers between devices with their start and end apart: 5 -> 5, of which waited for: 3 -> 2; matrix products, arithmetic and copies ran while one was open for 0% -> 0% of each run, Pallas kernels for 32% -> 33%
where the time goes in v7:
time: 33.9 us; the launch traced here: 33.3 us
  Pallas kernels  18.3 us (54%)
  starting transfers between devices  9.9 us (29%)
  waiting for transfers between devices  4.34 us (13%)
  between operations  0.74 us (2%)
    pallas_call x1, Pallas kernels, local(): pl.pallas_call(pre_kernel, out_shape=[taps_shape] * 2 + [conv_shape] * 2...  6.62 us
    ppermute x2, starting transfers between devices, local(): from_b = [lax.ppermute(v, 'slab', pairs_b) for v in to_b]  5.55 us
    pallas_call x1, Pallas kernels, local(): pl.pallas_call(post_kernel, out_shape=[placed_shape, placed_shape, send_s...  4.85 us
    pallas_call x1, Pallas kernels, local(): pl.pallas_call(mid_kernel, out_shape=[placed_shape, norm_shape, taps_shap...  4.38 us
    ppermute x1, starting transfers between devices, local(): got_b = lax.ppermute(send_b, 'slab', pairs_b)  3.54 us
    ppermute x1, waiting for transfers between devices, local(): got_b = lax.ppermute(send_b, 'slab', pairs_b)  3.24 us
    pallas_call x1, Pallas kernels, local(): pl.pallas_call(prep_kernel, out_shape=[shaped((PATCHES, planes) + cell, B...  1.47 us
    ppermute x2, waiting for transfers between devices, local(): from_b = [lax.ppermute(v, 'slab', pairs_b) for v in to_b]  1.09 us
  transfers between devices with their start and end apart: 5, of which 2 were waited for; matrix products, arithmetic and copies ran while one was open for 0% of the time, Pallas kernels for 33%

profile of v7, /device:TPU:11, one launch (start us, length us, event | category | flops | bytes accessed | tf_op | source)
XLA Modules:
  0.0 33.3 jit_solution(5435293946255957720)
XLA Ops:
  0.0 1.5 %prep.1 = (bf16[2,6,8,32,128]{4,3,2,1,0:T(8,128)(2,1)S(1)}, bf16[2,4,8,32,128]{4,3,2,1,0:T(8,128)(2,1)S(1)}, bf16[4,8,32,128]{3,2,1,0:T(8,128)(2,1)S(1)}, bf16[4...) custom-call(bf16[32,6,16,128]{3,2,1,0:T(8,128)(2,1)} %refs_0_.1, ...), custom_call_target="tpu_custom_call" | custom-call | tf_op jit(solution)/shard_map/prep/pallas_call | solution.py:409
  1.5 0.7 %collective-permute-start.2 = (bf16[2,4,8,32,128]{4,3,2,1,0:T(8,128)(2,1)S(1)}, bf16[2,4,8,32,128]{4,3,2,1,0:T(8,128)(2,1)S(1)}, u32[]{:S(2)}, u32[]{:S(2)}) collective-permute-start(bf16[2,4,8,32,128]{4,3,2,1,0:T(8,128)(2,1)S(1)} %get-tuple-element.38), channel_id=1, source_target_pairs={{0,1},{1,0},{2,3},{3,2},{4,5},{5,4},{6,7},{7,6},{8,9},{9,8},{10,11... | collective-permute-start | bytes 1572872 | tf_op jit(solution)/shard_map/ppermute | solution.py:421
  2.2 3.0 %collective-permute-start.1 = (bf16[4,8,32,128]{3,2,1,0:T(8,128)(2,1)S(1)}, bf16[4,8,32,128]{3,2,1,0:T(8,128)(2,1)S(1)}, u32[]{:S(2)}, u32[]{:S(2)}) collective-permute-start(bf16[4,8,32,128]{3,2,1,0:T(8,128)(2,1)S(1)} %get-tuple-element.36), channel_id=1, source_target_pairs={{1,2},{2,1},{3,4},{4,3},{5,6},{6,5},{7,8},{8,7},{9,10},{10,9},{11,... | collective-permute-start | bytes 786440 | tf_op jit(solution)/shard_map/ppermute | solution.py:422
  5.3 2.5 %collective-permute-start = (bf16[4,8,32,128]{3,2,1,0:T(8,128)(2,1)S(1)}, bf16[4,8,32,128]{3,2,1,0:T(8,128)(2,1)S(1)}, u32[]{:S(2)}, u32[]{:S(2)}) collective-permute-start(bf16[4,8,32,128]{3,2,1,0:T(8,128)(2,1)S(1)} %get-tuple-element.35), channel_id=1, source_target_pairs={{1,2},{2,1},{3,4},{4,3},{5,6},{6,5},{7,8},{8,7},{9,10},{10,9},{11,... | collective-permute-start | bytes 786440 | tf_op jit(solution)/shard_map/ppermute | solution.py:422
  7.8 0.0 collective-permute-done.2.from_a
  7.8 6.6 %pre.1 = (bf16[15,10,96,128]{3,2,1,0:T(8,128)(2,1)S(1)}, bf16[15,10,96,128]{3,2,1,0:T(8,128)(2,1)S(1)}, f32[10,4,128,256]{3,2,1,0:T(8,128)S(1)}, f32[10,4,128,25...) custom-call(s32[1,2]{1,0:T(1,128)S(1)} %get-tuple-element.33.offs, ...), custom_call_target="tpu_custom_call" | custom-call | tf_op jit(solution)/shard_map/pre/pallas_call | solution.py:433
  14.4 1.1 %collective-permute-done.1.from_b = bf16[4,8,32,128]{3,2,1,0:T(8,128)(2,1)S(1)} collective-permute-done((bf16[4,8,32,128]{3,2,1,0:T(8,128)(2,1)S(1)}, bf16[4,8,32,128]{3,2,1,0:T(8,128)(2,1)S(1)}, u32[]{:S(2)}, u32[]{:S(2)}) %collective-permute-start.1) | collective-permute-done | bytes 262176 | tf_op jit(solution)/shard_map/ppermute | solution.py:422
  15.5 4.4 %mid.1 = (f32[14,6,8,128]{3,2,1,0:T(8,128)S(1)}, f32[2,128,128]{2,1,0:T(8,128)S(1)}, bf16[15,10,96,128]{3,2,1,0:T(8,128)(2,1)S(1)}, f32[10,4,128,256]{3,2,1,0:T(8,128)S(1)}, f32[3,128,128]{2,1,0:T(8,128)S(1)}) custom-call(s32[1,2]{1,0:T(1,128)S(1)} %get-tuple-element.33.offs, ...), custom_call_target="tpu_custom_call", output_to_operand_aliasing={{2}: (3, {}), {3}: (4, {}), {4}: (5, {})} | custom-call | tf_op jit(solution)/shard_map/mid/pallas_call | solution.py:441
  19.9 0.0 collective-permute-done.from_b
  19.9 4.9 %post.1 = (f32[14,6,8,128]{3,2,1,0:T(8,128)S(1)}, f32[14,6,8,128]{3,2,1,0:T(8,128)S(1)}, s16[2,5,6,8,128]{4,3,2,1,0:T(8,128)(2,1)S(1)}, s16[2,5,6,8,128]{4,3,2,1...) custom-call(s32[1,2]{1,0:T(1,128)S(1)} %get-tuple-element.33.offs, ...), custom_call_target="tpu_custom_call", output_to_operand_aliasing={{0}: (12, {}), {4}: (9, {}), {5}: (10, {}), {6}: (11, {})} | custom-call | tf_op jit(solution)/shard_map/post/pallas_call | solution.py:450
  24.8 0.1 collective-permute-start.3
  24.9 3.5 %collective-permute-start.4 = (s16[2,5,6,8,128]{4,3,2,1,0:T(8,128)(2,1)S(1)}, s16[2,5,6,8,128]{4,3,2,1,0:T(8,128)(2,1)S(1)}, u32[]{:S(2)}, u32[]{:S(2)}) collective-permute-start(s16[2,5,6,8,128]{4,3,2,1,0:T(8,128)(2,1)S(1)} %get-tuple-element.60), channel_id=1, source_target_pairs={{1,2},{2,1},{3,4},{4,3},{5,6},{6,5},{7,8},{8,7},{9,10},{10,9},{11,... | collective-permute-start | bytes 368648 | tf_op jit(solution)/shard_map/ppermute | solution.py:461
  29.0 0.0 collective-permute-done.3.from_a
  29.1 0.1 gather.1.summed
  29.1 3.2 %collective-permute-done.4.from_b = s16[2,5,6,8,128]{4,3,2,1,0:T(8,128)(2,1)S(1)} collective-permute-done((s16[2,5,6,8,128]{4,3,2,1,0:T(8,128)(2,1)S(1)}, s16[2,5,6,8,128]{4,3,2,1,0:T(8,128)(2,1)S(1)}, u32[]{:S(2)}, u32[]{:S(2)}) %collective-permute-start.4) | collective-permute-done | bytes 122912 | tf_op jit(solution)/shard_map/ppermute | solution.py:461
  32.4 1.0 %merge.1 = f32[6,8,16,128]{3,2,1,0:T(8,128)} custom-call(s32[1]{0:T(128)S(6)} %copy.24.acq, f32[2,8,6,8,128]{4,3,2,1,0:T(8,128)S(1)} %gather.1.summed, s16[2,5,6,8,128]{4,3,2,1,0:T(8,128)(2,1)S(1)} %collective-permute-done.4.from_b), custom_call_target="tpu_custom_call" | custom-call | tf_op jit(solution)/shard_map/merge/pallas_call | solution.py:470
Async XLA Ops:
  1.5 6.3 %collective-permute-start.2 = (bf16[2,4,8,32,128]{4,3,2,1,0:T(8,128)(2,1)S(1)}, bf16[2,4,8,32,128]{4,3,2,1,0:T(8,128)(2,1)S(1)}, u32[]{:S(2)}, u32[]{:S(2)}) collective-permute-start(bf16[2,4,8,32,128]{4,3,2,1,0:T(8,128)(2,1)S(1)} %get-tuple-element.38), channel_id=1, source_target_pairs={{0,1},{1,0},{2,3},{3,2},{4,5},{5,4},{6,7},{7,6},{8,9},{9,8},{10,11... | collective-permute-start | bytes 1572872 | tf_op jit(solution)/shard_map/ppermute | solution.py:421
  2.2 13.3 %collective-permute-start.1 = (bf16[4,8,32,128]{3,2,1,0:T(8,128)(2,1)S(1)}, bf16[4,8,32,128]{3,2,1,0:T(8,128)(2,1)S(1)}, u32[]{:S(2)}, u32[]{:S(2)}) collective-permute-start(bf16[4,8,32,128]{3,2,1,0:T(8,128)(2,1)S(1)} %get-tuple-element.36), channel_id=1, source_target_pairs={{1,2},{2,1},{3,4},{4,3},{5,6},{6,5},{7,8},{8,7},{9,10},{10,9},{11,... | collective-permute-start | bytes 786440 | tf_op jit(solution)/shard_map/ppermute | solution.py:422
  5.3 14.6 %collective-permute-start = (bf16[4,8,32,128]{3,2,1,0:T(8,128)(2,1)S(1)}, bf16[4,8,32,128]{3,2,1,0:T(8,128)(2,1)S(1)}, u32[]{:S(2)}, u32[]{:S(2)}) collective-permute-start(bf16[4,8,32,128]{3,2,1,0:T(8,128)(2,1)S(1)} %get-tuple-element.35), channel_id=1, source_target_pairs={{1,2},{2,1},{3,4},{4,3},{5,6},{6,5},{7,8},{8,7},{9,10},{10,9},{11,... | collective-permute-start | bytes 786440 | tf_op jit(solution)/shard_map/ppermute | solution.py:422
  24.8 4.3 %collective-permute-start.3 = (s16[2,5,6,8,128]{4,3,2,1,0:T(8,128)(2,1)S(1)}, s16[2,5,6,8,128]{4,3,2,1,0:T(8,128)(2,1)S(1)}, u32[]{:S(2)}, u32[]{:S(2)}) collective-permute-start(s16[2,5,6,8,128]{4,3,2,1,0:T(8,128)(2,1)S(1)} %get-tuple-element.59), channel_id=1, source_target_pairs={{0,1},{1,0},{2,3},{3,2},{4,5},{5,4},{6,7},{7,6},{8,9},{9,8},{10,11... | collective-permute-start | bytes 368648 | tf_op jit(solution)/shard_map/ppermute | solution.py:460
  24.9 7.5 %collective-permute-start.4 = (s16[2,5,6,8,128]{4,3,2,1,0:T(8,128)(2,1)S(1)}, s16[2,5,6,8,128]{4,3,2,1,0:T(8,128)(2,1)S(1)}, u32[]{:S(2)}, u32[]{:S(2)}) collective-permute-start(s16[2,5,6,8,128]{4,3,2,1,0:T(8,128)(2,1)S(1)} %get-tuple-element.60), channel_id=1, source_target_pairs={{1,2},{2,1},{3,4},{4,3},{5,6},{6,5},{7,8},{8,7},{9,10},{10,9},{11,... | collective-permute-start | bytes 368648 | tf_op jit(solution)/shard_map/ppermute | solution.py:461
